TPU v7x, 32 devices: a whole 2x2x4 slice. The times are simulated.
32 devices in a mesh: batch: 4 (over y, core), seq: 8 (over z, x).
Axes of the slice: x: 2, y: 2, z: 4, core: 2. Of those that a mesh axis runs over, the one named last changes fastest.
Arguments:
- tokens: bfloat16 [4, 8192, 768], P('batch', 'seq'), may hold values from -6 to 6
- cluster_slot: int32 [4, 12, 8192], P('batch', None, 'seq'), may hold values from 0 to 8191, as said below
- loss_mask: int32 [4, 8192], P('batch', 'seq'), may hold values from 0 to 1, as said below
- out_grad: bfloat16 [4, 8192, 768], P('batch', 'seq'), may hold values from -6 to 6
- query_weight: bfloat16 [768, 768], P(('batch', 'seq')), may hold values from -0.21875 to 0.21875
- key_weight: bfloat16 [768, 768], P(('batch', 'seq')), may hold values from -0.21875 to 0.21875
- value_weight: bfloat16 [768, 768], P(('batch', 'seq')), may hold values from -0.21875 to 0.21875
- output_weight: bfloat16 [768, 768], P(('batch', 'seq')), may hold values from -0.875 to 0.875
- query_bias: bfloat16 [768], P(('batch', 'seq')), may hold values from -1.796875 to 1.796875
- value_bias: bfloat16 [768], P(('batch', 'seq')), may hold values from -1.796875 to 1.796875
- output_bias: bfloat16 [768], P(('batch', 'seq')), may hold values from -1.796875 to 1.796875
- first_gain: bfloat16 [768], P(('batch', 'seq')), may hold values from 0.5 to 1.5
- first_shift: bfloat16 [768], P(('batch', 'seq')), may hold values from -1.796875 to 1.796875
- up_weight: bfloat16 [768, 3072], P(('batch', 'seq')), may hold values from -0.21875 to 0.21875
- up_bias: bfloat16 [3072], P(('batch', 'seq')), may hold values from -1.796875 to 1.796875
- down_weight: bfloat16 [3072, 768], P(('batch', 'seq')), may hold values from -0.109375 to 0.109375
- down_bias: bfloat16 [768], P(('batch', 'seq')), may hold values from -1.796875 to 1.796875
- second_gain: bfloat16 [768], P(('batch', 'seq')), may hold values from 0.5 to 1.5
- second_shift: bfloat16 [768], P(('batch', 'seq')), may hold values from -1.796875 to 1.796875
Outputs:
- output: bfloat16 [4, 8192, 768], P('batch', 'seq')
- grad_tokens: bfloat16 [4, 8192, 768], P('batch', 'seq')
- grad_query_weight: float32 [768, 768], P(('batch', 'seq'))
- grad_key_weight: float32 [768, 768], P(('batch', 'seq'))
- grad_value_weight: float32 [768, 768], P(('batch', 'seq'))
- grad_output_weight: float32 [768, 768], P(('batch', 'seq'))
- grad_query_bias: float32 [768], P(('batch', 'seq'))
- grad_value_bias: float32 [768], P(('batch', 'seq'))
- grad_output_bias: float32 [768], P(('batch', 'seq'))
- grad_first_gain: float32 [768], P(('batch', 'seq'))
- grad_first_shift: float32 [768], P(('batch', 'seq'))
- grad_up_weight: float32 [768, 3072], P(('batch', 'seq'))
- grad_up_bias: float32 [3072], P(('batch', 'seq'))
- grad_down_weight: float32 [3072, 768], P(('batch', 'seq'))
- grad_down_bias: float32 [768], P(('batch', 'seq'))
- grad_second_gain: float32 [768], P(('batch', 'seq'))
- grad_second_shift: float32 [768], P(('batch', 'seq'))
- cluster_stats: float32 [2, 64], P(None, 'seq')
Inputs may be any that keep to these rules, and one draw needn't show every extreme that they name: For each sequence and head, cluster_slot is a permutation of 0 to 8191. Cut positions and places into aligned blocks of 1024; the tokens of position block s put exactly 128 tokens into each block of places, and the places they take leave the remainder s when divided by 8. `loss_mask`: the share of ones differs from sequence to sequence.
All inputs are finite; a program needn't handle non-finite values.
Results may differ from a plain program's by a relative error of at most 0.014.
Values may be sent and summed in bfloat16 or wider, within the bound.
A program may use at most 192 MiB of HBM per device.

v0:
```python
import jax
import jax.numpy as jnp
from jax import lax
from jax.sharding import PartitionSpec as P

CLUSTER = 128


EPSILON = 1e-12


def layer_norm(values, gain, shift):
    centre = jnp.mean(values, axis=-1, keepdims=True)
    centred = values - centre
    spread = jnp.mean(centred * centred, axis=-1, keepdims=True)
    return centred * lax.rsqrt(spread + EPSILON) * gain + shift


def gelu_exact(values):
    return jax.nn.gelu(values, approximate=False)


def matmul(left, right):
    return jnp.dot(left, right, preferred_element_type=jnp.float32)


def permute_rows(arrays, row_order):
    head_count, tok_count = row_order.shape
    splits = tuple(
        (array.reshape(tok_count, head_count, -1).transpose(1, 0, 2) for array in arrays)
    )
    column = jnp.arange(tok_count, dtype=jnp.int32)[None, :]

    def one_head(operands):
        picker = (operands[0][:, None] == column).astype(jnp.bfloat16)
        return tuple(
            (
                jnp.dot(picker, head_part, preferred_element_type=jnp.float32).astype(jnp.bfloat16)
                for head_part in operands[1:]
            )
        )

    shuffled = lax.map(one_head, (row_order,) + splits)
    return tuple((item.transpose(1, 0, 2).reshape(tok_count, -1) for item in shuffled))


def to_owner(arrays, sources, owners):
    shuffled = permute_rows(arrays, sources)
    return tuple(
        (item.reshape(owners, item.shape[0] // owners, item.shape[1]) for item in shuffled)
    )


def from_owner(buffers, places):
    flat = tuple((item.reshape(item.shape[0] * item.shape[1], item.shape[2]) for item in buffers))
    return permute_rows(flat, places)


def to_clusters(buffer, head_count):
    owners, per_owner, feat_width = buffer.shape
    per_source = CLUSTER // owners
    dev_blocks = per_owner // per_source
    shaped = buffer.reshape(owners, dev_blocks, per_source, head_count, feat_width // head_count)
    return shaped.transpose(3, 1, 0, 2, 4).reshape(
        head_count, dev_blocks, CLUSTER, feat_width // head_count
    )


def from_clusters(array, owners):
    head_count, dev_blocks, cluster_len, head_dim = array.shape
    per_source = cluster_len // owners
    shaped = array.reshape(head_count, dev_blocks, owners, per_source, head_dim)
    return shaped.transpose(2, 1, 3, 0, 4).reshape(
        owners, dev_blocks * per_source, head_count * head_dim
    )


def body(
    tokens,
    cluster_slot,
    loss_mask,
    out_grad,
    query_weight,
    key_weight,
    value_weight,
    output_weight,
    query_bias,
    value_bias,
    output_bias,
    first_gain,
    first_shift,
    up_weight,
    up_bias,
    down_weight,
    down_bias,
    second_gain,
    second_shift,
):
    inputs = tokens[0]
    tok_count = inputs.shape[0]
    head_count = cluster_slot.shape[1]
    feat_width = inputs.shape[1]
    head_dim = feat_width // head_count
    scale = head_dim ** (-0.5)
    owners = lax.axis_size("seq")
    sequences = lax.axis_size("batch")
    per_owner = tok_count // owners
    slot_rows = cluster_slot[0]
    places = slot_rows // tok_count * per_owner + slot_rows % tok_count // owners
    positions = jnp.broadcast_to(
        jnp.arange(tok_count, dtype=jnp.int32)[None, :], (head_count, tok_count)
    )
    head_rows = jnp.arange(head_count, dtype=jnp.int32)[:, None]
    sources = jnp.zeros((head_count, tok_count), jnp.int32).at[head_rows, places].set(positions)
    mask_float = loss_mask[0].astype(jnp.float32)
    attn_local = (
        query_weight,
        key_weight,
        value_weight,
        output_weight,
        query_bias,
        value_bias,
        output_bias,
        first_gain,
        first_shift,
    )
    ffn_local = (up_weight, down_weight, up_bias, down_bias, second_gain, second_shift)
    (
        query_full,
        key_full,
        value_full,
        out_full,
        query_add,
        value_add,
        out_add,
        gain_first,
        shift_first,
    ) = (
        lax.all_gather(attn_local[0], ("batch", "seq"), axis=0, tiled=True),
        lax.all_gather(attn_local[1], ("batch", "seq"), axis=0, tiled=True),
        lax.all_gather(attn_local[2], ("batch", "seq"), axis=0, tiled=True),
        lax.all_gather(attn_local[3], ("batch", "seq"), axis=0, tiled=True),
        lax.all_gather(attn_local[4], ("batch", "seq"), axis=0, tiled=True),
        lax.all_gather(attn_local[5], ("batch", "seq"), axis=0, tiled=True),
        lax.all_gather(attn_local[6], ("batch", "seq"), axis=0, tiled=True),
        lax.all_gather(attn_local[7], ("batch", "seq"), axis=0, tiled=True),
        lax.all_gather(attn_local[8], ("batch", "seq"), axis=0, tiled=True),
    )
    queries = (matmul(inputs, query_full) + query_add.astype(jnp.float32)).astype(jnp.bfloat16)
    keys = matmul(inputs, key_full).astype(jnp.bfloat16)
    values = (matmul(inputs, value_full) + value_add.astype(jnp.float32)).astype(jnp.bfloat16)
    mask_routed = (
        jnp.take(mask_float, sources.T).astype(jnp.bfloat16).reshape(owners, per_owner, head_count)
    )
    sent_query, sent_key, sent_value = to_owner((queries, keys, values), sources, owners)
    routed = (
        lax.all_to_all(sent_query, "seq", split_axis=0, concat_axis=0, tiled=True),
        lax.all_to_all(sent_key, "seq", split_axis=0, concat_axis=0, tiled=True),
        lax.all_to_all(sent_value, "seq", split_axis=0, concat_axis=0, tiled=True),
        lax.all_to_all(mask_routed, "seq", split_axis=0, concat_axis=0, tiled=True),
    )
    clus_query = to_clusters(routed[0], head_count)
    clus_key = to_clusters(routed[1], head_count)
    clus_value = to_clusters(routed[2], head_count)
    per_source = CLUSTER // owners
    dev_blocks = per_owner // per_source
    clus_mask = routed[3].reshape(owners, dev_blocks, per_source, head_count).transpose(3, 1, 0, 2)
    clus_mask = clus_mask.reshape(head_count, dev_blocks, CLUSTER).astype(jnp.float32)

    def attend_head(operands):
        head_query, head_key, head_value = operands
        scores = (
            jnp.einsum("cid,cjd->cij", head_query, head_key, preferred_element_type=jnp.float32)
            * scale
        )
        top = jnp.max(scores, axis=-1, keepdims=True)
        weights = jnp.exp(scores - top)
        totals = jnp.sum(weights, axis=-1, keepdims=True)
        probs = weights / totals
        log_total = top[..., 0] + jnp.log(totals[..., 0])
        mixed = jnp.einsum(
            "cij,cjd->cid",
            probs.astype(jnp.bfloat16),
            head_value,
            preferred_element_type=jnp.float32,
        ).astype(jnp.bfloat16)
        entropy = log_total - jnp.sum(probs * scores, axis=-1)
        return (mixed, log_total, entropy)

    attended_clus, log_totals, entropies = lax.map(attend_head, (clus_query, clus_key, clus_value))
    factor = 1.0 / (head_count * CLUSTER * sequences)
    entropy_sum = jnp.sum(entropies * clus_mask, axis=(0, 2)) * factor
    occupancy = jnp.sum(clus_mask, axis=(0, 2)) * factor
    cluster_stats = lax.psum(jnp.stack([entropy_sum, occupancy]), "batch")
    returned = lax.all_to_all(
        from_clusters(attended_clus, owners), "seq", split_axis=0, concat_axis=0, tiled=True
    )
    attended = from_owner((returned,), places)[0]
    branch = matmul(attended, out_full) + out_add.astype(jnp.float32)
    hidden_f, first_back = jax.vjp(
        layer_norm,
        inputs.astype(jnp.float32) + branch,
        gain_first.astype(jnp.float32),
        shift_first.astype(jnp.float32),
    )
    hidden = hidden_f.astype(jnp.bfloat16)
    up_full, down_full, up_add, down_add, gain_second, shift_second = (
        lax.all_gather(ffn_local[0], ("batch", "seq"), axis=0, tiled=True),
        lax.all_gather(ffn_local[1], ("batch", "seq"), axis=0, tiled=True),
        lax.all_gather(ffn_local[2], ("batch", "seq"), axis=0, tiled=True),
        lax.all_gather(ffn_local[3], ("batch", "seq"), axis=0, tiled=True),
        lax.all_gather(ffn_local[4], ("batch", "seq"), axis=0, tiled=True),
        lax.all_gather(ffn_local[5], ("batch", "seq"), axis=0, tiled=True),
    )
    up_pre = matmul(hidden, up_full) + up_add.astype(jnp.float32)
    act_f, gelu_back = jax.vjp(gelu_exact, up_pre)
    act = act_f.astype(jnp.bfloat16)
    ffn_out = matmul(act, down_full) + down_add.astype(jnp.float32)
    result, second_back = jax.vjp(
        layer_norm,
        hidden.astype(jnp.float32) + ffn_out,
        gain_second.astype(jnp.float32),
        shift_second.astype(jnp.float32),
    )
    output = result.astype(jnp.bfloat16)
    up_full, down_full, up_add, down_add, gain_second, shift_second = (
        lax.all_gather(ffn_local[0], ("batch", "seq"), axis=0, tiled=True),
        lax.all_gather(ffn_local[1], ("batch", "seq"), axis=0, tiled=True),
        lax.all_gather(ffn_local[2], ("batch", "seq"), axis=0, tiled=True),
        lax.all_gather(ffn_local[3], ("batch", "seq"), axis=0, tiled=True),
        lax.all_gather(ffn_local[4], ("batch", "seq"), axis=0, tiled=True),
        lax.all_gather(ffn_local[5], ("batch", "seq"), axis=0, tiled=True),
    )
    gout = out_grad[0].astype(jnp.float32) * mask_float[:, None]
    d_pre, grad_gain_two, grad_shift_two = second_back(gout)
    d_ffn = d_pre.astype(jnp.bfloat16)
    grad_down_add = jnp.sum(d_ffn.astype(jnp.float32), axis=0)
    grad_down = jnp.einsum("tf,td->fd", act, d_ffn, preferred_element_type=jnp.float32)
    d_act = jnp.einsum("td,fd->tf", d_ffn, down_full, preferred_element_type=jnp.float32)
    d_up = gelu_back(d_act)[0].astype(jnp.bfloat16)
    grad_up_add = jnp.sum(d_up.astype(jnp.float32), axis=0)
    grad_up = jnp.einsum("td,tf->df", hidden, d_up, preferred_element_type=jnp.float32)
    d_hidden = d_pre + jnp.einsum("tf,df->td", d_up, up_full, preferred_element_type=jnp.float32)
    ffn_grads = (
        lax.psum_scatter(grad_up, ("batch", "seq"), scatter_dimension=0, tiled=True),
        lax.psum_scatter(grad_down, ("batch", "seq"), scatter_dimension=0, tiled=True),
        lax.psum_scatter(grad_up_add, ("batch", "seq"), scatter_dimension=0, tiled=True),
        lax.psum_scatter(grad_down_add, ("batch", "seq"), scatter_dimension=0, tiled=True),
        lax.psum_scatter(grad_gain_two, ("batch", "seq"), scatter_dimension=0, tiled=True),
        lax.psum_scatter(grad_shift_two, ("batch", "seq"), scatter_dimension=0, tiled=True),
    )
    (
        query_full,
        key_full,
        value_full,
        out_full,
        query_add,
        value_add,
        out_add,
        gain_first,
        shift_first,
    ) = (
        lax.all_gather(attn_local[0], ("batch", "seq"), axis=0, tiled=True),
        lax.all_gather(attn_local[1], ("batch", "seq"), axis=0, tiled=True),
        lax.all_gather(attn_local[2], ("batch", "seq"), axis=0, tiled=True),
        lax.all_gather(attn_local[3], ("batch", "seq"), axis=0, tiled=True),
        lax.all_gather(attn_local[4], ("batch", "seq"), axis=0, tiled=True),
        lax.all_gather(attn_local[5], ("batch", "seq"), axis=0, tiled=True),
        lax.all_gather(attn_local[6], ("batch", "seq"), axis=0, tiled=True),
        lax.all_gather(attn_local[7], ("batch", "seq"), axis=0, tiled=True),
        lax.all_gather(attn_local[8], ("batch", "seq"), axis=0, tiled=True),
    )
    d_mid, grad_gain_one, grad_shift_one = first_back(d_hidden)
    d_branch = d_mid.astype(jnp.bfloat16)
    grad_out_add = jnp.sum(d_branch.astype(jnp.float32), axis=0)
    grad_out = jnp.einsum("ti,to->io", attended, d_branch, preferred_element_type=jnp.float32)
    d_att = jnp.einsum("to,io->ti", d_branch, out_full, preferred_element_type=jnp.float32).astype(
        jnp.bfloat16
    )
    routed_grad = lax.all_to_all(
        to_owner((d_att,), sources, owners)[0], "seq", split_axis=0, concat_axis=0, tiled=True
    )
    clus_grad = to_clusters(routed_grad, head_count)

    def head_back(operands):
        head_query, head_key, head_value, head_grad, head_log = operands
        scores = (
            jnp.einsum("cid,cjd->cij", head_query, head_key, preferred_element_type=jnp.float32)
            * scale
        )
        probs = jnp.exp(scores - head_log[..., None])
        d_value = jnp.einsum(
            "cij,cid->cjd",
            probs.astype(jnp.bfloat16),
            head_grad,
            preferred_element_type=jnp.float32,
        ).astype(jnp.bfloat16)
        d_prob = jnp.einsum(
            "cid,cjd->cij", head_grad, head_value, preferred_element_type=jnp.float32
        )
        inner = jnp.sum(probs * d_prob, axis=-1, keepdims=True)
        d_score = (probs * (d_prob - inner)).astype(jnp.bfloat16)
        d_query = (
            jnp.einsum("cij,cjd->cid", d_score, head_key, preferred_element_type=jnp.float32)
            * scale
        ).astype(jnp.bfloat16)
        d_key = (
            jnp.einsum("cij,cid->cjd", d_score, head_query, preferred_element_type=jnp.float32)
            * scale
        ).astype(jnp.bfloat16)
        return (d_query, d_key, d_value)

    d_clus_query, d_clus_key, d_clus_value = lax.map(
        head_back, (clus_query, clus_key, clus_value, clus_grad, log_totals)
    )
    grads_home = (
        lax.all_to_all(
            from_clusters(d_clus_query, owners), "seq", split_axis=0, concat_axis=0, tiled=True
        ),
        lax.all_to_all(
            from_clusters(d_clus_key, owners), "seq", split_axis=0, concat_axis=0, tiled=True
        ),
        lax.all_to_all(
            from_clusters(d_clus_value, owners), "seq", split_axis=0, concat_axis=0, tiled=True
        ),
    )
    d_queries, d_keys, d_values = from_owner((grads_home[0], grads_home[1], grads_home[2]), places)
    d_inputs = d_mid + jnp.einsum(
        "to,io->ti", d_queries, query_full, preferred_element_type=jnp.float32
    )
    d_inputs = d_inputs + jnp.einsum(
        "to,io->ti", d_keys, key_full, preferred_element_type=jnp.float32
    )
    d_inputs = d_inputs + jnp.einsum(
        "to,io->ti", d_values, value_full, preferred_element_type=jnp.float32
    )
    grad_tokens = d_inputs.astype(jnp.bfloat16)
    grad_query = jnp.einsum("ti,to->io", inputs, d_queries, preferred_element_type=jnp.float32)
    grad_key = jnp.einsum("ti,to->io", inputs, d_keys, preferred_element_type=jnp.float32)
    grad_value = jnp.einsum("ti,to->io", inputs, d_values, preferred_element_type=jnp.float32)
    grad_query_add = jnp.sum(d_queries.astype(jnp.float32), axis=0)
    grad_value_add = jnp.sum(d_values.astype(jnp.float32), axis=0)
    attn_grads = (
        lax.psum_scatter(grad_query, ("batch", "seq"), scatter_dimension=0, tiled=True),
        lax.psum_scatter(grad_key, ("batch", "seq"), scatter_dimension=0, tiled=True),
        lax.psum_scatter(grad_value, ("batch", "seq"), scatter_dimension=0, tiled=True),
        lax.psum_scatter(grad_out, ("batch", "seq"), scatter_dimension=0, tiled=True),
        lax.psum_scatter(grad_query_add, ("batch", "seq"), scatter_dimension=0, tiled=True),
        lax.psum_scatter(grad_value_add, ("batch", "seq"), scatter_dimension=0, tiled=True),
        lax.psum_scatter(grad_out_add, ("batch", "seq"), scatter_dimension=0, tiled=True),
        lax.psum_scatter(grad_gain_one, ("batch", "seq"), scatter_dimension=0, tiled=True),
        lax.psum_scatter(grad_shift_one, ("batch", "seq"), scatter_dimension=0, tiled=True),
    )
    return (
        output[None],
        grad_tokens[None],
        attn_grads[0],
        attn_grads[1],
        attn_grads[2],
        attn_grads[3],
        attn_grads[4],
        attn_grads[5],
        attn_grads[6],
        attn_grads[7],
        attn_grads[8],
        ffn_grads[0],
        ffn_grads[2],
        ffn_grads[1],
        ffn_grads[3],
        ffn_grads[4],
        ffn_grads[5],
        cluster_stats,
    )


def solution(mesh):
    return jax.shard_map(
        body,
        mesh=mesh,
        in_specs=(
            P("batch", "seq", None),
            P("batch", None, "seq"),
            P("batch", "seq"),
            P("batch", "seq", None),
            P(("batch", "seq"), None),
            P(("batch", "seq"), None),
            P(("batch", "seq"), None),
            P(("batch", "seq"), None),
            P(("batch", "seq")),
            P(("batch", "seq")),
            P(("batch", "seq")),
            P(("batch", "seq")),
            P(("batch", "seq")),
            P(("batch", "seq"), None),
            P(("batch", "seq")),
            P(("batch", "seq"), None),
            P(("batch", "seq")),
            P(("batch", "seq")),
            P(("batch", "seq")),
        ),
        out_specs=(
            P("batch", "seq", None),
            P("batch", "seq", None),
            P(("batch", "seq"), None),
            P(("batch", "seq"), None),
            P(("batch", "seq"), None),
            P(("batch", "seq"), None),
            P(("batch", "seq")),
            P(("batch", "seq")),
            P(("batch", "seq")),
            P(("batch", "seq")),
            P(("batch", "seq")),
            P(("batch", "seq"), None),
            P(("batch", "seq")),
            P(("batch", "seq"), None),
            P(("batch", "seq")),
            P(("batch", "seq")),
            P(("batch", "seq")),
            P(None, "seq"),
        ),
        check_vma=False,
    )
```

profile of v0, /device:TPU:0, one launch (start us, length us, event | category | flops | bytes accessed | tf_op | source)
XLA Modules:
  0.0 1654.2 jit_solution(4996622500704719033)
XLA Ops:
  17.0 42.4 %all-reduce.19 = (bf16[768]{0:T(1024)(128)(2,1)S(1)}, bf16[768]{0:T(1024)(128)(2,1)S(1)}, bf16[768]{0:T(1024)(128)(2,1)S(1)}, bf16[768]{0:T(1024)(128)(2,1)S(1)}...) all-reduce(bf16[768]{0:T(1024)(128)(2,1)S(1)} %dynamic-update-slice, ...), channel_id=1, replica_groups=mesh['batch'=4,'seq'=8] {'batch','seq'}, use_global_device_ids=true, to_apply=%add | all-reduce | flops 9216 | bytes 36864
  62.6 45.6 %scatter_custom_fusion = s32[12288]{0:T(1024)S(1)} fusion(s32[12288]{0:T(1024)S(1)} %reshape.464, s32[12288]{0:T(1024)S(1)} %reshape.466, s32[]{:T(128)} %copy.453), kind=kCustom, calls=%fused_computation.237 | custom fusion | bytes 49156
  108.3 3.2 add_convert_fusion.5
  114.2 9.8 all-gather.11.cloned.1.call-done
  129.6 50.6 %all-gather.9.cloned.1.call-done = bf16[768,768]{1,0:T(8,128)(2,1)} async-done(((bf16[24,768]{1,0:T(8,128)(2,1)}), bf16[768,768]{1,0:T(8,128)(2,1)}) %all-gather.9.cloned.1.call-update) | async-done | bytes 1179664 | tf_op jit(solution)/shard_map/all_gather | solution.py:140
  187.4 78.2 %while.82 = (s32[]{:T(128)}, bf16[12,1024,64]{1,2,0:T(8,128)(2,1)S(1)}, bf16[12,1024,64]{1,2,0:T(8,128)(2,1)S(1)}, bf16[12,1024,64]{1,2,0:T(8,128)(2,1)}, s32[12...) while((s32[]{:T(128)}, ...), condition=%wide.region_2.3_spmd.clone, body=%wide.region_1.2_spmd.clone.sunk | while | flops 405995520 | bytes 1203297 | solution.py:43
  270.1 4.4 all-to-all-start
  276.8 35.3 %all-to-all-done = bf16[8,128,768]{2,1,0:T(8,128)(2,1)} async-done(((bf16[8,128,768]{2,1,0:T(8,128)(2,1)}), bf16[8,128,768]{2,1,0:T(8,128)(2,1)}, u32[]{:S(2)}, u32[]{:S(2)}) %all-to-all-start) | async-done | bytes 1572896 | tf_op jit(solution)/shard_map/all_to_all | solution.py:157
  312.1 3.6 all-to-all-start.1
  319.5 33.4 %all-to-all-done.1 = bf16[8,128,768]{2,1,0:T(8,128)(2,1)S(1)} async-done(((bf16[8,128,768]{2,1,0:T(8,128)(2,1)}), bf16[8,128,768]{2,1,0:T(8,128)(2,1)S(1)}, u32[]{:S(2)}, u32[]{:S(2)}) %all-to-all-start.1) | async-done | bytes 1572896 | tf_op jit(solution)/shard_map/all_to_all | solution.py:158
  352.9 4.3 all-to-all-start.2
  358.4 5.9 reshape.428
  369.7 5.9 reshape.430
  381.1 13.6 all-to-all-done.2
  394.7 5.9 reshape.432
  406.4 39.2 %while.80 = (s32[]{:T(128)}, bf16[12,8,128,64]{2,3,1,0:T(8,128)(2,1)S(1)}, f32[12,8,128]{2,1,0:T(8,128)}, f32[12,8,128]{2,1,0:T(8,128)}, bf16[12,8,128,64]{2,3,1...) while((s32[]{:T(128)}, ...), condition=%wide.region_7.8_spmd, body=%wide.region_3.7_spmd.sunk | while | flops 35060736 | bytes 2677333 | solution.py:190
  449.8 5.7 copy.293
  455.5 6.2 reshape.435
  461.7 3.8 all-to-all-start.3
  469.6 45.6 %all-to-all-done.3 = bf16[8,128,768]{2,1,0:T(8,128)(2,1)S(1)} async-done(((bf16[8,128,768]{2,1,0:T(8,128)(2,1)}), bf16[8,128,768]{2,1,0:T(8,128)(2,1)S(1)}, u32[]{:S(2)}, u32[]{:S(2)}) %all-to-all-start.3) | async-done | bytes 1572896 | tf_op jit(solution)/shard_map/all_to_all | solution.py:195
  517.2 3.7 reshape_reshape.27
  522.2 31.0 %while.83 = (s32[]{:T(128)}, bf16[12,1024,64]{1,2,0:T(8,128)(2,1)}, s32[12,1024]{1,0:T(8,128)S(1)}, bf16[12,1024,64]{1,2,0:T(8,128)(2,1)}, s32[]{:T(128)}) while((s32[]{:T(128)}, bf16[12,1024,64]{1,2,0:T(8,128)(2,1)}, s32[12,1024]{1,0:T(8,128)S(1)}, bf16[12,1024,64]{1,2,0:T(8,128)(2,1)}, s32[]{:T(128)}) %tuple.205), condition=%wide.region_9.10_spmd.clone, body=%wide.region_8.9_spmd.clone.sunk | while | flops 135331840 | bytes 275521 | solution.py:43
  553.3 3.6 fusion.156
  558.9 37.9 %multiply_convert_fusion.1 = (bf16[1024,3072]{1,0:T(8,128)(2,1)}, f32[1024,3072]{1,0:T(8,128)}, f32[1024,3072]{1,0:T(8,128)}) fusion(f32[3072]{0:T(1024)S(1)} %convert_element_type.183, bf16[768,3072]{1,0:T(8,128)(2,1)} %all-gather.15.cloned.1.call-done, f32[1024,768]{0,1:T(8,128)} %copy-done.2, f32[768]{0:T(1024)S(1)} %convert_element_type.180, ...), kind=kOutput, calls=%fused_computation.143 | convolution fusion | flops 5043388416 | bytes 39348224 | tf_op jit(solution)/shard_map/dot_general | solution.py:24
  596.8 9.8 fusion.157
  609.9 3.5 convert_reduce_fusion.1
  613.4 18.1 %convert_reduce_fusion = (f32[3072]{0:T(1024)}, bf16[1024,3072]{1,0:T(8,128)(2,1)}) fusion(f32[1024,3072]{1,0:T(8,128)} %get-tuple-element.701, bf16[1024,768]{0,1:T(8,128)(2,1)S(1)} %get-tuple-element.695, bf16[3072,768]{1,0:T(8,128)(2,1)} %all-gather.17.cloned.1.call-done, f32[1024,3072]{1,0:T(8,128)} %get-tuple-element.713, ...), kind=kOutput, calls=%fused_computation.141 | convolution fusion | flops 4885312512 | bytes 37773312 | tf_op jit(solution)/shard_map/td,fd->tf/dot_general | solution.py:239
  631.5 11.7 multiply_reduce_fusion.2
  650.6 23.8 %while.84 = (s32[]{:T(128)}, bf16[12,1024,64]{1,2,0:T(8,128)(2,1)S(1)}, s32[12,1024]{1,0:T(8,128)S(1)}, bf16[12,1024,64]{2,1,0:T(8,128)(2,1)}, s32[]{:T(128)}) while((s32[]{:T(128)}, bf16[12,1024,64]{1,2,0:T(8,128)(2,1)S(1)}, s32[12,1024]{1,0:T(8,128)S(1)}, bf16[12,1024,64]{2,1,0:T(8,128)(2,1)}, s32[]{:T(128)}) %tuple.206), condition=%wide.region_19.20_spmd.clone, body=%wide.region_18.19_spmd.clone.sunk | while | flops 135331840 | bytes 406593 | solution.py:43
  676.8 3.6 all-to-all-start.4
  680.4 37.0 %all-to-all-done.4 = bf16[8,128,768]{2,1,0:T(8,128)(2,1)S(1)} async-done(((bf16[8,128,768]{2,1,0:T(8,128)(2,1)}), bf16[8,128,768]{2,1,0:T(8,128)(2,1)S(1)}, u32[]{:S(2)}, u32[]{:S(2)}) %all-to-all-start.4) | async-done | bytes 1572896 | tf_op jit(solution)/shard_map/all_to_all | solution.py:280
  717.3 3.8 reshape.438
  729.0 89.9 %while.81 = (s32[]{:T(128)}, bf16[12,8,128,64]{2,3,1,0:T(8,128)(2,1)S(1)}, bf16[12,8,128,64]{2,3,1,0:T(8,128)(2,1)S(1)}, bf16[12,8,128,64]{2,3,1,0:T(8,128)(2,1)...) while((s32[]{:T(128)}, ...), condition=%wide.region_22.23_spmd, body=%wide.region_20.22_spmd.sunk | while | flops 85261312 | bytes 5268585 | solution.py:313
  821.2 3.1 copy.305
  824.3 5.7 copy.306
  830.0 6.1 reshape.441
  836.1 4.5 all-to-all-start.5
  840.6 3.1 copy.308
  843.8 5.7 copy.309
  849.5 6.1 reshape.443
  855.6 21.7 %all-to-all-done.5 = bf16[8,128,768]{2,1,0:T(8,128)(2,1)} async-done(((bf16[8,128,768]{2,1,0:T(8,128)(2,1)}), bf16[8,128,768]{2,1,0:T(8,128)(2,1)}, u32[]{:S(2)}, u32[]{:S(2)}) %all-to-all-start.5) | async-done | bytes 1572896 | tf_op jit(solution)/shard_map/all_to_all | solution.py:317
  877.3 4.3 all-to-all-start.6
  881.6 3.1 copy.311
  884.7 5.7 copy.312
  890.4 6.2 reshape.445
  896.6 21.6 %all-to-all-done.6 = bf16[8,128,768]{2,1,0:T(8,128)(2,1)} async-done(((bf16[8,128,768]{2,1,0:T(8,128)(2,1)}), bf16[8,128,768]{2,1,0:T(8,128)(2,1)}, u32[]{:S(2)}, u32[]{:S(2)}) %all-to-all-start.6) | async-done | bytes 1572896 | tf_op jit(solution)/shard_map/all_to_all | solution.py:320
  918.2 3.6 all-to-all-start.7
  921.9 4.3 fusion.159
  935.1 23.9 %all-to-all-done.7 = bf16[8,128,768]{2,1,0:T(8,128)(2,1)S(1)} async-done(((bf16[8,128,768]{2,1,0:T(8,128)(2,1)}), bf16[8,128,768]{2,1,0:T(8,128)(2,1)S(1)}, u32[]{:S(2)}, u32[]{:S(2)}) %all-to-all-start.7) | async-done | bytes 1572896 | tf_op jit(solution)/shard_map/all_to_all | solution.py:323
  964.0 86.0 %while.85 = (s32[]{:T(128)}, bf16[12,1024,64]{1,2,0:T(8,128)(2,1)S(1)}, bf16[12,1024,64]{1,2,0:T(8,128)(2,1)}, bf16[12,1024,64]{1,2,0:T(8,128)(2,1)S(1)}, s32[12...) while((s32[]{:T(128)}, ...), condition=%wide.region_24.25_spmd.clone, body=%wide.region_23.24_spmd.clone.sunk | while | flops 405995520 | bytes 810081 | solution.py:43
  1050.0 4.3 convolution_bitcast_fusion.2
  1057.3 4.7 convolution_bitcast_fusion.1
  1065.2 4.3 convolution_bitcast_fusion
  1072.7 10.6 fusion.158
  1083.4 10.1 fusion.160
  1096.0 48.5 %gather_fusion = bf16[12288]{0:T(1024)(128)(2,1)S(1)} fusion(f32[1024]{0:T(1024)S(1)} %bitcast.409, s32[12288]{0:T(1024)S(1)} %broadcast_clamp_fusion), kind=kCustom, calls=%fused_computation | custom fusion | bytes 98304 | tf_op jit(solution)/shard_map/jit(_take)/gather | solution.py:153
  1146.0 3.7 all-to-all-start.8
  1149.6 6.7 all-to-all-done.8
  1161.4 6.2 psum.7
  1170.9 39.5 %all-reduce.18 = (f32[768]{0:T(1024)S(1)}, f32[768]{0:T(1024)S(1)}, f32[768]{0:T(1024)S(1)}, f32[768]{0:T(1024)S(1)}, f32[768]{0:T(1024)S(1)}, /*index=5*/f32[30...) all-reduce(f32[768]{0:T(1024)S(1)} %reduce_sum.252, ...), channel_id=6, replica_groups=mesh['batch'=4,'seq'=8] {'batch','seq'}, use_global_device_ids=true, to_apply=%region_30.31.clone | all-reduce | flops 9216 | bytes 73728
  1223.9 35.5 %reduce-scatter.21.cloned.1.call-done = f32[24,768]{1,0:T(8,128)} async-done(((f32[768,768]{1,0:T(8,128)}), f32[24,768]{1,0:T(8,128)}) %reduce-scatter.21.cloned.1.call-update) | async-done | bytes 73744
  1259.4 104.6 %reduce-scatter.23.cloned.1.call-done = f32[24,768]{1,0:T(8,128)} async-done(((f32[768,768]{1,0:T(8,128)}), f32[24,768]{1,0:T(8,128)}) %reduce-scatter.23.cloned.1.call-update) | async-done | bytes 73744
  1364.0 141.2 %reduce-scatter.15.cloned.1.call-done = f32[24,3072]{1,0:T(8,128)} async-done(((f32[768,3072]{1,0:T(8,128)}), f32[24,3072]{1,0:T(8,128)}) %reduce-scatter.15.cloned.1.call-update) | async-done | bytes 294928 | tf_op jit(solution)/shard_map/reduce_scatter | solution.py:245
  1505.2 141.9 %reduce-scatter.17.cloned.1.call-done = f32[96,768]{1,0:T(8,128)} async-done(((f32[3072,768]{1,0:T(8,128)}), f32[96,768]{1,0:T(8,128)}) %reduce-scatter.17.cloned.1.call-update) | async-done | bytes 294928 | tf_op jit(solution)/shard_map/reduce_scatter | solution.py:246
  (520 shorter events, 489.0 us)
Async XLA Ops:
  7.2 101.1 %all-gather.7.cloned.1.call-start = ((), (), s32[]{:S(2)}) async-start(), calls=%async_computation.15 | async-start | bytes 1216512 | tf_op jit(solution)/shard_map/all_gather | solution.py:139
  7.9 116.1 %all-gather.11.cloned.1.call-start = ((), (), s32[]{:S(2)}) async-start(), calls=%async_computation.17 | async-start | bytes 1216512 | tf_op jit(solution)/shard_map/all_gather | solution.py:141
  8.7 171.5 %all-gather.9.cloned.1.call-start = ((), (), s32[]{:S(2)}) async-start(), calls=%async_computation.16 | async-start | bytes 1216512 | tf_op jit(solution)/shard_map/all_gather | solution.py:140
  111.5 12.6 copy-start.8
  265.5 4.6 copy-start.16
  270.1 42.0 %all-to-all-start = ((bf16[8,128,768]{2,1,0:T(8,128)(2,1)}), bf16[8,128,768]{2,1,0:T(8,128)(2,1)}, u32[]{:S(2)}, u32[]{:S(2)}) async-start(bf16[8,128,768]{2,1,0:T(8,128)(2,1)} %copy.283), calls=%async_computation | async-start | bytes 3145728 | tf_op jit(solution)/shard_map/all_to_all | solution.py:157
  312.1 40.8 %all-to-all-start.1 = ((bf16[8,128,768]{2,1,0:T(8,128)(2,1)}), bf16[8,128,768]{2,1,0:T(8,128)(2,1)S(1)}, u32[]{:S(2)}, u32[]{:S(2)}) async-start(bf16[8,128,768]{2,1,0:T(8,128)(2,1)} %copy.285), calls=%async_computation.1 | async-start | bytes 3145728 | tf_op jit(solution)/shard_map/all_to_all | solution.py:158
  352.9 11.4 copy-start.4
  352.9 41.7 %all-to-all-start.2 = ((bf16[8,128,768]{2,1,0:T(8,128)(2,1)}), bf16[8,128,768]{2,1,0:T(8,128)(2,1)}, u32[]{:S(2)}, u32[]{:S(2)}) async-start(bf16[8,128,768]{2,1,0:T(8,128)(2,1)} %copy.287), calls=%async_computation.2 | async-start | bytes 3145728 | tf_op jit(solution)/shard_map/all_to_all | solution.py:159
  357.2 196.1 %all-gather.13.cloned.1.call-start = ((), (), s32[]{:S(2)}) async-start(), calls=%async_computation.18 | async-start | bytes 1216512 | tf_op jit(solution)/shard_map/all_gather | solution.py:142
  357.8 201.1 %all-gather.15.cloned.1.call-start = ((), (), s32[]{:S(2)}) async-start(), calls=%async_computation.19 | async-start | bytes 4866048 | tf_op jit(solution)/shard_map/all_gather | solution.py:208
  445.6 1.1 copy-start.5
  455.5 10.5 copy-start.9
  461.7 6.0 copy-start.27
  461.7 53.5 %all-to-all-start.3 = ((bf16[8,128,768]{2,1,0:T(8,128)(2,1)}), bf16[8,128,768]{2,1,0:T(8,128)(2,1)S(1)}, u32[]{:S(2)}, u32[]{:S(2)}) async-start(bf16[8,128,768]{2,1,0:T(8,128)(2,1)} %reshape.435), calls=%async_computation.3 | async-start | bytes 3145728 | tf_op jit(solution)/shard_map/all_to_all | solution.py:195
  465.5 131.4 %all-gather.17.cloned.1.call-start = ((), (), s32[]{:S(2)}) async-start(), calls=%async_computation.20 | async-start | bytes 4866048 | tf_op jit(solution)/shard_map/all_gather | solution.py:209
  466.0 3.5 copy-start.18
  522.2 31.1 %copy-start.10 = (bf16[1,1024,768]{1,2,0:T(8,128)(2,1)S(1)}, bf16[1,1024,768]{1,2,0:T(8,128)(2,1)}, u32[]{:S(2)}) copy-start(bf16[1,1024,768]{1,2,0:T(8,128)(2,1)} %copy.279) | copy-start | bytes 4718596
  553.3 3.6 copy-start.19
  556.9 1.6 copy-start.2
  613.4 18.1 %copy-start.14 = (bf16[1024,768]{0,1:T(8,128)(2,1)}, bf16[1024,768]{0,1:T(8,128)(2,1)S(1)}, u32[]{:S(2)}) copy-start(bf16[1024,768]{0,1:T(8,128)(2,1)S(1)} %get-tuple-element.695) | copy-start | bytes 4718596
  631.5 11.7 copy-start.3
  644.0 3.6 copy-start
  644.0 2.1 copy-start.31
  644.0 3.5 copy-start.20
  645.0 2.6 copy-start.13
  647.6 3.0 copy-start.17
  676.8 40.6 %all-to-all-start.4 = ((bf16[8,128,768]{2,1,0:T(8,128)(2,1)}), bf16[8,128,768]{2,1,0:T(8,128)(2,1)S(1)}, u32[]{:S(2)}, u32[]{:S(2)}) async-start(bf16[8,128,768]{2,1,0:T(8,128)(2,1)} %copy.299), calls=%async_computation.4 | async-start | bytes 3145728 | tf_op jit(solution)/shard_map/all_to_all | solution.py:280
  818.8 1.1 copy-start.6
  820.0 1.2 copy-start.7
  836.1 41.1 %all-to-all-start.5 = ((bf16[8,128,768]{2,1,0:T(8,128)(2,1)}), bf16[8,128,768]{2,1,0:T(8,128)(2,1)}, u32[]{:S(2)}, u32[]{:S(2)}) async-start(bf16[8,128,768]{2,1,0:T(8,128)(2,1)} %reshape.441), calls=%async_computation.5 | async-start | bytes 3145728 | tf_op jit(solution)/shard_map/all_to_all | solution.py:317
  877.3 40.9 %all-to-all-start.6 = ((bf16[8,128,768]{2,1,0:T(8,128)(2,1)}), bf16[8,128,768]{2,1,0:T(8,128)(2,1)}, u32[]{:S(2)}, u32[]{:S(2)}) async-start(bf16[8,128,768]{2,1,0:T(8,128)(2,1)} %reshape.443), calls=%async_computation.6 | async-start | bytes 3145728 | tf_op jit(solution)/shard_map/all_to_all | solution.py:320
  890.4 31.4 %copy-start.12 = (bf16[12,1024,64]{1,2,0:T(8,128)(2,1)S(1)}, bf16[12,1024,64]{1,2,0:T(8,128)(2,1)}, u32[]{:S(2)}) copy-start(bf16[12,1024,64]{1,2,0:T(8,128)(2,1)} %get-tuple-element.262) | copy-start | bytes 4718596
  918.2 40.8 %all-to-all-start.7 = ((bf16[8,128,768]{2,1,0:T(8,128)(2,1)}), bf16[8,128,768]{2,1,0:T(8,128)(2,1)S(1)}, u32[]{:S(2)}, u32[]{:S(2)}) async-start(bf16[8,128,768]{2,1,0:T(8,128)(2,1)} %reshape.445), calls=%async_computation.7 | async-start | bytes 3145728 | tf_op jit(solution)/shard_map/all_to_all | solution.py:323
  921.8 302.0 %reduce-scatter.13.cloned.1.call-start = ((), (), s32[]{:S(2)}) async-start(), calls=%async_computation.21 | async-start | bytes 2433024 | tf_op jit(solution)/shard_map/reduce_scatter | solution.py:347
  926.2 297.7 %reduce-scatter.19.cloned.1.call-start = ((), (), s32[]{:S(2)}) async-start(), calls=%async_computation.24 | async-start | bytes 2433024
  1057.3 202.1 %reduce-scatter.21.cloned.1.call-start = ((), (), s32[]{:S(2)}) async-start(), calls=%async_computation.25 | async-start | bytes 2433024
  1065.2 298.8 %reduce-scatter.23.cloned.1.call-start = ((), (), s32[]{:S(2)}) async-start(), calls=%async_computation.26 | async-start | bytes 2433024
  1072.7 432.6 %reduce-scatter.15.cloned.1.call-start = ((), (), s32[]{:S(2)}) async-start(), calls=%async_computation.22 | async-start | bytes 9732096 | tf_op jit(solution)/shard_map/reduce_scatter | solution.py:245
  1083.4 563.8 %reduce-scatter.17.cloned.1.call-start = ((), (), s32[]{:S(2)}) async-start(), calls=%async_computation.23 | async-start | bytes 9732096 | tf_op jit(solution)/shard_map/reduce_scatter | solution.py:246
  1146.0 10.4 all-to-all-start.8
  1167.6 3.2 copy-start.22
  1167.6 3.2 copy-start.23
  1167.6 3.2 copy-start.24
  1167.6 3.2 copy-start.25
  1167.6 3.3 copy-start.26
  1167.7 3.3 copy-start.28
  1167.7 3.3 copy-start.29
  1215.1 2.8 copy-start.11
  1215.1 2.8 copy-start.30
  1218.0 1.9 copy-start.1
  1218.0 2.3 copy-start.15
  1218.0 2.3 copy-start.21
Sparse Core Ops, SparseCore 0:
  11.0 57.0 all-gather.6
  71.1 52.9 all-gather.10
  127.0 53.0 all-gather.8
  360.7 63.0 all-gather.12
  426.7 83.8 all-gather.14
  513.4 60.9 all-gather.16
  928.5 100.5 reduce-scatter.12
  1057.4 98.1 reduce-scatter.18
  1161.5 97.8 reduce-scatter.20
  1266.0 97.9 reduce-scatter.22
  1370.5 134.6 reduce-scatter.14
  1512.6 134.5 reduce-scatter.16
where the time goes:
time: 1670 us; the launch traced here: 1650 us
  waiting for transfers between devices  726 us (43%)
  matrix products  453 us (27%)
  local copies, waits for them, and re-layouts  309 us (19%)
  blocking collectives  88.1 us (5%)
  starting transfers between devices  36.8 us (2%)
  other arithmetic  24.4 us (1%)
    dot_general x96, matrix products, one_head(): jnp.dot(picker, head_part, preferred_element_type=jnp.float32)  209 us
    unnamed x15, waiting for transfers between devices  143 us
    reduce_scatter x1, waiting for transfers between devices, body(): lax.psum_scatter(grad_down, ('batch', 'seq'), scatter_dimension=0, tiled=...  142 us
    reduce_scatter x1, waiting for transfers between devices, body(): lax.psum_scatter(grad_up, ('batch', 'seq'), scatter_dimension=0, tiled=True)  141 us
    unnamed x105, local copies, waits for them, and re-layouts  86.7 us
    unnamed x2, blocking collectives  81.9 us
    dot_general x6, matrix products, matmul(): return jnp.dot(left, right, preferred_element_type=jnp.float32)  59.9 us
    all_gather x1, waiting for transfers between devices, body(): lax.all_gather(attn_local[1], ('batch', 'seq'), axis=0, tiled=True)  50.6 us
  transfers between devices with their start and end apart: 21, of which 15 were waited for; matrix products, arithmetic and copies ran while one was open for 30% of the time, Pallas kernels for 0%

commit v1 on v0

v1 whole, which is shorter than its diff:
```python
import functools

import jax
import jax.numpy as jnp
from jax import lax
from jax.experimental import pallas as pl
from jax.experimental.pallas import tpu as pltpu
from jax.sharding import PartitionSpec as P

MESH = pl.DeviceIdType.MESH
F32 = jnp.float32
BF16 = jnp.bfloat16
EPSILON = 1e-12
CLUSTER = 128
PAIR = 128
Z = 4
VMEM_LIMIT = 58 * 1024 * 1024


class Grid:
    def __init__(self, mesh):
        self.batch, self.seq = mesh.shape["batch"], mesh.shape["seq"]
        self.Y, self.X = self.batch // 2, self.seq // Z
        self.half = self.seq // 2
        self.n = self.batch * self.seq

    def swap_pairs(self):
        pairs = []
        for b in range(self.batch):
            for s in range(self.seq):
                if b % 2 == s // self.half:
                    to = (b, s)
                else:
                    to = (b ^ 1, (s + self.half) % self.seq)
                pairs.append((b * self.seq + s, to[0] * self.seq + to[1]))
        return pairs


def coords(g):
    b, s = lax.axis_index("batch"), lax.axis_index("seq")
    return b // 2, b % 2, s // g.X, s % g.X


def device(g, y, c, z, x):
    return (y * 2 + c, z * g.X + x)


def group_place(g):
    b, s = lax.axis_index("batch"), lax.axis_index("seq")
    return b % 2 * g.half + s % g.half


def group_device(g, place):
    b, s = lax.axis_index("batch"), lax.axis_index("seq")
    return (b // 2 * 2 + place // g.half, s // g.half * g.half + place % g.half)


def line_peers(g):
    y, c, z, x = coords(g)
    peers = [device(g, y, c, (z + k) % Z, x) for k in range(1, Z)]
    peers += [device(g, y, c, z, (x + k) % g.X) for k in range(1, g.X)]
    peers += [device(g, (y + k) % g.Y, c, z, x) for k in range(1, g.Y)]
    peers.append(device(g, y, 1 - c, z, x))
    return peers


def greet(peers):
    barrier = pltpu.get_barrier_semaphore()
    for peer in peers:
        pl.semaphore_signal(barrier, inc=1, device_id=peer, device_id_type=MESH)
    pl.semaphore_wait(barrier, len(peers))


def remote(src, dst, send, recv, peer):
    return pltpu.make_async_remote_copy(
        src_ref=src,
        dst_ref=dst,
        send_sem=send,
        recv_sem=recv,
        device_id=peer,
        device_id_type=MESH,
    )


def lane_pieces(shape):
    rows, cols = shape
    if cols % PAIR or rows * cols <= 24 * 768:
        return [(0, cols)]
    count = {3072: 4, 768: 3}.get(cols, 1)
    return [(k * (cols // count), cols // count) for k in range(count)]


def gather_kernel(g, shapes, *refs):
    n = len(shapes)
    ins, outs = refs[:n], refs[n : 2 * n]
    sends, recvs, local_sem = refs[2 * n :]
    y, c, z, x = coords(g)
    greet(line_peers(g))

    units = []
    for index, shape in enumerate(shapes):
        for start, size in lane_pieces(shape):
            units.append((index, pl.ds(start, size)))
    stages = []
    slot = 0
    for number, (index, cols) in enumerate(units):
        src, out = ins[index], outs[index]

        def put(peer, part, slot, src=None, out=out, cols=cols):
            view = out.at[(*part, slice(None), cols)]
            return remote(
                view if src is None else src, view, sends.at[slot], recvs.at[slot], peer
            )

        own = pltpu.make_async_copy(
            src.at[:, cols], out.at[y, c, z, x, :, cols], local_sem.at[number]
        )
        a, w = slice(None), []
        w.append(
            [
                put(device(g, y, c, (z + k) % Z, x), (y, c, z, x), slot + k - 1, src.at[:, cols])
                for k in range(1, Z)
            ]
        )
        slot += Z - 1
        if number % 2 == 0:
            plan = [("x", (y, c, a, x)), ("y", (y, c, a, a))]
        else:
            plan = [("y", (y, c, a, x)), ("x", (a, c, a, x))]
        for axis, part in plan:
            if axis == "x":
                moves = [
                    put(device(g, y, c, z, (x + k) % g.X), part, slot + k - 1)
                    for k in range(1, g.X)
                ]
            else:
                moves = [
                    put(device(g, (y + k) % g.Y, c, z, x), part, slot + k - 1)
                    for k in range(1, g.Y)
                ]
            slot += len(moves)
            w.append(moves)
        w.append([put(device(g, y, 1 - c, z, x), (a, c, a, a), slot)])
        slot += 1
        stages.append((own, w))

    count = len(units)
    lead = 2
    for t in range(count + lead + 3):
        if t < count:
            own, w = stages[t]
            own.start()
            for copy in w[0]:
                copy.start()
        for level in range(1, 4):
            u = t - lead - level + 1
            if 0 <= u < count:
                own, w = stages[u]
                if level == 1:
                    own.wait()
                for copy in w[level - 1]:
                    copy.wait_recv()
                for copy in w[level]:
                    copy.start()
    for own, w in stages:
        w[3][0].wait_recv()
        for moves in w:
            for copy in moves:
                copy.wait_send()


def gather(g, arrays):
    shapes = [item.shape for item in arrays]
    units = sum(len(lane_pieces(shape)) for shape in shapes)
    slots = units * (Z + g.X + g.Y - 2)
    return pl.pallas_call(
        functools.partial(gather_kernel, g, shapes),
        out_shape=[
            jax.ShapeDtypeStruct((g.Y, 2, Z, g.X, *item.shape), item.dtype) for item in arrays
        ],
        in_specs=[pl.BlockSpec(memory_space=pl.ANY)] * len(arrays),
        out_specs=[pl.BlockSpec(memory_space=pl.ANY)] * len(arrays),
        scratch_shapes=[
            pltpu.SemaphoreType.DMA((slots,)),
            pltpu.SemaphoreType.DMA((slots,)),
            pltpu.SemaphoreType.DMA((units,)),
        ],
        compiler_params=pltpu.CompilerParams(
            collective_id=0, has_side_effects=True, vmem_limit_bytes=VMEM_LIMIT
        ),
        name="weight_gather",
    )(*arrays)


def scatter_kernel(g, shapes, *refs):
    n = len(shapes)
    ins, outs = refs[:n], refs[n : 2 * n]
    by_core, by_one, by_two, by_z = (refs[(2 + k) * n : (3 + k) * n] for k in range(4))
    sends, recvs = refs[6 * n :]
    y, c, z, x = coords(g)
    greet(line_peers(g))

    units = []
    for index, shape in enumerate(shapes):
        for start, size in lane_pieces(shape):
            units.append((index, slice(start, start + size)))

    per = Z + g.X + g.Y - 2

    def copies(number, level):
        index, cols = units[number]
        base = number * per
        every = slice(None)
        first_y = index % 2 == 0
        if level == 0:
            return [
                remote(
                    ins[index].at[:, 1 - c, :, :, :, cols],
                    by_core[index].at[:, :, :, :, cols],
                    sends.at[base],
                    recvs.at[base],
                    device(g, y, 1 - c, z, x),
                )
            ]
        base += 1
        along = {1: "y" if first_y else "x", 2: "x" if first_y else "y", 3: "z"}[level]
        if level == 2:
            base += (g.Y if first_y else g.X) - 1
        if level == 3:
            base += g.Y + g.X - 2
        size = {"y": g.Y, "x": g.X, "z": Z}[along]
        moves = []
        for k in range(1, size):
            if along == "y":
                to = (y + k) % g.Y
                peer = device(g, to, c, z, x)
            elif along == "x":
                to = (x + k) % g.X
                peer = device(g, y, c, z, to)
            else:
                to = (z + k) % Z
                peer = device(g, y, c, to, x)
            if level == 1 and first_y:
                src = by_core[index].at[to, :, :, :, cols]
            elif level == 1:
                src = by_core[index].at[:, :, to, :, cols]
            elif level == 2 and first_y:
                src = by_one[index].at[0, :, to, :, cols]
            elif level == 2:
                src = by_one[index].at[0, to, :, :, cols]
            else:
                src = by_two[index].at[0, to, :, cols]
            held = (by_one, by_two, by_z)[level - 1][index]
            slot = 0 if level < 3 else 0
            dst = held.at[(k, *([every] * (len(held.shape) - 2)), cols)]
            moves.append(remote(src, dst, sends.at[base + k - 1], recvs.at[base + k - 1], peer))
        return moves

    def add(number, level):
        index, cols = units[number]
        first_y = index % 2 == 0
        kind = ins[index].dtype
        if level == 0:

            def one(step, carry):
                for yy in range(g.Y):
                    for xx in range(g.X):
                        total = ins[index][yy, c, step, xx, :, cols].astype(F32)
                        total += by_core[index][yy, step, xx, :, cols].astype(F32)
                        by_core[index][yy, step, xx, :, cols] = total.astype(kind)
                return carry

            lax.fori_loop(0, Z, one, 0)
        elif level == 1:
            size, rest = (g.Y, g.X) if first_y else (g.X, g.Y)

            def one(step, carry):
                for r in range(rest):
                    if first_y:
                        total = by_core[index][y, step, r, :, cols].astype(F32)
                    else:
                        total = by_core[index][r, step, x, :, cols].astype(F32)
                    for k in range(1, size):
                        if first_y:
                            total += by_one[index][k, step, r, :, cols].astype(F32)
                        else:
                            total += by_one[index][k, r, step, :, cols].astype(F32)
                    if first_y:
                        by_one[index][0, step, r, :, cols] = total.astype(kind)
                    else:
                        by_one[index][0, r, step, :, cols] = total.astype(kind)
                return carry

            lax.fori_loop(0, Z, one, 0)
        elif level == 2:
            size = g.X if first_y else g.Y

            def one(step, carry):
                if first_y:
                    total = by_one[index][0, step, x, :, cols].astype(F32)
                else:
                    total = by_one[index][0, y, step, :, cols].astype(F32)
                for k in range(1, size):
                    total += by_two[index][k, step, :, cols].astype(F32)
                by_two[index][0, step, :, cols] = total.astype(kind)
                return carry

            lax.fori_loop(0, Z, one, 0)
        else:
            total = by_two[index][0, z, :, cols].astype(F32)
            for k in range(1, Z):
                total += by_z[index][k, :, cols].astype(F32)
            outs[index][:, cols] = total

    count = len(units)
    started = [[None] * 4 for _ in units]
    for t in range(count + 4):
        if t < count:
            started[t][0] = copies(t, 0)
            for copy in started[t][0]:
                copy.start()
        for level in range(4):
            u = t - level - 1
            if 0 <= u < count:
                for copy in started[u][level]:
                    copy.wait_recv()
                add(u, level)
                if level < 3:
                    started[u][level + 1] = copies(u, level + 1)
                    for copy in started[u][level + 1]:
                        copy.start()
    for levels in started:
        for moves in levels:
            for copy in moves:
                copy.wait_send()


def scatter(g, arrays):
    shapes = [item.shape[4:] for item in arrays]
    units = sum(len(lane_pieces(shape)) for shape in shapes)
    slots = units * (Z + g.X + g.Y - 2)
    scratch = [[], [], [], []]
    for index, (item, shape) in enumerate(zip(arrays, shapes)):
        scratch[0].append(pltpu.VMEM((g.Y, Z, g.X, *shape), item.dtype))
        if index % 2 == 0:
            scratch[1].append(pltpu.VMEM((g.Y, Z, g.X, *shape), item.dtype))
            scratch[2].append(pltpu.VMEM((g.X, Z, *shape), item.dtype))
        else:
            scratch[1].append(pltpu.VMEM((g.X, g.Y, Z, *shape), item.dtype))
            scratch[2].append(pltpu.VMEM((g.Y, Z, *shape), item.dtype))
        scratch[3].append(pltpu.VMEM((Z, *shape), item.dtype))
    return pl.pallas_call(
        functools.partial(scatter_kernel, g, shapes),
        out_shape=[jax.ShapeDtypeStruct(shape, F32) for shape in shapes],
        in_specs=[pl.BlockSpec(memory_space=pltpu.VMEM)] * len(arrays),
        out_specs=[pl.BlockSpec(memory_space=pltpu.VMEM)] * len(arrays),
        scratch_shapes=[item for level in scratch for item in level]
        + [pltpu.SemaphoreType.DMA((slots,)), pltpu.SemaphoreType.DMA((slots,))],
        compiler_params=pltpu.CompilerParams(
            collective_id=1, has_side_effects=True, vmem_limit_bytes=VMEM_LIMIT
        ),
        name="grad_scatter",
    )(*arrays)


def exchange_kernel(g, n, *refs):
    ins, outs = refs[:n], refs[n : 2 * n]
    sends, recvs, local_sem = refs[2 * n :]
    me = group_place(g)
    size = g.seq
    peers = [(me + k) % size for k in range(1, size)]
    greet([group_device(g, peer) for peer in peers])
    copies = []
    for index in range(n):
        own = pltpu.make_async_copy(
            ins[index].at[:, me], outs[index].at[:, me], local_sem.at[index]
        )
        own.start()
        for k, peer in enumerate(peers):
            slot = index * (size - 1) + k
            copy = remote(
                ins[index].at[:, peer],
                outs[index].at[:, me],
                sends.at[slot],
                recvs.at[slot],
                group_device(g, peer),
            )
            copy.start()
            copies.append(copy)
        copies.append(own)
    for copy in copies:
        copy.wait()


def exchange(g, arrays, number):
    n = len(arrays)
    return pl.pallas_call(
        functools.partial(exchange_kernel, g, n),
        out_shape=[jax.ShapeDtypeStruct(item.shape, item.dtype) for item in arrays],
        in_specs=[pl.BlockSpec(memory_space=pl.ANY)] * n,
        out_specs=[pl.BlockSpec(memory_space=pl.ANY)] * n,
        scratch_shapes=[
            pltpu.SemaphoreType.DMA((n * (g.seq - 1),)),
            pltpu.SemaphoreType.DMA((n * (g.seq - 1),)),
            pltpu.SemaphoreType.DMA((n,)),
        ],
        compiler_params=pltpu.CompilerParams(
            collective_id=number, has_side_effects=True, vmem_limit_bytes=VMEM_LIMIT
        ),
        name="exchange",
    )(*arrays)


def dot(left, right):
    return lax.dot_general(left, right, (((1,), (0,)), ((), ())), preferred_element_type=F32)


def dot_nt(left, right):
    return lax.dot_general(left, right, (((1,), (1,)), ((), ())), preferred_element_type=F32)


def dot_tn(left, right):
    return lax.dot_general(left, right, (((0,), (0,)), ((), ())), preferred_element_type=F32)


def head_lanes(shape):
    return lax.broadcasted_iota(jnp.int32, shape, 1) < PAIR // 2


def split_pair(value, axis=0):
    low = head_lanes(value.shape)
    zero = jnp.zeros_like(value)
    return jnp.concatenate(
        [jnp.where(low, value, zero), jnp.where(low, zero, value)], axis=axis
    )


def place_rows(places_ref, pair, start, size):
    tok = places_ref.shape[1]
    rows = lax.broadcasted_iota(jnp.int32, (size, tok), 0) + start
    parts = [
        (rows == places_ref[pl.ds(2 * pair + i, 1), :]).astype(F32).astype(BF16) for i in range(2)
    ]
    return jnp.concatenate(parts, axis=1)


def token_rows(cols_ref, pair, start, size):
    tok = cols_ref.shape[0]
    lanes = lax.broadcasted_iota(jnp.int32, (size, tok), 1)
    parts = [
        (lanes == cols_ref[pl.ds(start, size), 2 * pair + i : 2 * pair + i + 1])
        .astype(F32)
        .astype(BF16)
        for i in range(2)
    ]
    return jnp.concatenate(parts, axis=1)


def gather_rows(block_ref, lead, start, size, lanes):
    part = block_ref[(*lead, slice(None), pl.ds(start, size), lanes)]
    if size % 16:
        part = part.astype(F32)
    return part.reshape(part.shape[0] * size, part.shape[2]).astype(block_ref.dtype)


def spread_rows(value, sources, kind):
    size = value.shape[0] // sources
    if size % 16:
        return value.astype(F32).reshape(sources, size, value.shape[1]).astype(kind)
    return value.astype(kind).reshape(sources, size, value.shape[1])


ROWS = 256


def project_kernel(x_ref, wq_ref, wk_ref, wv_ref, bias_ref, places_ref, cols_ref, out_ref, mask_ref, rhs):
    tok = x_ref.shape[0]
    pairs = out_ref.shape[0]
    heads = 2 * pairs
    lanes = lax.broadcasted_iota(jnp.int32, (ROWS, PAIR), 1)
    for pair in range(pairs):
        head = slice(pair * PAIR, (pair + 1) * PAIR)

        def project(step, carry):
            rows = pl.ds(step * ROWS, ROWS)
            x = x_ref[rows, :]
            for part, w_ref in enumerate((wq_ref, wk_ref, wv_ref)):
                value = dot(x, w_ref[:, head]) + bias_ref[part : part + 1, head]
                value = value.astype(BF16)
                low = head_lanes(value.shape)
                zero = jnp.zeros_like(value)
                to = slice(part * PAIR, (part + 1) * PAIR)
                rhs[rows, to] = jnp.where(low, value, zero)
                rhs[pl.ds(tok + step * ROWS, ROWS), to] = jnp.where(low, zero, value)
            mask = cols_ref[rows, heads : heads + 1].astype(F32)
            for i in range(2):
                rhs[pl.ds(i * tok + step * ROWS, ROWS), 3 * PAIR :] = jnp.where(
                    lanes == 2 * pair + i, mask, 0.0
                ).astype(BF16)
            return carry

        lax.fori_loop(0, tok // ROWS, project, 0)

        def permute(step, carry):
            rows = pl.ds(step * ROWS, ROWS)
            picked = dot(place_rows(places_ref, pair, step * ROWS, ROWS), rhs[...])
            out_ref[pair, rows, :] = picked[:, : 3 * PAIR].astype(BF16)
            if pair == 0:
                mask_ref[rows, :] = picked[:, 3 * PAIR :].astype(BF16)
            else:
                mask_ref[rows, :] = mask_ref[rows, :] + picked[:, 3 * PAIR :].astype(BF16)
            return carry

        lax.fori_loop(0, tok // ROWS, permute, 0)


def vmem_call(kernel, out_shape, scratch, name):
    def call(*args):
        return pl.pallas_call(
            kernel,
            out_shape=out_shape,
            in_specs=[pl.BlockSpec(memory_space=pltpu.VMEM)] * len(args),
            out_specs=jax.tree.map(lambda _: pl.BlockSpec(memory_space=pltpu.VMEM), out_shape),
            scratch_shapes=scratch,
            compiler_params=pltpu.CompilerParams(vmem_limit_bytes=VMEM_LIMIT),
            name=name,
        )(*args)

    return call


def cluster_scores(q, k, scale):
    return dot_nt(q, k) * scale


def attend_kernel(scale, factor, qkv_ref, mask_ref, out_ref, stats_ref):
    pair = pl.program_id(0)
    _, sources, per_owner, _ = qkv_ref.shape
    size = CLUSTER // sources
    clusters = per_owner // size
    lanes = lax.broadcasted_iota(jnp.int32, (CLUSTER, PAIR), 1)
    spot = lax.broadcasted_iota(jnp.int32, stats_ref.shape, 1)
    row = lax.broadcasted_iota(jnp.int32, stats_ref.shape, 0)

    @pl.when(pair == 0)
    def _():
        stats_ref[...] = jnp.zeros_like(stats_ref)

    for cluster in range(clusters):
        q, k, v = (
            gather_rows(qkv_ref, (0,), cluster * size, size, slice(i * PAIR, (i + 1) * PAIR))
            for i in range(3)
        )
        scores = cluster_scores(split_pair(q), k, scale)
        top = jnp.max(scores, axis=1, keepdims=True)
        weights = jnp.exp(scores - top)
        totals = jnp.sum(weights, axis=1, keepdims=True)
        probs = weights / totals
        entropy = top + jnp.log(totals) - jnp.sum(probs * scores, axis=1, keepdims=True)
        low = probs.astype(BF16)
        mixed = dot(
            jnp.concatenate([low[:CLUSTER], low[CLUSTER:]], axis=1), split_pair(v)
        )
        out_ref[0, :, cluster * size : (cluster + 1) * size, :] = spread_rows(mixed, sources, BF16)
        mask = gather_rows(mask_ref, (), cluster * size, size, slice(None)).astype(F32)
        own = jnp.where(lanes == 2 * pair, entropy[:CLUSTER], 0.0) + jnp.where(
            lanes == 2 * pair + 1, entropy[CLUSTER:], 0.0
        )
        in_pair = (lanes == 2 * pair) | (lanes == 2 * pair + 1)
        entropy_sum = jnp.sum(own * mask) * factor
        count = jnp.sum(jnp.where(in_pair, mask, 0.0)) * factor
        stats_ref[...] += jnp.where(
            spot == cluster, jnp.where(row == 0, entropy_sum, jnp.where(row == 1, count, 0.0)), 0.0
        )


def attend(qkv, mask, scale, factor):
    pairs, sources, per_owner, width = qkv.shape
    return pl.pallas_call(
        functools.partial(attend_kernel, scale, factor),
        grid=(pairs,),
        out_shape=[
            jax.ShapeDtypeStruct((pairs, sources, per_owner, PAIR), BF16),
            jax.ShapeDtypeStruct((8, PAIR), F32),
        ],
        in_specs=[
            pl.BlockSpec((1, sources, per_owner, width), lambda i: (i, 0, 0, 0)),
            pl.BlockSpec((sources, per_owner, PAIR), lambda i: (0, 0, 0)),
        ],
        out_specs=[
            pl.BlockSpec((1, sources, per_owner, PAIR), lambda i: (i, 0, 0, 0)),
            pl.BlockSpec((8, PAIR), lambda i: (0, 0)),
        ],
        compiler_params=pltpu.CompilerParams(vmem_limit_bytes=VMEM_LIMIT),
        name="attend",
    )(qkv, mask)


def attend_back_kernel(scale, qkv_ref, grad_ref, out_ref):
    _, sources, per_owner, _ = qkv_ref.shape
    size = CLUSTER // sources
    clusters = per_owner // size
    for cluster in range(clusters):
        q, k, v = (
            gather_rows(qkv_ref, (0,), cluster * size, size, slice(i * PAIR, (i + 1) * PAIR))
            for i in range(3)
        )
        grad = gather_rows(grad_ref, (0,), cluster * size, size, slice(None))
        q2, g2 = split_pair(q), split_pair(grad)
        scores = cluster_scores(q2, k, scale)
        top = jnp.max(scores, axis=1, keepdims=True)
        weights = jnp.exp(scores - top)
        probs = weights / jnp.sum(weights, axis=1, keepdims=True)
        low = probs.astype(BF16)
        d_value = dot_tn(low, g2)
        d_prob = dot_nt(g2, v)
        inner = jnp.sum(probs * d_prob, axis=1, keepdims=True)
        d_score = (probs * (d_prob - inner)).astype(BF16)
        d_query = (
            dot(jnp.concatenate([d_score[:CLUSTER], d_score[CLUSTER:]], axis=1), split_pair(k))
            * scale
        )
        d_key = dot_tn(d_score, q2) * scale
        for i, value in enumerate((d_query, d_key, d_value)):
            out_ref[
                0, :, cluster * size : (cluster + 1) * size, i * PAIR : (i + 1) * PAIR
            ] = spread_rows(value, sources, BF16)


def attend_back(qkv, grad, scale):
    pairs, sources, per_owner, width = qkv.shape
    return pl.pallas_call(
        functools.partial(attend_back_kernel, scale),
        grid=(pairs,),
        out_shape=jax.ShapeDtypeStruct((pairs, sources, per_owner, width), BF16),
        in_specs=[
            pl.BlockSpec((1, sources, per_owner, width), lambda i: (i, 0, 0, 0)),
            pl.BlockSpec((1, sources, per_owner, PAIR), lambda i: (i, 0, 0, 0)),
        ],
        out_specs=pl.BlockSpec((1, sources, per_owner, width), lambda i: (i, 0, 0, 0)),
        compiler_params=pltpu.CompilerParams(vmem_limit_bytes=VMEM_LIMIT),
        name="attend_back",
    )(qkv, grad)


INV_SQRT2 = 0.7071067811865476
INV_SQRT_2PI = 0.3989422804014327


def norm_parts(value):
    centred = value - jnp.mean(value, axis=1, keepdims=True)
    rate = lax.rsqrt(jnp.mean(centred * centred, axis=1, keepdims=True) + EPSILON)
    return centred * rate, rate


def norm_back(grad, gain, normed, rate):
    inner = grad * gain
    return rate * (
        inner
        - jnp.mean(inner, axis=1, keepdims=True)
        - normed * jnp.mean(inner * normed, axis=1, keepdims=True)
    )


TILE = 256
COLS = 768


def middle_kernel(
    x_ref,
    att_ref,
    grad_ref,
    places_ref,
    cols_ref,
    wo_ref,
    up_ref,
    down_ref,
    vec_ref,
    up_bias_ref,
    out_ref,
    dmid_ref,
    datt_ref,
    g_out_ref,
    g_up_ref,
    g_down_ref,
    gvec_ref,
    g_upb_ref,
    attended,
    hidden_all,
    act_all,
    dup_all,
    dffn_all,
    datt_all,
    slope,
    ret,
):
    tok, width = x_ref.shape
    wide = up_ref.shape[1]
    pairs = att_ref.shape[0]
    heads = 2 * pairs
    gvec_ref[...] = jnp.zeros_like(gvec_ref)
    g_upb_ref[...] = jnp.zeros_like(g_upb_ref)
    bo, g1, s1, bd, g2, s2 = (vec_ref[i : i + 1, :] for i in range(6))

    def column_sum(value):
        return jnp.sum(value, axis=0, keepdims=True)

    for pair in range(pairs):
        to = slice(pair * PAIR, (pair + 1) * PAIR)

        def spread(step, carry):
            rows = pl.ds(step * TILE, TILE)
            value = att_ref[pair, rows, :]
            low = head_lanes(value.shape)
            zero = jnp.zeros_like(value)
            ret[rows, :] = jnp.where(low, value, zero)
            ret[pl.ds(tok + step * TILE, TILE), :] = jnp.where(low, zero, value)
            return carry

        lax.fori_loop(0, tok // TILE, spread, 0)

        def unpermute(step, carry):
            start = step * TILE
            attended[pl.ds(start, TILE), to] = dot(
                token_rows(cols_ref, pair, start, TILE), ret[...]
            ).astype(BF16)
            return carry

        lax.fori_loop(0, tok // TILE, unpermute, 0)

    def tile(step, carry):
        rows = pl.ds(step * TILE, TILE)
        branch = dot(attended[rows, :], wo_ref[...]) + bo
        n1, r1 = norm_parts(x_ref[rows, :].astype(F32) + branch)
        hidden = (n1 * g1 + s1).astype(BF16)
        hidden_all[rows, :] = hidden
        ffn = jnp.zeros((TILE, width), F32)
        for col in range(0, wide, COLS):
            to = slice(col, col + COLS)
            pre = dot(hidden, up_ref[:, to]) + up_bias_ref[0:1, to]
            cdf = 0.5 * (1.0 + lax.erf(pre * INV_SQRT2))
            act = (pre * cdf).astype(BF16)
            slope[:, to] = cdf + pre * (jnp.exp(-0.5 * pre * pre) * INV_SQRT_2PI)
            act_all[rows, to] = act
            ffn += dot(act, down_ref[to, :])
        n2, r2 = norm_parts(hidden.astype(F32) + ffn + bd)
        out_ref[rows, :] = (n2 * g2 + s2).astype(BF16)
        mask = cols_ref[rows, heads : heads + 1].astype(F32)
        gout = grad_ref[rows, :].astype(F32) * mask
        gvec_ref[4:5, :] += column_sum(gout * n2)
        gvec_ref[5:6, :] += column_sum(gout)
        d_pre = norm_back(gout, g2, n2, r2)
        d_ffn = d_pre.astype(BF16)
        dffn_all[rows, :] = d_ffn
        gvec_ref[3:4, :] += column_sum(d_ffn.astype(F32))
        d_hidden = d_pre
        for col in range(0, wide, COLS):
            to = slice(col, col + COLS)
            d_up = (dot_nt(d_ffn, down_ref[to, :]) * slope[:, to]).astype(BF16)
            dup_all[rows, to] = d_up
            g_upb_ref[0:1, to] += column_sum(d_up.astype(F32))
            d_hidden += dot_nt(d_up, up_ref[:, to])
        gvec_ref[1:2, :] += column_sum(d_hidden * n1)
        gvec_ref[2:3, :] += column_sum(d_hidden)
        d_mid = norm_back(d_hidden, g1, n1, r1)
        d_branch = d_mid.astype(BF16)
        dmid_ref[rows, :] = d_branch
        gvec_ref[0:1, :] += column_sum(d_branch.astype(F32))
        datt_all[rows, :] = dot_nt(d_branch, wo_ref[...]).astype(BF16)
        return carry

    lax.fori_loop(0, tok // TILE, tile, 0)

    for pair in range(pairs):
        to = slice(pair * PAIR, (pair + 1) * PAIR)

        def spread(step, carry):
            rows = pl.ds(step * TILE, TILE)
            value = datt_all[rows, to]
            low = head_lanes(value.shape)
            zero = jnp.zeros_like(value)
            ret[rows, :] = jnp.where(low, value, zero)
            ret[pl.ds(tok + step * TILE, TILE), :] = jnp.where(low, zero, value)
            return carry

        lax.fori_loop(0, tok // TILE, spread, 0)

        def permute(step, carry):
            start = step * TILE
            datt_ref[pair, pl.ds(start, TILE), :] = dot(
                place_rows(places_ref, pair, start, TILE), ret[...]
            ).astype(BF16)
            return carry

        lax.fori_loop(0, tok // TILE, permute, 0)

    def weights(step, carry):
        to = pl.ds(pl.multiple_of(step * TILE, TILE), TILE)
        g_down_ref[to, :] = dot_tn(act_all[:, to], dffn_all[...]).astype(BF16)
        g_up_ref[:, to] = dot_tn(hidden_all[...], dup_all[:, to]).astype(BF16)
        return carry

    lax.fori_loop(0, wide // TILE, weights, 0)

    def out_weights(step, carry):
        to = pl.ds(pl.multiple_of(step * TILE, TILE), TILE)
        g_out_ref[:, to] = dot_tn(attended[...], dmid_ref[:, to]).astype(BF16)
        return carry

    lax.fori_loop(0, width // TILE, out_weights, 0)


def final_kernel(
    x_ref,
    ret_ref,
    dmid_ref,
    cols_ref,
    wq_ref,
    wk_ref,
    wv_ref,
    gtok_ref,
    gq_ref,
    gk_ref,
    gv_ref,
    gvec_ref,
    rhs,
    dqkv,
):
    tok, width = x_ref.shape
    pairs = ret_ref.shape[0]
    gvec_ref[...] = jnp.zeros_like(gvec_ref)
    for pair in range(pairs):

        def spread(step, carry):
            rows = pl.ds(step * TILE, TILE)
            for part in range(3):
                to = slice(part * PAIR, (part + 1) * PAIR)
                value = ret_ref[pair, rows, to]
                low = head_lanes(value.shape)
                zero = jnp.zeros_like(value)
                rhs[rows, to] = jnp.where(low, value, zero)
                rhs[pl.ds(tok + step * TILE, TILE), to] = jnp.where(low, zero, value)
            return carry

        lax.fori_loop(0, tok // TILE, spread, 0)

        def unpermute(step, carry):
            start = step * TILE
            value = dot(token_rows(cols_ref, pair, start, TILE), rhs[...])
            for part in range(3):
                piece = value[:, part * PAIR : (part + 1) * PAIR]
                dqkv[part, pl.ds(start, TILE), pair * PAIR : (pair + 1) * PAIR] = piece.astype(BF16)
                gvec_ref[part : part + 1, pair * PAIR : (pair + 1) * PAIR] += jnp.sum(
                    piece, axis=0, keepdims=True
                )
            return carry

        lax.fori_loop(0, tok // TILE, unpermute, 0)

    def tokens(step, carry):
        rows = pl.ds(step * TILE, TILE)
        total = dmid_ref[rows, :].astype(F32)
        for part, w_ref in enumerate((wq_ref, wk_ref, wv_ref)):
            total += dot_nt(dqkv[part, rows, :], w_ref[...])
        gtok_ref[rows, :] = total.astype(BF16)
        return carry

    lax.fori_loop(0, tok // TILE, tokens, 0)

    def weights(step, carry):
        to = pl.ds(pl.multiple_of(step * TILE, TILE), TILE)
        for part, g_ref in enumerate((gq_ref, gk_ref, gv_ref)):
            g_ref[:, to] = dot_tn(x_ref[...], dqkv[part, :, to]).astype(BF16)
        return carry

    lax.fori_loop(0, width // TILE, weights, 0)


def body(
    g,
    tokens,
    cluster_slot,
    loss_mask,
    out_grad,
    query_weight,
    key_weight,
    value_weight,
    output_weight,
    query_bias,
    value_bias,
    output_bias,
    first_gain,
    first_shift,
    up_weight,
    up_bias,
    down_weight,
    down_bias,
    second_gain,
    second_shift,
):
    tok, width = tokens.shape[1:]
    heads = cluster_slot.shape[1]
    pairs = heads // 2
    wide = up_weight.shape[1]
    per_owner = tok // g.seq
    scale = (width // heads) ** -0.5
    both = ("batch", "seq")
    swap = functools.partial(lax.ppermute, axis_name=both, perm=g.swap_pairs())

    slots = cluster_slot[0]
    places = slots // tok * per_owner + slots % tok // g.seq
    table = jnp.concatenate(
        [places, loss_mask, jnp.zeros((16 - heads - 1, tok), jnp.int32)], axis=0
    )
    table = swap(table)
    x = swap(tokens[0])
    grad = swap(out_grad[0])
    cols = table.T

    vectors = (
        query_bias,
        value_bias,
        output_bias,
        first_gain,
        first_shift,
        down_bias,
        second_gain,
        second_shift,
    )
    count = query_bias.shape[0]
    packed = jnp.concatenate([*vectors, up_bias])
    room = -packed.shape[0] % PAIR
    packed = jnp.pad(packed, (0, room)).reshape(-1, PAIR)
    weights = (query_weight, key_weight, value_weight, output_weight, up_weight, down_weight)
    gathered = gather(g, [packed, *weights])
    wq, wk, wv, wo, up, down = (
        item.reshape(g.n * item.shape[4], item.shape[5]) for item in gathered[1:]
    )
    flat = gathered[0].reshape(g.n, -1).astype(F32)
    rows = flat[:, : 8 * count].reshape(g.n, 8, count).transpose(1, 0, 2).reshape(8, width)
    up_row = flat[:, 8 * count : 8 * count + up_bias.shape[0]].reshape(1, wide)
    qkv_bias = jnp.stack([rows[0], jnp.zeros((width,), F32), rows[1]])

    sent, sent_mask = vmem_call(
        project_kernel,
        [
            jax.ShapeDtypeStruct((pairs, tok, 3 * PAIR), BF16),
            jax.ShapeDtypeStruct((tok, PAIR), BF16),
        ],
        [pltpu.VMEM((2 * tok, 4 * PAIR), BF16)],
        "project",
    )(x, wq, wk, wv, qkv_bias, table, cols)
    qkv, mask = exchange(
        g,
        [
            sent.reshape(pairs, g.seq, per_owner, 3 * PAIR),
            sent_mask.reshape(1, g.seq, per_owner, PAIR),
        ],
        2,
    )
    mixed, stats = attend(qkv, mask[0], scale, 1.0 / (heads * CLUSTER * g.batch))
    (returned,) = exchange(g, [mixed], 3)

    shape = jax.ShapeDtypeStruct
    (out, d_mid, d_att, g_out, g_up, g_down, g_rows, g_upb) = vmem_call(
        middle_kernel,
        [
            shape((tok, width), BF16),
            shape((tok, width), BF16),
            shape((pairs, tok, PAIR), BF16),
            shape((width, width), BF16),
            shape((width, wide), BF16),
            shape((wide, width), BF16),
            shape((8, width), F32),
            shape((8, wide), F32),
        ],
        [
            pltpu.VMEM((tok, width), BF16),
            pltpu.VMEM((tok, width), BF16),
            pltpu.VMEM((tok, wide), BF16),
            pltpu.VMEM((tok, wide), BF16),
            pltpu.VMEM((tok, width), BF16),
            pltpu.VMEM((tok, width), BF16),
            pltpu.VMEM((TILE, wide), F32),
            pltpu.VMEM((2 * tok, PAIR), BF16),
        ],
        "middle",
    )(x, returned.reshape(pairs, tok, PAIR), grad, table, cols, wo, up, down, rows[2:], up_row)

    (routed,) = exchange(g, [d_att.reshape(pairs, g.seq, per_owner, PAIR)], 4)
    d_qkv = attend_back(qkv, routed, scale)
    (d_home,) = exchange(g, [d_qkv], 5)

    grad_tokens, g_query, g_key, g_value, g_rows_attn = vmem_call(
        final_kernel,
        [
            shape((tok, width), BF16),
            shape((width, width), BF16),
            shape((width, width), BF16),
            shape((width, width), BF16),
            shape((8, width), F32),
        ],
        [
            pltpu.VMEM((2 * tok, 3 * PAIR), BF16),
            pltpu.VMEM((3, tok, width), BF16),
        ],
        "final",
    )(x, d_home.reshape(pairs, tok, 3 * PAIR), d_mid, cols, wq, wk, wv)

    lines = jnp.stack([g_rows_attn[0], g_rows_attn[2], *(g_rows[i] for i in range(6))])
    lines = lines.reshape(8, g.n, count).transpose(1, 0, 2).reshape(g.n, 8 * count)
    place = group_place(g)
    blocks = stats.shape[1] and tok // CLUSTER
    here = jnp.arange(g.n, dtype=jnp.int32)[:, None] % g.seq == place
    own = jnp.where(here, stats[:2, :blocks].reshape(1, 2 * blocks), 0.0)
    small = jnp.concatenate([lines, g_upb[0].reshape(g.n, wide // g.n), own], axis=1)
    used = small.shape[1]
    small = jnp.pad(small, ((0, 0), (0, -used % (8 * PAIR))))
    split = (g.Y, 2, Z, g.X)

    def parts(item):
        rows, cols = item.shape[0] // g.n, item.shape[1]
        if rows % 8:
            rows, cols = rows * cols // PAIR, PAIR
        return item.reshape(*split, rows, cols)

    sums = scatter(
        g,
        [
            small.reshape(*split, -1, PAIR),
            parts(g_up),
            parts(g_down),
            parts(g_out),
            parts(g_query),
            parts(g_key),
            parts(g_value),
        ],
    )
    vector = sums[0].reshape(-1)
    gq, gv, go, gg1, gs1, gd, gg2, gs2 = (
        vector[i * count : (i + 1) * count] for i in range(8)
    )
    gu = vector[8 * count : 8 * count + wide // g.n]
    cluster_stats = vector[used - 2 * blocks : used].reshape(2, blocks)
    s_up, s_down, s_out, s_query, s_key, s_value = (
        item.reshape(local.shape)
        for item, local in zip(
            sums[1:],
            (up_weight, down_weight, output_weight, query_weight, key_weight, value_weight),
        )
    )
    return (
        swap(out)[None],
        swap(grad_tokens)[None],
        s_query,
        s_key,
        s_value,
        s_out,
        gq,
        gv,
        go,
        gg1,
        gs1,
        s_up,
        gu,
        s_down,
        gd,
        gg2,
        gs2,
        cluster_stats,
    )


def solution(mesh):
    g = Grid(mesh)
    tokens, rows, flat = P("batch", "seq", None), P(("batch", "seq"), None), P(("batch", "seq"))
    return jax.shard_map(
        functools.partial(body, g),
        mesh=mesh,
        in_specs=(
            tokens,
            P("batch", None, "seq"),
            P("batch", "seq"),
            tokens,
            *([rows] * 4),
            *([flat] * 5),
            rows,
            flat,
            rows,
            *([flat] * 3),
        ),
        out_specs=(
            tokens,
            tokens,
            *([rows] * 4),
            *([flat] * 5),
            rows,
            flat,
            rows,
            *([flat] * 3),
            P(None, "seq"),
        ),
        check_vma=False,
    )
```

time: 1670 us -> 680 us (0.41)
  waiting for transfers between devices: 726 us -> 0.01 us
  Pallas kernels: 0 us -> 625 us
  matrix products: 453 us -> 0 us
  local copies, waits for them, and re-layouts: 309 us -> 25.6 us
  blocking collectives: 88.1 us -> 0 us
  other arithmetic: 24.4 us -> 2.52 us
    pallas_call x0 -> x11, Pallas kernels: none -> 625 us  [the longest x4 154 us: exchange(): pl.pallas_call(functools.partial(exchange_kernel, g, n), out_shape=[jax.S...]
    dot_general x198 -> x0, matrix products: 453 us -> none  [the longest x96 209 us: one_head(): jnp.dot(picker, head_part, preferred_element_type=jnp.float32)]
    reduce_scatter x3 -> x0, waiting for transfers between devices: 283 us -> none  [the longest x1 142 us: body(): lax.psum_scatter(grad_down, ('batch', 'seq'), scatter_dimension=0, tiled=...]
    all_to_all x9 -> x0, waiting for transfers between devices: 239 us -> none  [the longest x1 45.6 us: body(): lax.all_to_all(from_clusters(attended_clus, owners), 'seq', split_axis=0,...]
    unnamed x15 -> x0, waiting for transfers between devices: 143 us -> none
    unnamed x2 -> x0, blocking collectives: 81.9 us -> none
    unnamed x105 -> x28, local copies, waits for them, and re-layouts: 86.7 us -> 8.87 us
    all_gather x6 -> x0, waiting for transfers between devices: 60.4 us -> none  [the longest x1 50.6 us: body(): lax.all_gather(attn_local[1], ('batch', 'seq'), axis=0, tiled=True)]
  transfers between devices with their start and end apart: 21 -> 5, of which waited for: 15 -> 0; matrix products, arithmetic and copies ran while one was open for 30% -> 3% of each run, Pallas kernels for 0% -> 59%
where the time goes in v1:
time: 680 us; the launch traced here: 674 us
  Pallas kernels  625 us (92%)
  local copies, waits for them, and re-layouts  25.6 us (4%)
  starting transfers between devices  20.1 us (3%)
    pallas_call x4, Pallas kernels, exchange(): pl.pallas_call(functools.partial(exchange_kernel, g, n), out_shape=[jax.S...  154 us
    pallas_call x3, Pallas kernels, call(): pl.pallas_call(kernel, out_shape=out_shape, in_specs=[pl.BlockSpec(memory...  150 us
    pallas_call x1, Pallas kernels, gather(): pl.pallas_call(functools.partial(gather_kernel, g, shapes), out_shape=[ja...  139 us
    pallas_call x1, Pallas kernels, scatter(): pl.pallas_call(functools.partial(scatter_kernel, g, shapes), out_shape=[j...  136 us
    pallas_call x1, Pallas kernels, attend_back(): pl.pallas_call(functools.partial(attend_back_kernel, scale), grid=(pairs,...  35.3 us
  transfers between devices with their start and end apart: 5, of which 0 were waited for; matrix products, arithmetic and copies ran while one was open for 3% of the time, Pallas kernels for 59%

profile of v1, /device:TPU:0, one launch (start us, length us, event | category | flops | bytes accessed | tf_op | source)
XLA Modules:
  0.0 674.1 jit_solution(5692886961202472959)
XLA Ops:
  0.7 2.1 collective-permute-start
  2.7 13.3 %collective-permute-start.2 = (bf16[1024,768]{1,0:T(8,128)(2,1)}, bf16[1024,768]{1,0:T(8,128)(2,1)}, u32[]{:S(2)}, u32[]{:S(2)}) collective-permute-start(bf16[1024,768]{1,0:T(8,128)(2,1)} %bitcast.93), channel_id=1, source_target_pairs={{0,0},{1,1},{2,2},{3,3},{4,8},{5,9},{6,10},{7,11},{8,4},{9,5},{10,... | collective-permute-start | bytes 4718600 | tf_op jit(solution)/shard_map/ppermute | solution.py:917
  16.0 0.1 pad.18.clone
  16.1 0.9 fusion.2
  17.0 0.8 add_add_fusion
  17.7 0.2 copy.49
  17.9 0.7 collective-permute-start.1
  18.6 6.1 concatenate.9
  24.7 0.6 pad_bitcast_fusion.refs_0_
  25.3 138.5 %weight_gather.1 = (bf16[2,2,4,2,3,128]{5,4,3,2,1,0:T(4,128)(2,1)}, bf16[2,2,4,2,24,768]{5,4,3,2,1,0:T(8,128)(2,1)}, bf16[2,2,4,2,24,768]{5,4,3,2,1,0:T(8,128)(2...) custom-call(bf16[3,128]{1,0:T(4,128)(2,1)} %pad_bitcast_fusion.refs_, ...), custom_call_target="tpu_custom_call" | custom-call | tf_op jit(solution)/shard_map/weight_gather/pallas_call | solution.py:176
  163.8 0.8 copy.73
  164.6 0.1 reshape.141
  164.7 0.1 slice_reduce_fusion.1
  164.8 0.1 slice.80
  164.9 0.1 slice.82
  165.0 0.1 pad.20.clone
  165.1 0.7 pad_maximum_fusion.1.bias_ref
  165.7 0.1 slice.106
  165.8 0.7 slice.84.vec_ref
  166.6 0.7 reshape.148.up_bias_ref
  167.2 0.0 collective-permute-done.1
  167.2 0.8 copy.50.places_ref
  168.1 0.0 collective-permute-done.x_ref
  168.1 1.1 copy-done
  169.2 33.8 %project.1 = (bf16[6,1024,384]{2,1,0:T(8,128)(2,1)}, bf16[1024,128]{1,0:T(8,128)(2,1)}) custom-call(bf16[1024,768]{1,0:T(8,128)(2,1)} %copy-done, bf16[768,768]{1,0:T(8,128)(2,1)} %bitcast.63, bf16[768,768]{1,0:T(8,128)(2,1)} %bitcast.65, bf16[768,768]{1,0:T(8,128)(2,1)} %bitcast.67, f32[3,768]{1,0:T(4,128)} %pad_maximum_fusion.1.bias_ref, ...), custom_call_target="tpu_custom_call" | custom-call | tf_op jit(solution)/shard_map/project/pallas_call | solution.py:519
  203.0 57.9 %exchange.4 = (bf16[6,8,128,384]{3,2,1,0:T(8,128)(2,1)}, bf16[1,8,128,128]{3,2,1,0:T(8,128)(2,1)}) custom-call(bf16[6,8,128,384]{3,2,1,0:T(8,128)(2,1)} %bitcast.69, bf16[1,8,128,128]{3,2,1,0:T(8,128)(2,1)} %bitcast.85), custom_call_target="tpu_custom_call" | custom-call | tf_op jit(solution)/shard_map/exchange/pallas_call | solution.py:397
  260.9 10.9 %attend.1 = (bf16[6,8,128,128]{3,2,1,0:T(8,128)(2,1)}, f32[8,128]{1,0:T(8,128)}) custom-call(bf16[6,8,128,384]{3,2,1,0:T(8,128)(2,1)} %get-tuple-element.57.qkv_ref, bf16[8,128,128]{2,1,0:T(8,128)(2,1)} %bitcast.84), custom_call_target="tpu_custom_call" | custom-call | tf_op jit(solution)/shard_map/attend/pallas_call | solution.py:579
  271.8 20.4 %exchange.5 = bf16[6,8,128,128]{3,2,1,0:T(8,128)(2,1)} custom-call(bf16[6,8,128,128]{3,2,1,0:T(8,128)(2,1)} %get-tuple-element.59.refs_0_), custom_call_target="tpu_custom_call" | custom-call | tf_op jit(solution)/shard_map/exchange/pallas_call | solution.py:397
  292.2 0.0 collective-permute-done.2.grad_ref
  292.2 80.8 %middle.1 = (bf16[1024,768]{1,0:T(8,128)(2,1)}, bf16[1024,768]{1,0:T(8,128)(2,1)}, bf16[6,1024,128]{2,1,0:T(8,128)(2,1)}, bf16[768,768]{1,0:T(8,128)(2,1)}, bf16...) custom-call(bf16[1024,768]{1,0:T(8,128)(2,1)} %copy-done, ...), custom_call_target="tpu_custom_call" | custom-call | tf_op jit(solution)/shard_map/middle/pallas_call | solution.py:519
  373.0 21.1 %exchange.6.grad_ref = bf16[6,8,128,128]{3,2,1,0:T(8,128)(2,1)} custom-call(bf16[6,8,128,128]{3,2,1,0:T(8,128)(2,1)} %bitcast.74), custom_call_target="tpu_custom_call" | custom-call | tf_op jit(solution)/shard_map/exchange/pallas_call | solution.py:397
  394.1 35.3 %attend_back.1.refs_0_ = bf16[6,8,128,384]{3,2,1,0:T(8,128)(2,1)} custom-call(bf16[6,8,128,384]{3,2,1,0:T(8,128)(2,1)} %get-tuple-element.57.qkv_ref, bf16[6,8,128,128]{3,2,1,0:T(8,128)(2,1)} %exchange.6.grad_ref), custom_call_target="tpu_custom_call" | custom-call | tf_op jit(solution)/shard_map/attend_back/pallas_call | solution.py:632
  429.4 54.2 %exchange.7 = bf16[6,8,128,384]{3,2,1,0:T(8,128)(2,1)} custom-call(bf16[6,8,128,384]{3,2,1,0:T(8,128)(2,1)} %attend_back.1.refs_0_), custom_call_target="tpu_custom_call" | custom-call | tf_op jit(solution)/shard_map/exchange/pallas_call | solution.py:397
  483.6 0.0 copy-start.8
  483.6 35.9 %final.1 = (bf16[1024,768]{1,0:T(8,128)(2,1)}, bf16[768,768]{1,0:T(8,128)(2,1)}, bf16[768,768]{1,0:T(8,128)(2,1)}, bf16[768,768]{1,0:T(8,128)(2,1)}, f32[8,768]{1,0:T(8,128)}) custom-call(bf16[1024,768]{1,0:T(8,128)(2,1)} %copy-done, bf16[6,1024,384]{2,1,0:T(8,128)(2,1)} %bitcast.56, bf16[1024,768]{1,0:T(8,128)(2,1)} %get-tuple-element.65.dmid_ref, ...), custom_call_target="tpu_custom_call" | custom-call | tf_op jit(solution)/shard_map/final/pallas_call | solution.py:519
  519.5 2.1 collective-permute-start.4
  521.5 2.1 collective-permute-start.3
  523.6 0.8 fusion.9
  524.4 0.0 copy-done.8
  524.4 0.1 reshape.151
  524.5 0.1 copy.53
  524.6 0.1 reshape.152
  524.7 0.9 slice_reduce_fusion.2
  525.7 0.1 reshape_squeeze.3
  525.7 0.7 slice.90
  526.4 0.1 broadcast_in_dim.36
  526.5 0.1 broadcast_select_fusion
  526.6 0.1 fusion
  526.7 0.7 copy.56
  527.3 136.1 %grad_scatter.1 = (f32[8,128]{1,0:T(8,128)}, f32[24,3072]{1,0:T(8,128)}, f32[96,768]{1,0:T(8,128)}, f32[24,768]{1,0:T(8,128)}, f32[24,768]{1,0:T(8,128)}, /*index=5*/f32[24,768]{1,0:T(8,128)}, f32[24,768]{1,0:T(8,128)}) custom-call(f32[2,2,4,2,8,128]{5,4,3,2,1,0:T(8,128)} %bitcast.82, bf16[2,2,4,2,24,3072]{5,4,3,2,1,0:T(8,128)(2,1)} %bitcast.61, ...), custom_call_target="tpu_custom_call" | custom-call | tf_op jit(solution)/shard_map/grad_scatter/pallas_call | solution.py:352
  663.5 0.8 slice.100
  664.2 0.6 slice.107
  664.8 1.3 slice.96
  666.1 1.6 fusion.10
  667.6 0.0 collective-permute-done.4
  667.6 0.0 collective-permute-done.3
  667.6 1.1 copy.82
  668.8 1.1 copy.83
  670.0 0.6 copy.84
  670.6 0.6 copy.85
  671.2 0.6 copy.86
  671.9 0.6 copy.87
  672.5 0.7 copy.88
  673.2 0.7 copy.89
  (21 shorter events, 0.1 us)
Async XLA Ops:
  0.7 167.4 %collective-permute-start = (bf16[1024,768]{1,0:T(8,128)(2,1)}, bf16[1024,768]{1,0:T(8,128)(2,1)S(1)}, u32[]{:S(2)}, u32[]{:S(2)}) collective-permute-start(bf16[1024,768]{1,0:T(8,128)(2,1)} %bitcast.92), channel_id=1, source_target_pairs={{0,0},{1,1},{2,2},{3,3},{4,8},{5,9},{6,10},{7,11},{8,4},{9,5},{10,... | collective-permute-start | bytes 4718600 | tf_op jit(solution)/shard_map/ppermute | solution.py:916
  2.7 289.5 %collective-permute-start.2 = (bf16[1024,768]{1,0:T(8,128)(2,1)}, bf16[1024,768]{1,0:T(8,128)(2,1)}, u32[]{:S(2)}, u32[]{:S(2)}) collective-permute-start(bf16[1024,768]{1,0:T(8,128)(2,1)} %bitcast.93), channel_id=1, source_target_pairs={{0,0},{1,1},{2,2},{3,3},{4,8},{5,9},{6,10},{7,11},{8,4},{9,5},{10,... | collective-permute-start | bytes 4718600 | tf_op jit(solution)/shard_map/ppermute | solution.py:917
  17.9 149.3 %collective-permute-start.1 = (s32[16,1024]{0,1:T(8,128)S(1)}, s32[16,1024]{0,1:T(8,128)S(1)}, u32[]{:S(2)}, u32[]{:S(2)}) collective-permute-start(s32[16,1024]{0,1:T(8,128)S(1)} %copy.49), channel_id=1, source_target_pairs={{0,0},{1,1},{2,2},{3,3},{4,8},{5,9},{6,10},{7,11},{8,4},{9,5},{10,... | collective-permute-start | bytes 196616 | tf_op jit(solution)/shard_map/ppermute | solution.py:915
  167.2 0.9 copy-start.1
  168.1 1.1 copy-start
  483.6 40.8 %copy-start.8 = (f32[8,768]{1,0:T(8,128)S(1)}, f32[8,768]{1,0:T(8,128)}, u32[]{:S(2)}) copy-start(f32[8,768]{1,0:T(8,128)} %get-tuple-element.68) | copy-start | bytes 73732
  519.5 148.2 %collective-permute-start.4 = (bf16[1024,768]{1,0:T(8,128)(2,1)}, bf16[1024,768]{1,0:T(8,128)(2,1)S(1)}, u32[]{:S(2)}, u32[]{:S(2)}) collective-permute-start(bf16[1024,768]{1,0:T(8,128)(2,1)} %get-tuple-element.66), channel_id=1, source_target_pairs={{0,0},{1,1},{2,2},{3,3},{4,8},{5,9},{6,10},{7,11},{8,4},{9,5},{10,... | collective-permute-start | bytes 4718600 | tf_op jit(solution)/shard_map/ppermute | solution.py:1054
  521.5 146.1 %collective-permute-start.3 = (bf16[1024,768]{1,0:T(8,128)(2,1)}, bf16[1024,768]{1,0:T(8,128)(2,1)S(1)}, u32[]{:S(2)}, u32[]{:S(2)}) collective-permute-start(bf16[1024,768]{1,0:T(8,128)(2,1)} %get-tuple-element.63), channel_id=1, source_target_pairs={{0,0},{1,1},{2,2},{3,3},{4,8},{5,9},{6,10},{7,11},{8,4},{9,5},{10,... | collective-permute-start | bytes 4718600 | tf_op jit(solution)/shard_map/ppermute | solution.py:1053
  668.8 1.2 copy-start.7
  668.8 1.8 copy-start.6
  668.8 2.4 copy-start.5
  668.8 3.1 copy-start.4
  668.8 3.7 copy-start.3
  668.8 4.4 copy-start.2

commit v2 on v1

--- a/solution.py
+++ b/solution.py
@@ -90,106 +90,177 @@
     return [(k * (cols // count), cols // count) for k in range(count)]
 
 
-def gather_kernel(g, shapes, *refs):
-    n = len(shapes)
-    ins, outs = refs[:n], refs[n : 2 * n]
-    sends, recvs, local_sem = refs[2 * n :]
-    y, c, z, x = coords(g)
-    greet(line_peers(g))
-
-    units = []
-    for index, shape in enumerate(shapes):
-        for start, size in lane_pieces(shape):
-            units.append((index, pl.ds(start, size)))
-    stages = []
-    slot = 0
-    for number, (index, cols) in enumerate(units):
-        src, out = ins[index], outs[index]
-
-        def put(peer, part, slot, src=None, out=out, cols=cols):
-            view = out.at[(*part, slice(None), cols)]
-            return remote(
-                view if src is None else src, view, sends.at[slot], recvs.at[slot], peer
+class Gather:
+    def __init__(self, g, ins, outs, sends, recvs, local_sem, mixed):
+        self.g, self.ins, self.outs = g, ins, outs
+        self.sends, self.recvs, self.local_sem = sends, recvs, local_sem
+        self.at = coords(g)
+        self.mixed = mixed
+        self.units = [
+            (index, pl.ds(start, size))
+            for index, item in enumerate(ins)
+            for start, size in lane_pieces(item.shape)
+        ]
+
+    @staticmethod
+    def slots(g, shapes):
+        units = sum(len(lane_pieces(shape)) for shape in shapes)
+        return units, units * (Z + g.X + g.Y - 2)
+
+    def own(self, unit):
+        index, cols = self.units[unit]
+        y, c, z, x = self.at
+        return pltpu.make_async_copy(
+            self.ins[index].at[:, cols],
+            self.outs[index].at[y, c, z, x, :, cols],
+            self.local_sem.at[unit],
+        )
+
+    def moves(self, unit, level):
+        g = self.g
+        index, cols = self.units[unit]
+        out = self.outs[index]
+        y, c, z, x = self.at
+        a = slice(None)
+        base = unit * (Z + g.X + g.Y - 2)
+        x_first = not self.mixed or unit % 2 == 0
+        axis = ("z", "x" if x_first else "y", "y" if x_first else "x", "c")[level]
+        base += (0, Z - 1, Z - 1 + (g.X if x_first else g.Y) - 1, Z + g.X + g.Y - 3)[level]
+        if level == 0:
+            part = (y, c, z, x)
+        elif level == 1:
+            part = (y, c, a, x)
+        elif level == 2:
+            part = (y, c, a, a) if x_first else (a, c, a, x)
+        else:
+            part = (a, c, a, a)
+        view = out.at[(*part, a, cols)]
+        src = self.ins[index].at[:, cols] if level == 0 else view
+        size = {"z": Z, "x": g.X, "y": g.Y, "c": 2}[axis]
+        made = []
+        for k in range(1, size):
+            peer = {
+                "z": (y, c, (z + k) % Z, x),
+                "x": (y, c, z, (x + k) % g.X),
+                "y": ((y + k) % g.Y, c, z, x),
+                "c": (y, 1 - c, z, x),
+            }[axis]
+            slot = base + k - 1
+            made.append(
+                remote(src, view, self.sends.at[slot], self.recvs.at[slot], device(g, *peer))
             )
-
-        own = pltpu.make_async_copy(
-            src.at[:, cols], out.at[y, c, z, x, :, cols], local_sem.at[number]
-        )
-        a, w = slice(None), []
-        w.append(
-            [
-                put(device(g, y, c, (z + k) % Z, x), (y, c, z, x), slot + k - 1, src.at[:, cols])
-                for k in range(1, Z)
-            ]
-        )
-        slot += Z - 1
-        if number % 2 == 0:
-            plan = [("x", (y, c, a, x)), ("y", (y, c, a, a))]
+        return made
+
+    def start(self, unit, level):
+        if level == 0:
+            self.own(unit).start()
         else:
-            plan = [("y", (y, c, a, x)), ("x", (a, c, a, x))]
-        for axis, part in plan:
-            if axis == "x":
-                moves = [
-                    put(device(g, y, c, z, (x + k) % g.X), part, slot + k - 1)
-                    for k in range(1, g.X)
-                ]
-            else:
-                moves = [
-                    put(device(g, (y + k) % g.Y, c, z, x), part, slot + k - 1)
-                    for k in range(1, g.Y)
-                ]
-            slot += len(moves)
-            w.append(moves)
-        w.append([put(device(g, y, 1 - c, z, x), (a, c, a, a), slot)])
-        slot += 1
-        stages.append((own, w))
-
-    count = len(units)
-    lead = 2
-    for t in range(count + lead + 3):
-        if t < count:
-            own, w = stages[t]
-            own.start()
-            for copy in w[0]:
-                copy.start()
+            if level == 1:
+                self.own(unit).wait()
+            for copy in self.moves(unit, level - 1):
+                copy.wait_recv()
+        for copy in self.moves(unit, level):
+            copy.start()
+
+    def finish(self):
+        for unit in range(len(self.units)):
+            for copy in self.moves(unit, 3):
+                copy.wait_recv()
+        for unit in range(len(self.units)):
+            for level in range(4):
+                for copy in self.moves(unit, level):
+                    copy.wait_send()
+
+
+class Swap:
+    def __init__(self, g, src, dst, send, recv):
+        b, s = lax.axis_index("batch"), lax.axis_index("seq")
+        self.native = b % 2 == s // g.half
+        self.peer = swap_partner(g)
+        self.ends = (src, dst, send, recv)
+
+    def start(self):
+        src, dst, send, recv = self.ends
+
+        @pl.when(self.native)
+        def _():
+            pltpu.make_async_copy(src, dst, recv).start()
+
+        @pl.when(jnp.logical_not(self.native))
+        def _():
+            remote(src, dst, send, recv, self.peer).start()
+
+    def wait(self):
+        src, dst, send, recv = self.ends
+
+        @pl.when(self.native)
+        def _():
+            pltpu.make_async_copy(src, dst, recv).wait()
+
+        @pl.when(jnp.logical_not(self.native))
+        def _():
+            remote(src, dst, send, recv, self.peer).wait()
+
+
+def swap_partner(g):
+    b, s = lax.axis_index("batch"), lax.axis_index("seq")
+    return (b // 2 * 2 + 1 - b % 2, (s + g.half) % g.seq)
+
+
+def open_kernel(g, *refs):
+    n = 5
+    ins, outs = refs[:n], refs[n + 2 : 2 * n + 2]
+    x_ref, table_ref = refs[n : n + 2]
+    x_out, table_out = refs[2 * n + 2 : 2 * n + 4]
+    sends, recvs, local_sem, swap_send, swap_recv = refs[2 * n + 4 :]
+    greet(line_peers(g) + [swap_partner(g)])
+    plan = Gather(g, ins, outs, sends, recvs, local_sem, True)
+    count = len(plan.units)
+    for unit in range(count):
+        plan.start(unit, 0)
+    swaps = [
+        Swap(g, x_ref, x_out, swap_send.at[0], swap_recv.at[0]),
+        Swap(g, table_ref, table_out, swap_send.at[1], swap_recv.at[1]),
+    ]
+    for swap in swaps:
+        swap.start()
+    lag = 2
+    for t in range(count + 2 * lag):
         for level in range(1, 4):
-            u = t - lead - level + 1
-            if 0 <= u < count:
-                own, w = stages[u]
-                if level == 1:
-                    own.wait()
-                for copy in w[level - 1]:
-                    copy.wait_recv()
-                for copy in w[level]:
-                    copy.start()
-    for own, w in stages:
-        w[3][0].wait_recv()
-        for moves in w:
-            for copy in moves:
-                copy.wait_send()
-
-
-def gather(g, arrays):
-    shapes = [item.shape for item in arrays]
-    units = sum(len(lane_pieces(shape)) for shape in shapes)
-    slots = units * (Z + g.X + g.Y - 2)
-    return pl.pallas_call(
-        functools.partial(gather_kernel, g, shapes),
+            unit = t - (level - 1) * lag
+            if 0 <= unit < count:
+                plan.start(unit, level)
+    plan.finish()
+    for swap in swaps:
+        swap.wait()
+
+
+def open_call(g, arrays, x, table):
+    units, slots = Gather.slots(g, [item.shape for item in arrays])
+    any_space = pl.BlockSpec(memory_space=pl.ANY)
+    shape = jax.ShapeDtypeStruct
+    made = pl.pallas_call(
+        functools.partial(open_kernel, g),
         out_shape=[
-            jax.ShapeDtypeStruct((g.Y, 2, Z, g.X, *item.shape), item.dtype) for item in arrays
+            *(shape((g.Y, 2, Z, g.X, *item.shape), item.dtype) for item in arrays),
+            shape(x.shape, x.dtype),
+            shape(table.shape, table.dtype),
         ],
-        in_specs=[pl.BlockSpec(memory_space=pl.ANY)] * len(arrays),
-        out_specs=[pl.BlockSpec(memory_space=pl.ANY)] * len(arrays),
+        in_specs=[any_space] * (len(arrays) + 2),
+        out_specs=[any_space] * (len(arrays) + 2),
         scratch_shapes=[
             pltpu.SemaphoreType.DMA((slots,)),
             pltpu.SemaphoreType.DMA((slots,)),
             pltpu.SemaphoreType.DMA((units,)),
+            pltpu.SemaphoreType.DMA((2,)),
+            pltpu.SemaphoreType.DMA((2,)),
         ],
         compiler_params=pltpu.CompilerParams(
             collective_id=0, has_side_effects=True, vmem_limit_bytes=VMEM_LIMIT
         ),
-        name="weight_gather",
-    )(*arrays)
+        name="open",
+    )(*arrays, x, table)
+    return made[:-2], made[-2], made[-1]
 
 
 def scatter_kernel(g, shapes, *refs):
@@ -473,82 +544,50 @@
 ROWS = 256
 
 
-def project_kernel(x_ref, wq_ref, wk_ref, wv_ref, bias_ref, places_ref, cols_ref, out_ref, mask_ref, rhs):
+def project_pair(pair, x_ref, w_refs, bias_ref, places_ref, cols_ref, out_ref, mask_ref, rhs):
     tok = x_ref.shape[0]
-    pairs = out_ref.shape[0]
-    heads = 2 * pairs
+    heads = bias_ref.shape[1] // (PAIR // 2)
     lanes = lax.broadcasted_iota(jnp.int32, (ROWS, PAIR), 1)
-    for pair in range(pairs):
-        head = slice(pair * PAIR, (pair + 1) * PAIR)
-
-        def project(step, carry):
-            rows = pl.ds(step * ROWS, ROWS)
-            x = x_ref[rows, :]
-            for part, w_ref in enumerate((wq_ref, wk_ref, wv_ref)):
-                value = dot(x, w_ref[:, head]) + bias_ref[part : part + 1, head]
-                value = value.astype(BF16)
-                low = head_lanes(value.shape)
-                zero = jnp.zeros_like(value)
-                to = slice(part * PAIR, (part + 1) * PAIR)
-                rhs[rows, to] = jnp.where(low, value, zero)
-                rhs[pl.ds(tok + step * ROWS, ROWS), to] = jnp.where(low, zero, value)
-            mask = cols_ref[rows, heads : heads + 1].astype(F32)
-            for i in range(2):
-                rhs[pl.ds(i * tok + step * ROWS, ROWS), 3 * PAIR :] = jnp.where(
-                    lanes == 2 * pair + i, mask, 0.0
-                ).astype(BF16)
-            return carry
-
-        lax.fori_loop(0, tok // ROWS, project, 0)
-
-        def permute(step, carry):
-            rows = pl.ds(step * ROWS, ROWS)
-            picked = dot(place_rows(places_ref, pair, step * ROWS, ROWS), rhs[...])
-            out_ref[pair, rows, :] = picked[:, : 3 * PAIR].astype(BF16)
-            if pair == 0:
-                mask_ref[rows, :] = picked[:, 3 * PAIR :].astype(BF16)
-            else:
-                mask_ref[rows, :] = mask_ref[rows, :] + picked[:, 3 * PAIR :].astype(BF16)
-            return carry
-
-        lax.fori_loop(0, tok // ROWS, permute, 0)
-
-
-def vmem_call(kernel, out_shape, scratch, name):
-    def call(*args):
-        return pl.pallas_call(
-            kernel,
-            out_shape=out_shape,
-            in_specs=[pl.BlockSpec(memory_space=pltpu.VMEM)] * len(args),
-            out_specs=jax.tree.map(lambda _: pl.BlockSpec(memory_space=pltpu.VMEM), out_shape),
-            scratch_shapes=scratch,
-            compiler_params=pltpu.CompilerParams(vmem_limit_bytes=VMEM_LIMIT),
-            name=name,
-        )(*args)
-
-    return call
-
-
-def cluster_scores(q, k, scale):
-    return dot_nt(q, k) * scale
-
-
-def attend_kernel(scale, factor, qkv_ref, mask_ref, out_ref, stats_ref):
-    pair = pl.program_id(0)
+    head = pl.ds(pl.multiple_of(pair * PAIR, PAIR), PAIR)
+
+    def project(step, carry):
+        rows = pl.ds(step * ROWS, ROWS)
+        x = x_ref[rows, :]
+        for part, w_ref in enumerate(w_refs):
+            value = dot(x, w_ref[:, head]) + bias_ref[part : part + 1, head]
+            value = value.astype(BF16)
+            low = head_lanes(value.shape)
+            zero = jnp.zeros_like(value)
+            to = slice(part * PAIR, (part + 1) * PAIR)
+            rhs[rows, to] = jnp.where(low, value, zero)
+            rhs[pl.ds(tok + step * ROWS, ROWS), to] = jnp.where(low, zero, value)
+        mask = cols_ref[rows, heads : heads + 1].astype(F32)
+        for i in range(2):
+            rhs[pl.ds(i * tok + step * ROWS, ROWS), 3 * PAIR :] = jnp.where(
+                lanes == 2 * pair + i, mask, 0.0
+            ).astype(BF16)
+        return carry
+
+    lax.fori_loop(0, tok // ROWS, project, 0)
+
+    def permute(step, carry):
+        rows = pl.ds(step * ROWS, ROWS)
+        picked = dot(place_rows(places_ref, pair, step * ROWS, ROWS), rhs[...])
+        out_ref[pair, rows, :] = picked[:, : 3 * PAIR].astype(BF16)
+        mask_ref[rows, :] = mask_ref[rows, :] + picked[:, 3 * PAIR :].astype(BF16)
+        return carry
+
+    lax.fori_loop(0, tok // ROWS, permute, 0)
+
+
+def attend_pair(pair, scale, qkv_ref, out_ref, entropy_ref):
     _, sources, per_owner, _ = qkv_ref.shape
     size = CLUSTER // sources
     clusters = per_owner // size
     lanes = lax.broadcasted_iota(jnp.int32, (CLUSTER, PAIR), 1)
-    spot = lax.broadcasted_iota(jnp.int32, stats_ref.shape, 1)
-    row = lax.broadcasted_iota(jnp.int32, stats_ref.shape, 0)
-
-    @pl.when(pair == 0)
-    def _():
-        stats_ref[...] = jnp.zeros_like(stats_ref)
-
     for cluster in range(clusters):
         q, k, v = (
-            gather_rows(qkv_ref, (0,), cluster * size, size, slice(i * PAIR, (i + 1) * PAIR))
+            gather_rows(qkv_ref, (pair,), cluster * size, size, slice(i * PAIR, (i + 1) * PAIR))
             for i in range(3)
         )
         scores = cluster_scores(split_pair(q), k, scale)
@@ -561,39 +600,260 @@
         mixed = dot(
             jnp.concatenate([low[:CLUSTER], low[CLUSTER:]], axis=1), split_pair(v)
         )
-        out_ref[0, :, cluster * size : (cluster + 1) * size, :] = spread_rows(mixed, sources, BF16)
-        mask = gather_rows(mask_ref, (), cluster * size, size, slice(None)).astype(F32)
-        own = jnp.where(lanes == 2 * pair, entropy[:CLUSTER], 0.0) + jnp.where(
-            lanes == 2 * pair + 1, entropy[CLUSTER:], 0.0
+        out_ref[pair, :, cluster * size : (cluster + 1) * size, :] = spread_rows(
+            mixed, sources, BF16
         )
-        in_pair = (lanes == 2 * pair) | (lanes == 2 * pair + 1)
-        entropy_sum = jnp.sum(own * mask) * factor
-        count = jnp.sum(jnp.where(in_pair, mask, 0.0)) * factor
-        stats_ref[...] += jnp.where(
+        entropy_ref[cluster] = jnp.where(
+            lanes == 2 * pair,
+            entropy[:CLUSTER],
+            jnp.where(lanes == 2 * pair + 1, entropy[CLUSTER:], entropy_ref[cluster]),
+        )
+
+
+class Exchange:
+    def __init__(self, g, src, dst, sends, recvs, local_sem):
+        self.g, self.src, self.dst = g, src, dst
+        self.sends, self.recvs, self.local_sem = sends, recvs, local_sem
+        self.me = group_place(g)
+
+    def block(self, pair, peer):
+        if len(self.src.shape) == 4:
+            return self.src.at[pair, peer]
+        per = self.src.shape[1] // self.g.seq
+        return self.src.at[pair, pl.ds(pl.multiple_of(peer * per, per), per), :]
+
+    def own(self, pair):
+        return pltpu.make_async_copy(
+            self.block(pair, self.me), self.dst.at[pair, self.me], self.local_sem.at[pair]
+        )
+
+    def moves(self, pair):
+        g = self.g
+        made = []
+        for k in range(1, g.seq):
+            peer = (self.me + k) % g.seq
+            made.append(
+                remote(
+                    self.block(pair, peer),
+                    self.dst.at[pair, self.me],
+                    self.sends.at[pair, k - 1],
+                    self.recvs.at[pair, k - 1],
+                    group_device(g, peer),
+                )
+            )
+        return made
+
+    def start(self, pair):
+        for copy in self.moves(pair):
+            copy.start()
+        self.own(pair).start()
+
+    def arrive(self, pair):
+        self.own(pair).wait()
+        for copy in self.moves(pair):
+            copy.wait_recv()
+
+    def sent(self, pair):
+        for copy in self.moves(pair):
+            copy.wait_send()
+
+
+def exchange_sems(g, pairs):
+    return [
+        pltpu.SemaphoreType.DMA((pairs, g.seq - 1)),
+        pltpu.SemaphoreType.DMA((pairs, g.seq - 1)),
+        pltpu.SemaphoreType.DMA((pairs,)),
+    ]
+
+
+LAG = 2
+
+
+def forward_kernel(
+    g,
+    scale,
+    factor,
+    x_ref,
+    wq_ref,
+    wk_ref,
+    wv_ref,
+    bias_ref,
+    places_ref,
+    cols_ref,
+    up_ref,
+    down_ref,
+    grad_ref,
+    up_all,
+    down_all,
+    grad_out,
+    qkv_out,
+    ret_out,
+    stats_ref,
+    rhs,
+    sent,
+    routed,
+    mixed,
+    mask_sent,
+    mask_routed,
+    entropy,
+    *sems,
+):
+    pairs = sent.shape[0]
+    group = [group_device(g, (group_place(g) + k) % g.seq) for k in range(1, g.seq)]
+    greet(line_peers(g) + group + [swap_partner(g)])
+    plan = Gather(g, [up_ref, down_ref], [up_all, down_all], *sems[:3], False)
+    swap = Swap(g, grad_ref, grad_out, *(sem.at[0] for sem in sems[3:5]))
+    there = Exchange(g, sent, routed, *sems[5:8])
+    back = Exchange(g, mixed, ret_out, *sems[8:11])
+    masks = Exchange(g, mask_sent, mask_routed, *sems[11:14])
+    save_sem = sems[14]
+    units = len(plan.units)
+
+    def keep(pair):
+        return pltpu.make_async_copy(routed.at[pair], qkv_out.at[pair], save_sem.at[pair])
+
+    mask_sent[...] = jnp.zeros_like(mask_sent)
+    entropy[...] = jnp.zeros_like(entropy)
+
+    def step(t, carry):
+        for when in range(pairs + LAG):
+            todo = [
+                (unit, level)
+                for level in (3, 2, 1, 0)
+                for unit in range(units)
+                if unit // 2 + level == when
+            ]
+            if todo or when == 1:
+
+                @pl.when(t == when)
+                def _(todo=todo, when=when):
+                    for unit, level in todo:
+                        plan.start(unit, level)
+                    if when == 1:
+                        swap.start()
+
+        @pl.when(t < pairs)
+        def _():
+            project_pair(
+                t,
+                x_ref,
+                (wq_ref, wk_ref, wv_ref),
+                bias_ref,
+                places_ref,
+                cols_ref,
+                sent,
+                mask_sent.at[0],
+                rhs,
+            )
+            there.start(t)
+
+        @pl.when(t == pairs - 1)
+        def _():
+            masks.start(0)
+
+        @pl.when(t >= LAG)
+        def _():
+            pair = t - LAG
+            there.arrive(pair)
+            keep(pair).start()
+            attend_pair(pair, scale, routed, mixed, entropy)
+            back.start(pair)
+
+        return carry
+
+    lax.fori_loop(0, pairs + LAG, step, 0)
+
+    masks.arrive(0)
+    sources, per_owner = mask_routed.shape[1:3]
+    size = CLUSTER // sources
+    spot = lax.broadcasted_iota(jnp.int32, stats_ref.shape, 1)
+    row = lax.broadcasted_iota(jnp.int32, stats_ref.shape, 0)
+    stats = jnp.zeros(stats_ref.shape, F32)
+    for cluster in range(per_owner // size):
+        mask = gather_rows(mask_routed, (0,), cluster * size, size, slice(None)).astype(F32)
+        entropy_sum = jnp.sum(entropy[cluster] * mask) * factor
+        count = jnp.sum(mask) * factor
+        stats += jnp.where(
             spot == cluster, jnp.where(row == 0, entropy_sum, jnp.where(row == 1, count, 0.0)), 0.0
         )
-
-
-def attend(qkv, mask, scale, factor):
-    pairs, sources, per_owner, width = qkv.shape
+    stats_ref[...] = stats
+    plan.finish()
+    swap.wait()
+
+    def close(pair, carry):
+        keep(pair).wait()
+        back.arrive(pair)
+        there.sent(pair)
+        back.sent(pair)
+        return carry
+
+    lax.fori_loop(0, pairs, close, 0)
+    masks.sent(0)
+
+
+def forward(g, scale, factor, x, wq, wk, wv, bias, places, cols, up, down, grad):
+    tok, width = x.shape
+    pairs = width // PAIR
+    per_owner = tok // g.seq
+    clusters = tok // CLUSTER
+    units, slots = Gather.slots(g, [up.shape, down.shape])
+    shape = jax.ShapeDtypeStruct
+    any_space, vmem = pl.BlockSpec(memory_space=pl.ANY), pl.BlockSpec(memory_space=pltpu.VMEM)
+    dma = pltpu.SemaphoreType.DMA
     return pl.pallas_call(
-        functools.partial(attend_kernel, scale, factor),
-        grid=(pairs,),
+        functools.partial(forward_kernel, g, scale, factor),
         out_shape=[
-            jax.ShapeDtypeStruct((pairs, sources, per_owner, PAIR), BF16),
-            jax.ShapeDtypeStruct((8, PAIR), F32),
+            shape((g.Y, 2, Z, g.X, *up.shape), BF16),
+            shape((g.Y, 2, Z, g.X, *down.shape), BF16),
+            shape(grad.shape, BF16),
+            shape((pairs, g.seq, per_owner, 3 * PAIR), BF16),
+            shape((pairs, g.seq, per_owner, PAIR), BF16),
+            shape((8, PAIR), F32),
         ],
-        in_specs=[
-            pl.BlockSpec((1, sources, per_owner, width), lambda i: (i, 0, 0, 0)),
-            pl.BlockSpec((sources, per_owner, PAIR), lambda i: (0, 0, 0)),
+        in_specs=[vmem] * 7 + [any_space] * 3,
+        out_specs=[any_space] * 5 + [vmem],
+        scratch_shapes=[
+            pltpu.VMEM((2 * tok, 4 * PAIR), BF16),
+            pltpu.VMEM((pairs, tok, 3 * PAIR), BF16),
+            pltpu.VMEM((pairs, g.seq, per_owner, 3 * PAIR), BF16),
+            pltpu.VMEM((pairs, g.seq, per_owner, PAIR), BF16),
+            pltpu.VMEM((1, tok, PAIR), BF16),
+            pltpu.VMEM((1, g.seq, per_owner, PAIR), BF16),
+            pltpu.VMEM((clusters, CLUSTER, PAIR), F32),
+            dma((slots,)),
+            dma((slots,)),
+            dma((units,)),
+            dma((1,)),
+            dma((1,)),
+            *exchange_sems(g, pairs),
+            *exchange_sems(g, pairs),
+            *exchange_sems(g, 1),
+            dma((pairs,)),
         ],
-        out_specs=[
-            pl.BlockSpec((1, sources, per_owner, PAIR), lambda i: (i, 0, 0, 0)),
-            pl.BlockSpec((8, PAIR), lambda i: (0, 0)),
-        ],
-        compiler_params=pltpu.CompilerParams(vmem_limit_bytes=VMEM_LIMIT),
-        name="attend",
-    )(qkv, mask)
+        compiler_params=pltpu.CompilerParams(
+            collective_id=2, has_side_effects=True, vmem_limit_bytes=VMEM_LIMIT
+        ),
+        name="forward",
+    )(x, wq, wk, wv, bias, places, cols, up, down, grad)
+
+
+def vmem_call(kernel, out_shape, scratch, name):
+    def call(*args):
+        return pl.pallas_call(
+            kernel,
+            out_shape=out_shape,
+            in_specs=[pl.BlockSpec(memory_space=pltpu.VMEM)] * len(args),
+            out_specs=jax.tree.map(lambda _: pl.BlockSpec(memory_space=pltpu.VMEM), out_shape),
+            scratch_shapes=scratch,
+            compiler_params=pltpu.CompilerParams(vmem_limit_bytes=VMEM_LIMIT),
+            name=name,
+        )(*args)
+
+    return call
+
+
+def cluster_scores(q, k, scale):
+    return dot_nt(q, k) * scale
 
 
 def attend_back_kernel(scale, qkv_ref, grad_ref, out_ref):
@@ -912,11 +1172,6 @@
     table = jnp.concatenate(
         [places, loss_mask, jnp.zeros((16 - heads - 1, tok), jnp.int32)], axis=0
     )
-    table = swap(table)
-    x = swap(tokens[0])
-    grad = swap(out_grad[0])
-    cols = table.T
-
     vectors = (
         query_bias,
         value_bias,
@@ -931,35 +1186,31 @@
     packed = jnp.concatenate([*vectors, up_bias])
     room = -packed.shape[0] % PAIR
     packed = jnp.pad(packed, (0, room)).reshape(-1, PAIR)
-    weights = (query_weight, key_weight, value_weight, output_weight, up_weight, down_weight)
-    gathered = gather(g, [packed, *weights])
-    wq, wk, wv, wo, up, down = (
-        item.reshape(g.n * item.shape[4], item.shape[5]) for item in gathered[1:]
-    )
+    weights = (query_weight, key_weight, value_weight, output_weight)
+    gathered, x, table = open_call(g, [packed, *weights], tokens[0], table)
+    cols = table.T
+    wq, wk, wv, wo = (item.reshape(g.n * item.shape[4], item.shape[5]) for item in gathered[1:])
     flat = gathered[0].reshape(g.n, -1).astype(F32)
     rows = flat[:, : 8 * count].reshape(g.n, 8, count).transpose(1, 0, 2).reshape(8, width)
     up_row = flat[:, 8 * count : 8 * count + up_bias.shape[0]].reshape(1, wide)
     qkv_bias = jnp.stack([rows[0], jnp.zeros((width,), F32), rows[1]])
 
-    sent, sent_mask = vmem_call(
-        project_kernel,
-        [
-            jax.ShapeDtypeStruct((pairs, tok, 3 * PAIR), BF16),
-            jax.ShapeDtypeStruct((tok, PAIR), BF16),
-        ],
-        [pltpu.VMEM((2 * tok, 4 * PAIR), BF16)],
-        "project",
-    )(x, wq, wk, wv, qkv_bias, table, cols)
-    qkv, mask = exchange(
+    up, down, grad, qkv, returned, stats = forward(
         g,
-        [
-            sent.reshape(pairs, g.seq, per_owner, 3 * PAIR),
-            sent_mask.reshape(1, g.seq, per_owner, PAIR),
-        ],
-        2,
+        scale,
+        1.0 / (heads * CLUSTER * g.batch),
+        x,
+        wq,
+        wk,
+        wv,
+        qkv_bias,
+        table,
+        cols,
+        up_weight,
+        down_weight,
+        out_grad[0],
     )
-    mixed, stats = attend(qkv, mask[0], scale, 1.0 / (heads * CLUSTER * g.batch))
-    (returned,) = exchange(g, [mixed], 3)
+    up, down = (item.reshape(g.n * item.shape[4], item.shape[5]) for item in (up, down))
 
     shape = jax.ShapeDtypeStruct
     (out, d_mid, d_att, g_out, g_up, g_down, g_rows, g_upb) = vmem_call(

time: 680 us -> 574 us (0.84)
  Pallas kernels: 625 us -> 540 us
  starting transfers between devices: 20.1 us -> 4.11 us
    pallas_call x4 -> x2, Pallas kernels: 154 us -> 75.5 us  [exchange(): pl.pallas_call(functools.partial(exchange_kernel, g, n), out_shape=[jax.S...]
    pallas_call x2, Pallas kernels: 149 us -> 187 us  [the longest x1 126 us: forward(): pl.pallas_call(functools.partial(forward_kernel, g, scale, factor), out_s...]
    pallas_call x3 -> x2, Pallas kernels: 150 us -> 117 us  [call(): pl.pallas_call(kernel, out_shape=out_shape, in_specs=[pl.BlockSpec(memory...]
    ppermute x3 -> x0, starting transfers between devices: 16 us -> none  [the longest x1 13.3 us: body(): grad = swap(out_grad[0])]
    pallas_call x1, Pallas kernels: 35.3 us -> 26.2 us  [attend_back(): pl.pallas_call(functools.partial(attend_back_kernel, scale), grid=(pairs,...]
  transfers between devices with their start and end apart: 5 -> 2, of which waited for: 0 -> 0; matrix products, arithmetic and copies ran while one was open for 3% -> 1% of each run, Pallas kernels for 59% -> 24%
where the time goes in v2:
time: 574 us
  Pallas kernels  540 us (94%)
  local copies, waits for them, and re-layouts  25.3 us (4%)
    pallas_call x1, Pallas kernels, scatter(): pl.pallas_call(functools.partial(scatter_kernel, g, shapes), out_shape=[j...  135 us
    pallas_call x1, Pallas kernels, forward(): pl.pallas_call(functools.partial(forward_kernel, g, scale, factor), out_s...  126 us
    pallas_call x2, Pallas kernels, call(): pl.pallas_call(kernel, out_shape=out_shape, in_specs=[pl.BlockSpec(memory...  117 us
    pallas_call x2, Pallas kernels, exchange(): pl.pallas_call(functools.partial(exchange_kernel, g, n), out_shape=[jax.S...  75.5 us
    pallas_call x1, Pallas kernels, open_call(): pl.pallas_call(functools.partial(open_kernel, g), out_shape=[*(shape((g.Y...  60.9 us
    pallas_call x1, Pallas kernels, attend_back(): pl.pallas_call(functools.partial(attend_back_kernel, scale), grid=(pairs,...  26.2 us
  transfers between devices with their start and end apart: 2, of which 0 were waited for; matrix products, arithmetic and copies ran while one was open for 1% of the time, Pallas kernels for 24%

profile of v2, /device:TPU:0, one launch (start us, length us, event | category | flops | bytes accessed | tf_op | source)
XLA Modules:
  0.0 573.7 jit_solution(8880402747016849095)
XLA Ops:
  0.7 0.9 fusion.2
  1.6 0.1 pad.21.clone
  1.6 6.1 %concatenate.9 = bf16[288]{0:T(512)(128)(2,1)S(1)} concatenate(bf16[24]{0:T(256)(128)(2,1)} %param.27, bf16[24]{0:T(256)(128)(2,1)} %param.28, bf16[24]{0:T(256)(128)(2,1)} %param.29, bf16[24]{0:T(256)(128)(2,1)} %param.30, bf16[24]{0:T(256)(128)(2,1)} %param.31, bf16[24]{0:T(256)(128)(2,1)} %param.35, bf16[24]{0:T(256)(128)(2,1)} %param.36, bf16[24]{0:T(256)(128)(2,1)} %param.37, ...), dimensions={0} | concatenate | bytes 1152 | tf_op jit(solution)/shard_map/concatenate | solution.py:1186
  7.7 0.6 pad_bitcast_fusion.refs_0_
  8.3 1.4 add_add_fusion.refs_6_
  9.7 60.9 %open.1 = (bf16[2,2,4,2,3,128]{5,4,3,2,1,0:T(4,128)(2,1)}, bf16[2,2,4,2,24,768]{5,4,3,2,1,0:T(8,128)(2,1)}, bf16[2,2,4,2,24,768]{5,4,3,2,1,0:T(8,128)(2,1)}, bf1...) custom-call(bf16[3,128]{1,0:T(4,128)(2,1)} %pad_bitcast_fusion.refs_, ...), custom_call_target="tpu_custom_call" | custom-call | tf_op jit(solution)/shard_map/open/pallas_call | solution.py:242
  70.6 0.8 copy.62
  71.4 0.1 reshape.135
  71.5 0.1 slice_reduce_fusion.1
  71.6 0.1 slice.106
  71.7 0.1 slice.80
  71.8 0.1 slice.82
  71.8 1.9 copy.40
  73.7 0.7 slice.84.vec_ref
  74.4 0.7 reshape.140.up_bias_ref
  75.1 0.1 pad.17.clone
  75.2 0.7 pad_maximum_fusion.1.bias_ref
  75.9 126.2 %forward.1 = (bf16[2,2,4,2,24,3072]{5,4,3,2,1,0:T(8,128)(2,1)}, bf16[2,2,4,2,96,768]{5,4,3,2,1,0:T(8,128)(2,1)}, bf16[1024,768]{1,0:T(8,128)(2,1)}, bf16[6,8,128...) custom-call(bf16[1024,768]{1,0:T(8,128)(2,1)} %get-tuple-element.51.x_ref, ...), custom_call_target="tpu_custom_call" | custom-call | tf_op jit(solution)/shard_map/forward/pallas_call | solution.py:803
  202.1 80.7 %middle.1 = (bf16[1024,768]{1,0:T(8,128)(2,1)}, bf16[1024,768]{1,0:T(8,128)(2,1)}, bf16[6,1024,128]{2,1,0:T(8,128)(2,1)}, bf16[768,768]{1,0:T(8,128)(2,1)}, bf16...) custom-call(bf16[1024,768]{1,0:T(8,128)(2,1)} %get-tuple-element.51.x_ref, ...), custom_call_target="tpu_custom_call" | custom-call | tf_op jit(solution)/shard_map/middle/pallas_call | solution.py:842
  282.8 20.5 %exchange.2.grad_ref = bf16[6,8,128,128]{3,2,1,0:T(8,128)(2,1)} custom-call(bf16[6,8,128,128]{3,2,1,0:T(8,128)(2,1)} %bitcast.71), custom_call_target="tpu_custom_call" | custom-call | tf_op jit(solution)/shard_map/exchange/pallas_call | solution.py:468
  303.3 26.2 %attend_back.1.refs_0_ = bf16[6,8,128,384]{3,2,1,0:T(8,128)(2,1)} custom-call(bf16[6,8,128,384]{3,2,1,0:T(8,128)(2,1)} %get-tuple-element.63.qkv_ref, bf16[6,8,128,128]{3,2,1,0:T(8,128)(2,1)} %exchange.2.grad_ref), custom_call_target="tpu_custom_call" | custom-call | tf_op jit(solution)/shard_map/attend_back/pallas_call | solution.py:892
  329.4 55.0 %exchange.3 = bf16[6,8,128,384]{3,2,1,0:T(8,128)(2,1)} custom-call(bf16[6,8,128,384]{3,2,1,0:T(8,128)(2,1)} %attend_back.1.refs_0_), custom_call_target="tpu_custom_call" | custom-call | tf_op jit(solution)/shard_map/exchange/pallas_call | solution.py:468
  384.4 0.0 copy-start.6
  384.4 35.8 %final.1 = (bf16[1024,768]{1,0:T(8,128)(2,1)}, bf16[768,768]{1,0:T(8,128)(2,1)}, bf16[768,768]{1,0:T(8,128)(2,1)}, bf16[768,768]{1,0:T(8,128)(2,1)}, f32[8,768]{1,0:T(8,128)}) custom-call(bf16[1024,768]{1,0:T(8,128)(2,1)} %get-tuple-element.51.x_ref, bf16[6,1024,384]{2,1,0:T(8,128)(2,1)} %bitcast.53, bf16[1024,768]{1,0:T(8,128)(2,1)} %get-tuple-element.65.dmid_ref, ...), custom_call_target="tpu_custom_call" | custom-call | tf_op jit(solution)/shard_map/final/pallas_call | solution.py:842
  420.2 2.1 collective-permute-start.1
  422.3 2.1 collective-permute-start
  424.3 0.8 fusion.9
  425.2 0.0 copy-done.6
  425.2 0.1 reshape.143
  425.3 0.1 copy.42
  425.4 0.1 reshape.144
  425.5 0.9 slice_reduce_fusion.2
  426.4 0.1 reshape_squeeze.3
  426.5 0.7 slice.90
  427.2 0.1 broadcast_in_dim.36
  427.3 0.1 broadcast_select_fusion
  427.3 0.1 fusion
  427.4 0.7 copy.45
  428.1 135.1 %grad_scatter.1 = (f32[8,128]{1,0:T(8,128)}, f32[24,3072]{1,0:T(8,128)}, f32[96,768]{1,0:T(8,128)}, f32[24,768]{1,0:T(8,128)}, f32[24,768]{1,0:T(8,128)}, /*index=5*/f32[24,768]{1,0:T(8,128)}, f32[24,768]{1,0:T(8,128)}) custom-call(f32[2,2,4,2,8,128]{5,4,3,2,1,0:T(8,128)} %bitcast.80, bf16[2,2,4,2,24,3072]{5,4,3,2,1,0:T(8,128)(2,1)} %bitcast.57, ...), custom_call_target="tpu_custom_call" | custom-call | tf_op jit(solution)/shard_map/grad_scatter/pallas_call | solution.py:423
  563.2 0.8 slice.100
  564.0 0.6 slice.107
  564.5 1.3 slice.96
  565.8 1.6 fusion.10
  567.4 0.0 collective-permute-done.1
  567.4 0.0 collective-permute-done
  567.4 1.1 copy.71
  568.5 0.0 copy-start.5
  568.5 0.0 copy-start.4
  568.5 0.0 copy-start.3
  568.5 0.0 copy-start.1
  568.5 0.0 copy-start
  568.6 1.1 copy.72
  569.7 0.0 copy-done.5
  569.7 0.6 copy.73
  570.3 0.0 copy-done.4
  570.3 0.6 copy.74
  571.0 0.0 copy-done.3
  571.0 0.6 copy.75
  571.6 0.0 copy-done.2
  571.6 0.6 copy.76
  572.2 0.0 copy-done.1
  572.2 0.7 copy.77
  573.0 0.0 copy-done
  573.0 0.7 copy.78
  (7 shorter events, 0.1 us)
Async XLA Ops:
  384.4 40.8 %copy-start.6 = (f32[8,768]{1,0:T(8,128)S(1)}, f32[8,768]{1,0:T(8,128)}, u32[]{:S(2)}) copy-start(f32[8,768]{1,0:T(8,128)} %get-tuple-element.68) | copy-start | bytes 73732
  420.2 147.1 %collective-permute-start.1 = (bf16[1024,768]{1,0:T(8,128)(2,1)}, bf16[1024,768]{1,0:T(8,128)(2,1)S(1)}, u32[]{:S(2)}, u32[]{:S(2)}) collective-permute-start(bf16[1024,768]{1,0:T(8,128)(2,1)} %get-tuple-element.66), channel_id=1, source_target_pairs={{0,0},{1,1},{2,2},{3,3},{4,8},{5,9},{6,10},{7,11},{8,4},{9,5},{10,... | collective-permute-start | bytes 4718600 | tf_op jit(solution)/shard_map/ppermute | solution.py:1305
  422.3 145.1 %collective-permute-start = (bf16[1024,768]{1,0:T(8,128)(2,1)}, bf16[1024,768]{1,0:T(8,128)(2,1)S(1)}, u32[]{:S(2)}, u32[]{:S(2)}) collective-permute-start(bf16[1024,768]{1,0:T(8,128)(2,1)} %get-tuple-element.62), channel_id=1, source_target_pairs={{0,0},{1,1},{2,2},{3,3},{4,8},{5,9},{6,10},{7,11},{8,4},{9,5},{10,... | collective-permute-start | bytes 4718600 | tf_op jit(solution)/shard_map/ppermute | solution.py:1304
  568.5 1.2 copy-start.5
  568.5 1.8 copy-start.4
  568.5 2.4 copy-start.3
  568.5 3.1 copy-start.2
  568.5 3.7 copy-start.1
  568.5 4.4 copy-start

commit v3 on v2

--- a/solution.py
+++ b/solution.py
@@ -23,17 +23,6 @@
         self.Y, self.X = self.batch // 2, self.seq // Z
         self.half = self.seq // 2
         self.n = self.batch * self.seq
-
-    def swap_pairs(self):
-        pairs = []
-        for b in range(self.batch):
-            for s in range(self.seq):
-                if b % 2 == s // self.half:
-                    to = (b, s)
-                else:
-                    to = (b ^ 1, (s + self.half) % self.seq)
-                pairs.append((b * self.seq + s, to[0] * self.seq + to[1]))
-        return pairs
 
 
 def coords(g):
@@ -263,223 +252,188 @@
     return made[:-2], made[-2], made[-1]
 
 
-def scatter_kernel(g, shapes, *refs):
-    n = len(shapes)
-    ins, outs = refs[:n], refs[n : 2 * n]
-    by_core, by_one, by_two, by_z = (refs[(2 + k) * n : (3 + k) * n] for k in range(4))
-    sends, recvs = refs[6 * n :]
-    y, c, z, x = coords(g)
-    greet(line_peers(g))
-
-    units = []
-    for index, shape in enumerate(shapes):
-        for start, size in lane_pieces(shape):
-            units.append((index, slice(start, start + size)))
-
-    per = Z + g.X + g.Y - 2
-
-    def copies(number, level):
-        index, cols = units[number]
-        base = number * per
-        every = slice(None)
-        first_y = index % 2 == 0
+class Scatter:
+    def __init__(self, g, ins, outs, bufs, sends, recvs, mixed):
+        self.g, self.ins, self.outs, self.bufs = g, ins, outs, bufs
+        self.sends, self.recvs, self.mixed = sends, recvs, mixed
+        self.at = coords(g)
+        self.units = [
+            (index, pl.ds(start, size))
+            for index, item in enumerate(ins)
+            for start, size in lane_pieces(item.shape[4:])
+        ]
+
+    @staticmethod
+    def scratch(g, shapes, mixed):
+        made = []
+        for index, (y, _, z, x, rows, cols) in enumerate(shapes):
+            made.append(pltpu.VMEM((y, z, x, rows, cols), BF16))
+            if Scatter.y_first(index, mixed):
+                made.append(pltpu.VMEM((max(y - 1, 1), z, x, rows, cols), BF16))
+                made.append(pltpu.VMEM((max(x - 1, 1), z, rows, cols), BF16))
+            else:
+                made.append(pltpu.VMEM((max(x - 1, 1), y, z, rows, cols), BF16))
+                made.append(pltpu.VMEM((max(y - 1, 1), z, rows, cols), BF16))
+            made.append(pltpu.VMEM((z - 1, rows, cols), BF16))
+        units = sum(len(lane_pieces(shape[4:])) for shape in shapes)
+        slots = units * (Z + g.X + g.Y - 2)
+        return [*made, pltpu.SemaphoreType.DMA((slots,)), pltpu.SemaphoreType.DMA((slots,))]
+
+    @staticmethod
+    def y_first(index, mixed):
+        return not mixed or index % 2 == 0
+
+    def moves(self, unit, level):
+        g = self.g
+        index, cols = self.units[unit]
+        y, c, z, x = self.at
+        a = slice(None)
+        core, one, two, three = self.bufs[4 * index : 4 * index + 4]
+        y_first = self.y_first(index, self.mixed)
+        axis = ("c", "y" if y_first else "x", "x" if y_first else "y", "z")[level]
+        base = unit * (Z + g.X + g.Y - 2)
+        base += (0, 1, (g.Y if y_first else g.X), g.X + g.Y - 1)[level]
         if level == 0:
             return [
                 remote(
-                    ins[index].at[:, 1 - c, :, :, :, cols],
-                    by_core[index].at[:, :, :, :, cols],
-                    sends.at[base],
-                    recvs.at[base],
+                    self.ins[index].at[a, 1 - c, a, a, a, cols],
+                    core.at[a, a, a, a, cols],
+                    self.sends.at[base],
+                    self.recvs.at[base],
                     device(g, y, 1 - c, z, x),
                 )
             ]
-        base += 1
-        along = {1: "y" if first_y else "x", 2: "x" if first_y else "y", 3: "z"}[level]
-        if level == 2:
-            base += (g.Y if first_y else g.X) - 1
+        held = (one, two, three)[level - 1]
+        size = {"y": g.Y, "x": g.X, "z": Z}[axis]
+        made = []
+        for k in range(1, size):
+            to_y, to_x, to_z = (y + k) % g.Y, (x + k) % g.X, (z + k) % Z
+            peer, src = {
+                ("y", 1): ((to_y, c, z, x), (to_y, a, a)),
+                ("x", 1): ((y, c, z, to_x), (a, a, to_x)),
+                ("x", 2): ((y, c, z, to_x), (y, a, to_x)),
+                ("y", 2): ((to_y, c, z, x), (to_y, a, x)),
+                ("z", 3): ((y, c, to_z, x), (y, to_z, x)),
+            }[axis, level]
+            rest = (a,) * (len(held.shape) - 2)
+            slot = base + k - 1
+            made.append(
+                remote(
+                    core.at[(*src, a, cols)],
+                    held.at[(k - 1, *rest, cols)],
+                    self.sends.at[slot],
+                    self.recvs.at[slot],
+                    device(g, *peer),
+                )
+            )
+        return made
+
+    def add(self, unit, level):
+        g = self.g
+        index, cols = self.units[unit]
+        y, c, z, x = self.at
+        core, one, two, three = self.bufs[4 * index : 4 * index + 4]
+        y_first = self.y_first(index, self.mixed)
+        a = slice(None)
+
+        def fold(where, *others):
+            total = core[(*where, a, cols)].astype(F32)
+            for ref, spot in others:
+                total += ref[(*spot, a, cols)].astype(F32)
+            core[(*where, a, cols)] = total.astype(BF16)
+
         if level == 3:
-            base += g.Y + g.X - 2
-        size = {"y": g.Y, "x": g.X, "z": Z}[along]
-        moves = []
-        for k in range(1, size):
-            if along == "y":
-                to = (y + k) % g.Y
-                peer = device(g, to, c, z, x)
-            elif along == "x":
-                to = (x + k) % g.X
-                peer = device(g, y, c, z, to)
-            else:
-                to = (z + k) % Z
-                peer = device(g, y, c, to, x)
-            if level == 1 and first_y:
-                src = by_core[index].at[to, :, :, :, cols]
-            elif level == 1:
-                src = by_core[index].at[:, :, to, :, cols]
-            elif level == 2 and first_y:
-                src = by_one[index].at[0, :, to, :, cols]
-            elif level == 2:
-                src = by_one[index].at[0, to, :, :, cols]
-            else:
-                src = by_two[index].at[0, to, :, cols]
-            held = (by_one, by_two, by_z)[level - 1][index]
-            slot = 0 if level < 3 else 0
-            dst = held.at[(k, *([every] * (len(held.shape) - 2)), cols)]
-            moves.append(remote(src, dst, sends.at[base + k - 1], recvs.at[base + k - 1], peer))
-        return moves
-
-    def add(number, level):
-        index, cols = units[number]
-        first_y = index % 2 == 0
-        kind = ins[index].dtype
-        if level == 0:
-
-            def one(step, carry):
+            total = core[y, z, x, :, cols].astype(F32)
+            for k in range(Z - 1):
+                total += three[k, :, cols].astype(F32)
+            self.outs[index][:, cols] = total
+            return
+
+        def one_z(zz, carry):
+            if level == 0:
                 for yy in range(g.Y):
                     for xx in range(g.X):
-                        total = ins[index][yy, c, step, xx, :, cols].astype(F32)
-                        total += by_core[index][yy, step, xx, :, cols].astype(F32)
-                        by_core[index][yy, step, xx, :, cols] = total.astype(kind)
-                return carry
-
-            lax.fori_loop(0, Z, one, 0)
-        elif level == 1:
-            size, rest = (g.Y, g.X) if first_y else (g.X, g.Y)
-
-            def one(step, carry):
-                for r in range(rest):
-                    if first_y:
-                        total = by_core[index][y, step, r, :, cols].astype(F32)
-                    else:
-                        total = by_core[index][r, step, x, :, cols].astype(F32)
-                    for k in range(1, size):
-                        if first_y:
-                            total += by_one[index][k, step, r, :, cols].astype(F32)
-                        else:
-                            total += by_one[index][k, r, step, :, cols].astype(F32)
-                    if first_y:
-                        by_one[index][0, step, r, :, cols] = total.astype(kind)
-                    else:
-                        by_one[index][0, r, step, :, cols] = total.astype(kind)
-                return carry
-
-            lax.fori_loop(0, Z, one, 0)
-        elif level == 2:
-            size = g.X if first_y else g.Y
-
-            def one(step, carry):
-                if first_y:
-                    total = by_one[index][0, step, x, :, cols].astype(F32)
-                else:
-                    total = by_one[index][0, y, step, :, cols].astype(F32)
-                for k in range(1, size):
-                    total += by_two[index][k, step, :, cols].astype(F32)
-                by_two[index][0, step, :, cols] = total.astype(kind)
-                return carry
-
-            lax.fori_loop(0, Z, one, 0)
-        else:
-            total = by_two[index][0, z, :, cols].astype(F32)
-            for k in range(1, Z):
-                total += by_z[index][k, :, cols].astype(F32)
-            outs[index][:, cols] = total
-
-    count = len(units)
-    started = [[None] * 4 for _ in units]
-    for t in range(count + 4):
-        if t < count:
-            started[t][0] = copies(t, 0)
-            for copy in started[t][0]:
+                        fold((yy, zz, xx), (self.ins[index], (yy, c, zz, xx)))
+            elif level == 1 and y_first:
+                for xx in range(g.X):
+                    fold((y, zz, xx), *((one, (k, zz, xx)) for k in range(g.Y - 1)))
+            elif level == 1:
+                for yy in range(g.Y):
+                    fold((yy, zz, x), *((one, (k, yy, zz)) for k in range(g.X - 1)))
+            else:
+                size = g.X if y_first else g.Y
+                fold((y, zz, x), *((two, (k, zz)) for k in range(size - 1)))
+            return carry
+
+        lax.fori_loop(0, Z, one_z, 0)
+
+    def step(self, unit, level):
+        if level:
+            for copy in self.moves(unit, level - 1):
+                copy.wait_recv()
+            self.add(unit, level - 1)
+        if level < 4:
+            for copy in self.moves(unit, level):
                 copy.start()
+
+    def sent(self):
+        for unit in range(len(self.units)):
+            for level in range(4):
+                for copy in self.moves(unit, level):
+                    copy.wait_send()
+
+
+class Total:
+    def __init__(self, g, held, bufs, sends, recvs):
+        self.g, self.held, self.bufs = g, held, bufs
+        self.sends, self.recvs = sends, recvs
+        self.at = coords(g)
+
+    @staticmethod
+    def scratch(g, shape):
+        sizes = (2, g.Y, g.X, Z)
+        slots = sum(sizes)
+        return [
+            *(pltpu.VMEM((size, *shape), F32) for size in sizes),
+            pltpu.SemaphoreType.DMA((slots,)),
+            pltpu.SemaphoreType.DMA((slots,)),
+        ]
+
+    def moves(self, level):
+        g = self.g
+        y, c, z, x = self.at
+        sizes = (2, g.Y, g.X, Z)
+        mine = (c, y, x, z)[level]
+        made = []
+        for k in range(1, sizes[level]):
+            to = (mine + k) % sizes[level]
+            peer = ((y, to, z, x), (to, c, z, x), (y, c, z, to), (y, c, to, x))[level]
+            slot = sum(sizes[:level]) + k
+            view = self.bufs[level].at[mine]
+            made.append(
+                remote(view, view, self.sends.at[slot], self.recvs.at[slot], device(g, *peer))
+            )
+        return made
+
+    def start(self, level, value):
+        y, c, z, x = self.at
+        self.bufs[level][(c, y, x, z)[level]] = value
+        for copy in self.moves(level):
+            copy.start()
+
+    def take(self, level):
+        for copy in self.moves(level):
+            copy.wait_recv()
+        buf = self.bufs[level]
+        total = buf[0]
+        for k in range(1, buf.shape[0]):
+            total = total + buf[k]
+        return total
+
+    def sent(self):
         for level in range(4):
-            u = t - level - 1
-            if 0 <= u < count:
-                for copy in started[u][level]:
-                    copy.wait_recv()
-                add(u, level)
-                if level < 3:
-                    started[u][level + 1] = copies(u, level + 1)
-                    for copy in started[u][level + 1]:
-                        copy.start()
-    for levels in started:
-        for moves in levels:
-            for copy in moves:
+            for copy in self.moves(level):
                 copy.wait_send()
-
-
-def scatter(g, arrays):
-    shapes = [item.shape[4:] for item in arrays]
-    units = sum(len(lane_pieces(shape)) for shape in shapes)
-    slots = units * (Z + g.X + g.Y - 2)
-    scratch = [[], [], [], []]
-    for index, (item, shape) in enumerate(zip(arrays, shapes)):
-        scratch[0].append(pltpu.VMEM((g.Y, Z, g.X, *shape), item.dtype))
-        if index % 2 == 0:
-            scratch[1].append(pltpu.VMEM((g.Y, Z, g.X, *shape), item.dtype))
-            scratch[2].append(pltpu.VMEM((g.X, Z, *shape), item.dtype))
-        else:
-            scratch[1].append(pltpu.VMEM((g.X, g.Y, Z, *shape), item.dtype))
-            scratch[2].append(pltpu.VMEM((g.Y, Z, *shape), item.dtype))
-        scratch[3].append(pltpu.VMEM((Z, *shape), item.dtype))
-    return pl.pallas_call(
-        functools.partial(scatter_kernel, g, shapes),
-        out_shape=[jax.ShapeDtypeStruct(shape, F32) for shape in shapes],
-        in_specs=[pl.BlockSpec(memory_space=pltpu.VMEM)] * len(arrays),
-        out_specs=[pl.BlockSpec(memory_space=pltpu.VMEM)] * len(arrays),
-        scratch_shapes=[item for level in scratch for item in level]
-        + [pltpu.SemaphoreType.DMA((slots,)), pltpu.SemaphoreType.DMA((slots,))],
-        compiler_params=pltpu.CompilerParams(
-            collective_id=1, has_side_effects=True, vmem_limit_bytes=VMEM_LIMIT
-        ),
-        name="grad_scatter",
-    )(*arrays)
-
-
-def exchange_kernel(g, n, *refs):
-    ins, outs = refs[:n], refs[n : 2 * n]
-    sends, recvs, local_sem = refs[2 * n :]
-    me = group_place(g)
-    size = g.seq
-    peers = [(me + k) % size for k in range(1, size)]
-    greet([group_device(g, peer) for peer in peers])
-    copies = []
-    for index in range(n):
-        own = pltpu.make_async_copy(
-            ins[index].at[:, me], outs[index].at[:, me], local_sem.at[index]
-        )
-        own.start()
-        for k, peer in enumerate(peers):
-            slot = index * (size - 1) + k
-            copy = remote(
-                ins[index].at[:, peer],
-                outs[index].at[:, me],
-                sends.at[slot],
-                recvs.at[slot],
-                group_device(g, peer),
-            )
-            copy.start()
-            copies.append(copy)
-        copies.append(own)
-    for copy in copies:
-        copy.wait()
-
-
-def exchange(g, arrays, number):
-    n = len(arrays)
-    return pl.pallas_call(
-        functools.partial(exchange_kernel, g, n),
-        out_shape=[jax.ShapeDtypeStruct(item.shape, item.dtype) for item in arrays],
-        in_specs=[pl.BlockSpec(memory_space=pl.ANY)] * n,
-        out_specs=[pl.BlockSpec(memory_space=pl.ANY)] * n,
-        scratch_shapes=[
-            pltpu.SemaphoreType.DMA((n * (g.seq - 1),)),
-            pltpu.SemaphoreType.DMA((n * (g.seq - 1),)),
-            pltpu.SemaphoreType.DMA((n,)),
-        ],
-        compiler_params=pltpu.CompilerParams(
-            collective_id=number, has_side_effects=True, vmem_limit_bytes=VMEM_LIMIT
-        ),
-        name="exchange",
-    )(*arrays)
 
 
 def dot(left, right):
@@ -516,14 +470,14 @@
 
 
 def token_rows(cols_ref, pair, start, size):
-    tok = cols_ref.shape[0]
+    tok, width = cols_ref.shape
     lanes = lax.broadcasted_iota(jnp.int32, (size, tok), 1)
-    parts = [
-        (lanes == cols_ref[pl.ds(start, size), 2 * pair + i : 2 * pair + i + 1])
-        .astype(F32)
-        .astype(BF16)
-        for i in range(2)
-    ]
+    heads = lax.broadcasted_iota(jnp.int32, (size, width), 1)
+    table = cols_ref[pl.ds(start, size), :].astype(F32)
+    parts = []
+    for i in range(2):
+        place = jnp.sum(jnp.where(heads == 2 * pair + i, table, 0.0), axis=1, keepdims=True)
+        parts.append((lanes == place.astype(jnp.int32)).astype(F32).astype(BF16))
     return jnp.concatenate(parts, axis=1)
 
 
@@ -774,7 +728,8 @@
         entropy_sum = jnp.sum(entropy[cluster] * mask) * factor
         count = jnp.sum(mask) * factor
         stats += jnp.where(
-            spot == cluster, jnp.where(row == 0, entropy_sum, jnp.where(row == 1, count, 0.0)), 0.0
+            spot == group_place(g) * (per_owner // size) + cluster,
+            jnp.where(row == 0, entropy_sum, jnp.where(row == 1, count, 0.0)), 0.0
         )
     stats_ref[...] = stats
     plan.finish()
@@ -837,35 +792,20 @@
     )(x, wq, wk, wv, bias, places, cols, up, down, grad)
 
 
-def vmem_call(kernel, out_shape, scratch, name):
-    def call(*args):
-        return pl.pallas_call(
-            kernel,
-            out_shape=out_shape,
-            in_specs=[pl.BlockSpec(memory_space=pltpu.VMEM)] * len(args),
-            out_specs=jax.tree.map(lambda _: pl.BlockSpec(memory_space=pltpu.VMEM), out_shape),
-            scratch_shapes=scratch,
-            compiler_params=pltpu.CompilerParams(vmem_limit_bytes=VMEM_LIMIT),
-            name=name,
-        )(*args)
-
-    return call
-
-
 def cluster_scores(q, k, scale):
     return dot_nt(q, k) * scale
 
 
-def attend_back_kernel(scale, qkv_ref, grad_ref, out_ref):
+def attend_back_pair(slot, pair, scale, qkv_ref, grad_ref, out_ref):
     _, sources, per_owner, _ = qkv_ref.shape
     size = CLUSTER // sources
     clusters = per_owner // size
     for cluster in range(clusters):
         q, k, v = (
-            gather_rows(qkv_ref, (0,), cluster * size, size, slice(i * PAIR, (i + 1) * PAIR))
+            gather_rows(qkv_ref, (slot,), cluster * size, size, slice(i * PAIR, (i + 1) * PAIR))
             for i in range(3)
         )
-        grad = gather_rows(grad_ref, (0,), cluster * size, size, slice(None))
+        grad = gather_rows(grad_ref, (slot,), cluster * size, size, slice(None))
         q2, g2 = split_pair(q), split_pair(grad)
         scores = cluster_scores(q2, k, scale)
         top = jnp.max(scores, axis=1, keepdims=True)
@@ -883,24 +823,8 @@
         d_key = dot_tn(d_score, q2) * scale
         for i, value in enumerate((d_query, d_key, d_value)):
             out_ref[
-                0, :, cluster * size : (cluster + 1) * size, i * PAIR : (i + 1) * PAIR
+                pair, :, cluster * size : (cluster + 1) * size, i * PAIR : (i + 1) * PAIR
             ] = spread_rows(value, sources, BF16)
-
-
-def attend_back(qkv, grad, scale):
-    pairs, sources, per_owner, width = qkv.shape
-    return pl.pallas_call(
-        functools.partial(attend_back_kernel, scale),
-        grid=(pairs,),
-        out_shape=jax.ShapeDtypeStruct((pairs, sources, per_owner, width), BF16),
-        in_specs=[
-            pl.BlockSpec((1, sources, per_owner, width), lambda i: (i, 0, 0, 0)),
-            pl.BlockSpec((1, sources, per_owner, PAIR), lambda i: (i, 0, 0, 0)),
-        ],
-        out_specs=pl.BlockSpec((1, sources, per_owner, width), lambda i: (i, 0, 0, 0)),
-        compiler_params=pltpu.CompilerParams(vmem_limit_bytes=VMEM_LIMIT),
-        name="attend_back",
-    )(qkv, grad)
 
 
 INV_SQRT2 = 0.7071067811865476
@@ -927,6 +851,7 @@
 
 
 def middle_kernel(
+    g,
     x_ref,
     att_ref,
     grad_ref,
@@ -953,7 +878,13 @@
     datt_all,
     slope,
     ret,
+    datt_sent,
+    ex_send,
+    ex_recv,
+    ex_local,
 ):
+    greet([group_device(g, (group_place(g) + k) % g.seq) for k in range(1, g.seq)])
+    there = Exchange(g, datt_sent, datt_ref, ex_send, ex_recv, ex_local)
     tok, width = x_ref.shape
     wide = up_ref.shape[1]
     pairs = att_ref.shape[0]
@@ -1047,12 +978,13 @@
 
         def permute(step, carry):
             start = step * TILE
-            datt_ref[pair, pl.ds(start, TILE), :] = dot(
+            datt_sent[pair, pl.ds(start, TILE), :] = dot(
                 place_rows(places_ref, pair, start, TILE), ret[...]
             ).astype(BF16)
             return carry
 
         lax.fori_loop(0, tok // TILE, permute, 0)
+        there.start(pair)
 
     def weights(step, carry):
         to = pl.ds(pl.multiple_of(step * TILE, TILE), TILE)
@@ -1068,72 +1000,279 @@
         return carry
 
     lax.fori_loop(0, width // TILE, out_weights, 0)
-
-
-def final_kernel(
+    for pair in range(pairs):
+        there.arrive(pair)
+        there.sent(pair)
+
+
+def middle(g, *args):
+    x, up = args[0], args[6]
+    tok, width = x.shape
+    wide = up.shape[1]
+    pairs = width // PAIR
+    shape = jax.ShapeDtypeStruct
+    any_space, vmem = pl.BlockSpec(memory_space=pl.ANY), pl.BlockSpec(memory_space=pltpu.VMEM)
+    return pl.pallas_call(
+        functools.partial(middle_kernel, g),
+        out_shape=[
+            shape((tok, width), BF16),
+            shape((tok, width), BF16),
+            shape((pairs, g.seq, tok // g.seq, PAIR), BF16),
+            shape((width, width), BF16),
+            shape((width, wide), BF16),
+            shape((wide, width), BF16),
+            shape((8, width), F32),
+            shape((8, wide), F32),
+        ],
+        in_specs=[vmem] * len(args),
+        out_specs=[vmem, vmem, any_space] + [vmem] * 5,
+        scratch_shapes=[
+            pltpu.VMEM((tok, width), BF16),
+            pltpu.VMEM((tok, width), BF16),
+            pltpu.VMEM((tok, wide), BF16),
+            pltpu.VMEM((tok, wide), BF16),
+            pltpu.VMEM((tok, width), BF16),
+            pltpu.VMEM((tok, width), BF16),
+            pltpu.VMEM((TILE, wide), F32),
+            pltpu.VMEM((2 * tok, PAIR), BF16),
+            pltpu.VMEM((pairs, tok, PAIR), BF16),
+            *exchange_sems(g, pairs),
+        ],
+        compiler_params=pltpu.CompilerParams(
+            collective_id=3, has_side_effects=True, vmem_limit_bytes=VMEM_LIMIT
+        ),
+        name="middle",
+    )(*args)
+
+
+def backward_kernel(
+    g,
+    scale,
+    n,
     x_ref,
-    ret_ref,
-    dmid_ref,
-    cols_ref,
     wq_ref,
     wk_ref,
     wv_ref,
-    gtok_ref,
-    gq_ref,
-    gk_ref,
-    gv_ref,
-    gvec_ref,
-    rhs,
-    dqkv,
+    dmid_ref,
+    cols_ref,
+    *refs,
 ):
+    terms, refs = refs[:n], refs[n:]
+    qkv_ref, grad_ref, out_ref, gtok_ref, gq_ref, gk_ref, gv_ref, gvec_ref = refs[:8]
+    sums, refs = refs[8 : 8 + n], refs[8 + n :]
+    out_home, qkv_slots, grad_slots, sent, home, rhs, local, flat, total = refs[:9]
+    bufs, refs = refs[9 : 9 + 4 * n], refs[9 + 4 * n :]
+    rs_send, rs_recv, ex_send, ex_recv, ex_local, load_sem, swap_send, swap_recv = refs
+    pairs = sent.shape[0]
     tok, width = x_ref.shape
-    pairs = ret_ref.shape[0]
+    group = [group_device(g, (group_place(g) + k) % g.seq) for k in range(1, g.seq)]
+    greet(line_peers(g) + group + [swap_partner(g)])
+    plan = Scatter(g, terms, sums, bufs, rs_send, rs_recv, False)
+    swap = Swap(g, out_ref, out_home, swap_send.at[0], swap_recv.at[0])
+    there = Exchange(g, sent, home, ex_send, ex_recv, ex_local)
+    units = len(plan.units)
+
+    def loads(pair):
+        slot = pair % 2
+        return (
+            pltpu.make_async_copy(qkv_ref.at[pair], qkv_slots.at[slot], load_sem.at[0, slot]),
+            pltpu.make_async_copy(grad_ref.at[pair], grad_slots.at[slot], load_sem.at[1, slot]),
+        )
+
+    for copy in loads(0):
+        copy.start()
     gvec_ref[...] = jnp.zeros_like(gvec_ref)
-    for pair in range(pairs):
-
-        def spread(step, carry):
-            rows = pl.ds(step * TILE, TILE)
-            for part in range(3):
-                to = slice(part * PAIR, (part + 1) * PAIR)
-                value = ret_ref[pair, rows, to]
-                low = head_lanes(value.shape)
-                zero = jnp.zeros_like(value)
-                rhs[rows, to] = jnp.where(low, value, zero)
-                rhs[pl.ds(tok + step * TILE, TILE), to] = jnp.where(low, zero, value)
-            return carry
-
-        lax.fori_loop(0, tok // TILE, spread, 0)
-
-        def unpermute(step, carry):
-            start = step * TILE
-            value = dot(token_rows(cols_ref, pair, start, TILE), rhs[...])
-            for part in range(3):
-                piece = value[:, part * PAIR : (part + 1) * PAIR]
-                dqkv[part, pl.ds(start, TILE), pair * PAIR : (pair + 1) * PAIR] = piece.astype(BF16)
-                gvec_ref[part : part + 1, pair * PAIR : (pair + 1) * PAIR] += jnp.sum(
-                    piece, axis=0, keepdims=True
-                )
-            return carry
-
-        lax.fori_loop(0, tok // TILE, unpermute, 0)
-
-    def tokens(step, carry):
-        rows = pl.ds(step * TILE, TILE)
-        total = dmid_ref[rows, :].astype(F32)
-        for part, w_ref in enumerate((wq_ref, wk_ref, wv_ref)):
-            total += dot_nt(dqkv[part, rows, :], w_ref[...])
-        gtok_ref[rows, :] = total.astype(BF16)
+    total[...] = dmid_ref[...].astype(F32)
+
+    def step(t, carry):
+        @pl.when(t < pairs)
+        def _():
+            for copy in loads(t):
+                copy.wait()
+
+            @pl.when(t + 1 < pairs)
+            def _():
+                for copy in loads(t + 1):
+                    copy.start()
+
+            attend_back_pair(t % 2, t, scale, qkv_slots, grad_slots, sent)
+            there.start(t)
+
+        for when in range(pairs + LAG):
+            todo = [
+                (unit, level)
+                for level in (4, 3, 2, 1, 0)
+                for unit in range(units)
+                if unit // 2 + level == when
+            ]
+            if todo or when == 1:
+
+                @pl.when(t == when)
+                def _(todo=todo, when=when):
+                    for unit, level in todo:
+                        plan.step(unit, level)
+                    if when == 1:
+                        swap.start()
+
+        @pl.when(t >= LAG)
+        def _():
+            pair = t - LAG
+            head = pl.ds(pl.multiple_of(pair * PAIR, PAIR), PAIR)
+            there.arrive(pair)
+            per = tok // g.seq
+
+            def spread(owner, carry):
+                for part in range(3):
+                    to = slice(part * PAIR, (part + 1) * PAIR)
+                    value = home[pair, owner, :, to]
+                    low = head_lanes(value.shape)
+                    zero = jnp.zeros_like(value)
+                    at = pl.multiple_of(owner * per, per)
+                    rhs[pl.ds(at, per), to] = jnp.where(low, value, zero)
+                    rhs[pl.ds(tok + at, per), to] = jnp.where(low, zero, value)
+                return carry
+
+            lax.fori_loop(0, g.seq, spread, 0)
+            for part, w_ref in enumerate((wq_ref, wk_ref, wv_ref)):
+                flat[:, part * PAIR : (part + 1) * PAIR] = w_ref[:, head]
+
+            def unpermute(k, carry):
+                start = k * TILE
+                rows = pl.ds(start, TILE)
+                value = dot(token_rows(cols_ref, pair, start, TILE), rhs[...])
+                for part in range(3):
+                    piece = value[:, part * PAIR : (part + 1) * PAIR]
+                    gvec_ref[part : part + 1, head] += jnp.sum(piece, axis=0, keepdims=True)
+                value = value.astype(BF16)
+                local[rows, :] = value
+                total[rows, :] += dot_nt(value, flat[...])
+                return carry
+
+            lax.fori_loop(0, tok // TILE, unpermute, 0)
+
+            def weights(k, carry):
+                rows = pl.ds(pl.multiple_of(k * TILE, TILE), TILE)
+                value = dot_tn(x_ref[:, rows], local[...]).astype(BF16)
+                for part, g_ref in enumerate((gq_ref, gk_ref, gv_ref)):
+                    g_ref[rows, head] = value[:, part * PAIR : (part + 1) * PAIR]
+                return carry
+
+            lax.fori_loop(0, width // TILE, weights, 0)
+
         return carry
 
-    lax.fori_loop(0, tok // TILE, tokens, 0)
-
-    def weights(step, carry):
-        to = pl.ds(pl.multiple_of(step * TILE, TILE), TILE)
-        for part, g_ref in enumerate((gq_ref, gk_ref, gv_ref)):
-            g_ref[:, to] = dot_tn(x_ref[...], dqkv[part, :, to]).astype(BF16)
+    lax.fori_loop(0, pairs + LAG, step, 0)
+    gtok_ref[...] = total[...].astype(BF16)
+    for when in range(pairs + LAG, units // 2 + 6):
+        for level in (4, 3, 2, 1, 0):
+            for unit in range(units):
+                if unit // 2 + level == when:
+                    plan.step(unit, level)
+    swap.wait()
+    plan.sent()
+
+    def close(pair, carry):
+        there.sent(pair)
         return carry
 
-    lax.fori_loop(0, width // TILE, weights, 0)
+    lax.fori_loop(0, pairs, close, 0)
+
+
+def backward(g, scale, x, wq, wk, wv, d_mid, cols, terms, qkv, grad, out):
+    tok, width = x.shape
+    pairs = width // PAIR
+    n = len(terms)
+    shape = jax.ShapeDtypeStruct
+    any_space, vmem = pl.BlockSpec(memory_space=pl.ANY), pl.BlockSpec(memory_space=pltpu.VMEM)
+    dma = pltpu.SemaphoreType.DMA
+    made = pl.pallas_call(
+        functools.partial(backward_kernel, g, scale, n),
+        out_shape=[
+            shape((tok, width), BF16),
+            *([shape((width, width), BF16)] * 3),
+            shape((8, width), F32),
+            *(shape(item.shape[4:], F32) for item in terms),
+            shape(out.shape, BF16),
+        ],
+        in_specs=[vmem] * (6 + n) + [any_space] * 3,
+        out_specs=[vmem] * (5 + n) + [any_space],
+        scratch_shapes=[
+            pltpu.VMEM((2, *qkv.shape[1:]), BF16),
+            pltpu.VMEM((2, *grad.shape[1:]), BF16),
+            pltpu.VMEM(qkv.shape, BF16),
+            pltpu.VMEM(qkv.shape, BF16),
+            pltpu.VMEM((2 * tok, 3 * PAIR), BF16),
+            pltpu.VMEM((tok, 3 * PAIR), BF16),
+            pltpu.VMEM((width, 3 * PAIR), BF16),
+            pltpu.VMEM((tok, width), F32),
+            *Scatter.scratch(g, [item.shape for item in terms], False),
+            *exchange_sems(g, pairs),
+            dma((2, 2)),
+            dma((1,)),
+            dma((1,)),
+        ],
+        compiler_params=pltpu.CompilerParams(
+            collective_id=5, has_side_effects=True, vmem_limit_bytes=VMEM_LIMIT
+        ),
+        name="backward",
+    )(x, wq, wk, wv, d_mid, cols, *terms, qkv, grad, out)
+    return made[0], made[1:4], made[4], made[5 : 5 + n], made[-1]
+
+
+def close_kernel(g, n, small_ref, *refs):
+    terms, gtok_ref, refs = refs[:n], refs[n], refs[n + 1 :]
+    small_out, sums, gtok_home, refs = refs[0], refs[1 : 1 + n], refs[1 + n], refs[2 + n :]
+    bufs, refs = refs[: 4 * n], refs[4 * n :]
+    rs_send, rs_recv, small_bufs, refs = refs[0], refs[1], refs[2:6], refs[6:]
+    small_send, small_recv, swap_send, swap_recv = refs
+    greet(line_peers(g) + [swap_partner(g)])
+    plan = Scatter(g, terms, sums, bufs, rs_send, rs_recv, True)
+    swap = Swap(g, gtok_ref, gtok_home, swap_send.at[0], swap_recv.at[0])
+    small = Total(g, small_ref, small_bufs, small_send, small_recv)
+    units = len(plan.units)
+    for unit in range(units):
+        plan.step(unit, 0)
+    small.start(0, small_ref[...])
+    swap.start()
+    for level in range(1, 5):
+        for unit in range(units):
+            plan.step(unit, level)
+        value = small.take(level - 1)
+        if level < 4:
+            small.start(level, value)
+        else:
+            small_out[...] = value
+    swap.wait()
+    plan.sent()
+    small.sent()
+
+
+def close_call(g, small, terms, gtok):
+    n = len(terms)
+    shape = jax.ShapeDtypeStruct
+    any_space, vmem = pl.BlockSpec(memory_space=pl.ANY), pl.BlockSpec(memory_space=pltpu.VMEM)
+    dma = pltpu.SemaphoreType.DMA
+    made = pl.pallas_call(
+        functools.partial(close_kernel, g, n),
+        out_shape=[
+            shape(small.shape, F32),
+            *(shape(item.shape[4:], F32) for item in terms),
+            shape(gtok.shape, BF16),
+        ],
+        in_specs=[vmem] * (1 + n) + [any_space],
+        out_specs=[vmem] * (1 + n) + [any_space],
+        scratch_shapes=[
+            *Scatter.scratch(g, [item.shape for item in terms], True),
+            *Total.scratch(g, small.shape),
+            dma((1,)),
+            dma((1,)),
+        ],
+        compiler_params=pltpu.CompilerParams(
+            collective_id=6, has_side_effects=True, vmem_limit_bytes=VMEM_LIMIT
+        ),
+        name="close",
+    )(small, *terms, gtok)
+    return made[0], made[1:-1], made[-1]
 
 
 def body(
@@ -1164,8 +1303,6 @@
     wide = up_weight.shape[1]
     per_owner = tok // g.seq
     scale = (width // heads) ** -0.5
-    both = ("batch", "seq")
-    swap = functools.partial(lax.ppermute, axis_name=both, perm=g.swap_pairs())
 
     slots = cluster_slot[0]
     places = slots // tok * per_owner + slots % tok // g.seq
@@ -1212,97 +1349,61 @@
     )
     up, down = (item.reshape(g.n * item.shape[4], item.shape[5]) for item in (up, down))
 
-    shape = jax.ShapeDtypeStruct
-    (out, d_mid, d_att, g_out, g_up, g_down, g_rows, g_upb) = vmem_call(
-        middle_kernel,
-        [
-            shape((tok, width), BF16),
-            shape((tok, width), BF16),
-            shape((pairs, tok, PAIR), BF16),
-            shape((width, width), BF16),
-            shape((width, wide), BF16),
-            shape((wide, width), BF16),
-            shape((8, width), F32),
-            shape((8, wide), F32),
-        ],
-        [
-            pltpu.VMEM((tok, width), BF16),
-            pltpu.VMEM((tok, width), BF16),
-            pltpu.VMEM((tok, wide), BF16),
-            pltpu.VMEM((tok, wide), BF16),
-            pltpu.VMEM((tok, width), BF16),
-            pltpu.VMEM((tok, width), BF16),
-            pltpu.VMEM((TILE, wide), F32),
-            pltpu.VMEM((2 * tok, PAIR), BF16),
-        ],
-        "middle",
-    )(x, returned.reshape(pairs, tok, PAIR), grad, table, cols, wo, up, down, rows[2:], up_row)
-
-    (routed,) = exchange(g, [d_att.reshape(pairs, g.seq, per_owner, PAIR)], 4)
-    d_qkv = attend_back(qkv, routed, scale)
-    (d_home,) = exchange(g, [d_qkv], 5)
-
-    grad_tokens, g_query, g_key, g_value, g_rows_attn = vmem_call(
-        final_kernel,
-        [
-            shape((tok, width), BF16),
-            shape((width, width), BF16),
-            shape((width, width), BF16),
-            shape((width, width), BF16),
-            shape((8, width), F32),
-        ],
-        [
-            pltpu.VMEM((2 * tok, 3 * PAIR), BF16),
-            pltpu.VMEM((3, tok, width), BF16),
-        ],
-        "final",
-    )(x, d_home.reshape(pairs, tok, 3 * PAIR), d_mid, cols, wq, wk, wv)
-
-    lines = jnp.stack([g_rows_attn[0], g_rows_attn[2], *(g_rows[i] for i in range(6))])
-    lines = lines.reshape(8, g.n, count).transpose(1, 0, 2).reshape(g.n, 8 * count)
-    place = group_place(g)
-    blocks = stats.shape[1] and tok // CLUSTER
-    here = jnp.arange(g.n, dtype=jnp.int32)[:, None] % g.seq == place
-    own = jnp.where(here, stats[:2, :blocks].reshape(1, 2 * blocks), 0.0)
-    small = jnp.concatenate([lines, g_upb[0].reshape(g.n, wide // g.n), own], axis=1)
-    used = small.shape[1]
-    small = jnp.pad(small, ((0, 0), (0, -used % (8 * PAIR))))
-    split = (g.Y, 2, Z, g.X)
+    out, d_mid, routed, g_out, g_up, g_down, g_rows, g_upb = middle(
+        g,
+        x,
+        returned.reshape(pairs, tok, PAIR),
+        grad,
+        table,
+        cols,
+        wo,
+        up,
+        down,
+        rows[2:],
+        up_row,
+    )
 
     def parts(item):
         rows, cols = item.shape[0] // g.n, item.shape[1]
         if rows % 8:
             rows, cols = rows * cols // PAIR, PAIR
-        return item.reshape(*split, rows, cols)
-
-    sums = scatter(
-        g,
+        return item.reshape(g.Y, 2, Z, g.X, rows, cols)
+
+    grad_tokens, g_attn, g_bias, s_ffn, out = backward(
+        g, scale, x, wq, wk, wv, d_mid, cols, [parts(g_up), parts(g_down), parts(g_out)], qkv, routed, out
+    )
+    lines = wide // width
+    small = jnp.concatenate(
         [
-            small.reshape(*split, -1, PAIR),
-            parts(g_up),
-            parts(g_down),
-            parts(g_out),
-            parts(g_query),
-            parts(g_key),
-            parts(g_value),
+            g_bias[0:1],
+            g_bias[2:3],
+            g_rows[:6],
+            g_upb[0].reshape(lines, width),
+            jnp.pad(stats[:2], ((0, 0), (0, width - stats.shape[1]))),
+            jnp.zeros((6 - lines, width), F32),
         ],
+        axis=0,
     )
-    vector = sums[0].reshape(-1)
-    gq, gv, go, gg1, gs1, gd, gg2, gs2 = (
-        vector[i * count : (i + 1) * count] for i in range(8)
-    )
-    gu = vector[8 * count : 8 * count + wide // g.n]
-    cluster_stats = vector[used - 2 * blocks : used].reshape(2, blocks)
+    small, s_attn, grad_tokens = close_call(g, small, [parts(item) for item in g_attn], grad_tokens)
+
+    b, s = lax.axis_index("batch"), lax.axis_index("seq")
+    here = b * g.seq + s
+    mine = lax.dynamic_slice(small, (0, here * count), (8, count))
+    wide_count = wide // g.n
+    gu = lax.dynamic_slice(small[8 : 8 + lines].reshape(wide), (here * wide_count,), (wide_count,))
+    blocks = tok // CLUSTER
+    cluster_stats = lax.dynamic_slice(small, (8 + lines, s * blocks), (2, blocks))
     s_up, s_down, s_out, s_query, s_key, s_value = (
         item.reshape(local.shape)
         for item, local in zip(
-            sums[1:],
+            (*s_ffn, *s_attn),
             (up_weight, down_weight, output_weight, query_weight, key_weight, value_weight),
         )
     )
+    gq, gv, go, gg1, gs1, gd, gg2, gs2 = (mine[i] for i in range(8))
     return (
-        swap(out)[None],
-        swap(grad_tokens)[None],
+        out[None],
+        grad_tokens[None],
         s_query,
         s_key,
         s_value,

time: 574 us -> 479 us (0.83)
  Pallas kernels: 540 us -> 448 us
    pallas_call x6 -> x3, Pallas kernels: 353 us -> 261 us  [the longest x1 120 us: backward(): pl.pallas_call(functools.partial(backward_kernel, g, scale, n), out_shape...]
  transfers between devices with their start and end apart: 2 -> 0, of which waited for: 0 -> 0; matrix products, arithmetic and copies ran while one was open for 1% -> 0% of each run, Pallas kernels for 24% -> 0%
where the time goes in v3:
time: 479 us; the launch traced here: 478 us
  Pallas kernels  448 us (94%)
  local copies, waits for them, and re-layouts  26.1 us (5%)
    pallas_call x1, Pallas kernels, forward(): pl.pallas_call(functools.partial(forward_kernel, g, scale, factor), out_s...  126 us
    pallas_call x1, Pallas kernels, backward(): pl.pallas_call(functools.partial(backward_kernel, g, scale, n), out_shape...  120 us
    pallas_call x1, Pallas kernels, middle(): pl.pallas_call(functools.partial(middle_kernel, g), out_shape=[shape((tok...  85.6 us
    pallas_call x1, Pallas kernels, open_call(): pl.pallas_call(functools.partial(open_kernel, g), out_shape=[*(shape((g.Y...  60.9 us
    pallas_call x1, Pallas kernels, close_call(): pl.pallas_call(functools.partial(close_kernel, g, n), out_shape=[shape(sm...  55.1 us

profile of v3, /device:TPU:0, one launch (start us, length us, event | category | flops | bytes accessed | tf_op | source)
XLA Modules:
  0.0 478.1 jit_solution(15956210842200254239)
XLA Ops:
  0.7 0.9 fusion.1
  1.6 0.1 pad.15.clone
  1.6 1.4 add_add_fusion.refs_6_
  3.0 6.1 %concatenate.9 = bf16[288]{0:T(512)(128)(2,1)S(1)} concatenate(bf16[24]{0:T(256)(128)(2,1)} %param.27, bf16[24]{0:T(256)(128)(2,1)} %param.28, bf16[24]{0:T(256)(128)(2,1)} %param.29, bf16[24]{0:T(256)(128)(2,1)} %param.30, bf16[24]{0:T(256)(128)(2,1)} %param.31, bf16[24]{0:T(256)(128)(2,1)} %param.35, bf16[24]{0:T(256)(128)(2,1)} %param.36, bf16[24]{0:T(256)(128)(2,1)} %param.37, ...), dimensions={0} | concatenate | bytes 1152 | tf_op jit(solution)/shard_map/concatenate | solution.py:1323
  9.1 0.6 pad_bitcast_fusion.refs_0_
  9.7 60.9 %open.1 = (bf16[2,2,4,2,3,128]{5,4,3,2,1,0:T(4,128)(2,1)}, bf16[2,2,4,2,24,768]{5,4,3,2,1,0:T(8,128)(2,1)}, bf16[2,2,4,2,24,768]{5,4,3,2,1,0:T(8,128)(2,1)}, bf1...) custom-call(bf16[3,128]{1,0:T(4,128)(2,1)} %pad_bitcast_fusion.refs_, ...), custom_call_target="tpu_custom_call" | custom-call | tf_op jit(solution)/shard_map/open/pallas_call | solution.py:231
  70.6 0.8 copy.59
  71.4 0.1 reshape.98
  71.5 0.1 slice_reduce_fusion.1
  71.6 0.1 slice.68
  71.7 0.1 slice.70
  71.8 0.1 pad.11.clone
  71.8 0.7 pad_maximum_fusion.bias_ref
  72.5 1.8 copy.39
  74.3 126.2 %forward.1 = (bf16[2,2,4,2,24,3072]{5,4,3,2,1,0:T(8,128)(2,1)}, bf16[2,2,4,2,96,768]{5,4,3,2,1,0:T(8,128)(2,1)}, bf16[1024,768]{1,0:T(8,128)(2,1)}, bf16[6,8,128...) custom-call(bf16[1024,768]{1,0:T(8,128)(2,1)} %get-tuple-element.53.x_ref, ...), custom_call_target="tpu_custom_call" | custom-call | tf_op jit(solution)/shard_map/forward/pallas_call | solution.py:758
  200.6 0.7 slice.72.vec_ref
  201.3 0.1 slice.92
  201.3 0.7 reshape.103.up_bias_ref
  202.0 85.6 %middle.1 = (bf16[1024,768]{1,0:T(8,128)(2,1)}, bf16[1024,768]{1,0:T(8,128)(2,1)}, bf16[6,8,128,128]{3,2,1,0:T(8,128)(2,1)}, bf16[768,768]{1,0:T(8,128)(2,1)}, b...) custom-call(bf16[1024,768]{1,0:T(8,128)(2,1)} %get-tuple-element.53.x_ref, ...), custom_call_target="tpu_custom_call" | custom-call | tf_op jit(solution)/shard_map/middle/pallas_call | solution.py:1015
  287.7 0.0 copy-start.8
  287.7 120.5 %backward.1 = (bf16[1024,768]{1,0:T(8,128)(2,1)}, bf16[768,768]{1,0:T(8,128)(2,1)}, bf16[768,768]{1,0:T(8,128)(2,1)}, bf16[768,768]{1,0:T(8,128)(2,1)}, f32[8,76...) custom-call(bf16[1024,768]{1,0:T(8,128)(2,1)} %get-tuple-element.53.x_r, ...), custom_call_target="tpu_custom_call" | custom-call | tf_op jit(solution)/shard_map/backward/pallas_call | solution.py:1188
  408.2 0.8 fusion.7
  409.0 0.9 slice_reduce_fusion.2
  409.9 0.7 slice.78
  410.6 0.0 copy-done.8
  410.6 1.3 concatenate.11.small_ref
  411.9 0.0 copy-start
  411.9 55.1 %close.1 = (f32[16,768]{1,0:T(8,128)}, f32[24,768]{1,0:T(8,128)}, f32[24,768]{1,0:T(8,128)}, f32[24,768]{1,0:T(8,128)}, bf16[1024,768]{1,0:T(8,128)(2,1)}) custom-call(f32[16,768]{1,0:T(8,128)} %concatenate.11.small_ref, bf16[2,2,4,2,24,768]{5,4,3,2,1,0:T(8,128)(2,1)} %bitcast.81, bf16[2,2,4,2,24,768]{5,4,3,2,1,0:T(8,128)(2,1)} %bitcast.82, ...), custom_call_target="tpu_custom_call" | custom-call | tf_op jit(solution)/shard_map/close/pallas_call | solution.py:1255
  467.0 0.7 slice.84
  467.7 0.6 dynamic_slice.10
  468.3 0.8 constant_dynamic-slice_fusion.1
  469.1 0.5 slice_bitcast_fusion
  469.6 1.3 constant_dynamic-slice_fusion
  470.9 0.0 copy-done
  470.9 0.0 copy-start.1
  470.9 1.1 copy.68
  472.1 0.8 copy-done.1
  472.9 0.0 copy-start.7
  472.9 0.0 copy-start.6
  472.9 0.0 copy-start.5
  472.9 0.0 copy-start.4
  472.9 0.0 copy-start.3
  472.9 0.0 copy-start.2
  472.9 1.1 copy.69
  474.1 0.0 copy-done.7
  474.1 0.6 copy.70
  474.7 0.0 copy-done.6
  474.7 0.6 copy.71
  475.4 0.0 copy-done.5
  475.4 0.6 copy.72
  476.0 0.0 copy-done.4
  476.0 0.6 copy.73
  476.6 0.0 copy-done.3
  476.6 0.7 copy.74
  477.3 0.0 copy-done.2
  477.3 0.7 copy.75
  (8 shorter events, 0.1 us)
Async XLA Ops:
  287.7 122.9 %copy-start.8 = (f32[8,768]{1,0:T(8,128)S(1)}, f32[8,768]{1,0:T(8,128)}, u32[]{:S(2)}) copy-start(f32[8,768]{1,0:T(8,128)} %get-tuple-element.73) | copy-start | bytes 73732
  411.9 59.1 %copy-start = (bf16[1024,768]{1,0:T(8,128)(2,1)S(1)}, bf16[1024,768]{1,0:T(8,128)(2,1)}, u32[]{:S(2)}) copy-start(bf16[1024,768]{1,0:T(8,128)(2,1)} %get-tuple-element.71) | copy-start | bytes 4718596
  470.9 2.0 copy-start.1
  472.9 1.2 copy-start.7
  472.9 1.8 copy-start.6
  472.9 2.4 copy-start.5
  472.9 3.1 copy-start.4
  472.9 3.7 copy-start.3
  472.9 4.4 copy-start.2

commit v4 on v3

v4 whole, which is shorter than its diff:
```python
import functools

import jax
import jax.numpy as jnp
from jax import lax
from jax.experimental import pallas as pl
from jax.experimental.pallas import tpu as pltpu
from jax.sharding import PartitionSpec as P

MESH = pl.DeviceIdType.MESH
F32 = jnp.float32
BF16 = jnp.bfloat16
EPSILON = 1e-12
CLUSTER = 128
PAIR = 128
Z = 4
VMEM_LIMIT = 58 * 1024 * 1024


class Grid:
    def __init__(self, mesh):
        self.batch, self.seq = mesh.shape["batch"], mesh.shape["seq"]
        self.Y, self.X = self.batch // 2, self.seq // Z
        self.half = self.seq // 2
        self.n = self.batch * self.seq


AXES = ("y", "c", "h", "l", "x")


def sizes(g):
    return {"y": g.Y, "c": 2, "h": 2, "l": Z // 2, "x": g.X}


def coords(g):
    b, s = lax.axis_index("batch"), lax.axis_index("seq")
    z = s // g.X
    return {"y": b // 2, "c": b % 2, "h": z // (Z // 2), "l": z % (Z // 2), "x": s % g.X}


def device(g, at):
    return (at["y"] * 2 + at["c"], (at["h"] * (Z // 2) + at["l"]) * g.X + at["x"])


def along(g, at, axis):
    size = sizes(g)[axis]
    places = [(at[axis] + k) % size for k in range(1, size)]
    return [(place, device(g, {**at, axis: place})) for place in places]


def group_place(g):
    b, s = lax.axis_index("batch"), lax.axis_index("seq")
    return b % 2 * g.half + s % g.half


def group_device(g, place):
    b, s = lax.axis_index("batch"), lax.axis_index("seq")
    return (b // 2 * 2 + place // g.half, s // g.half * g.half + place % g.half)


def line_peers(g, axes=AXES):
    at = coords(g)
    return [peer for axis in axes for _, peer in along(g, at, axis)]


def greet(peers):
    barrier = pltpu.get_barrier_semaphore()
    for peer in peers:
        pl.semaphore_signal(barrier, inc=1, device_id=peer, device_id_type=MESH)
    pl.semaphore_wait(barrier, len(peers))


def remote(src, dst, send, recv, peer):
    return pltpu.make_async_remote_copy(
        src_ref=src,
        dst_ref=dst,
        send_sem=send,
        recv_sem=recv,
        device_id=peer,
        device_id_type=MESH,
    )


def lane_pieces(shape):
    rows, cols = shape
    if cols % PAIR or rows * cols <= 24 * 768:
        return [(0, cols)]
    count = {3072: 4, 768: 3}.get(cols, 1)
    return [(k * (cols // count), cols // count) for k in range(count)]


class Gather:
    def __init__(self, g, ins, outs, dims, done, plan, sends, recvs, local_sem):
        self.g, self.ins, self.outs, self.dims, self.done = g, ins, outs, dims, done
        self.plan = plan
        self.sends, self.recvs, self.local_sem = sends, recvs, local_sem
        self.at = coords(g)
        self.units = [
            (index, pl.ds(start, size))
            for index, item in enumerate(ins)
            for start, size in lane_pieces(item.shape[-2:])
        ]

    @staticmethod
    def sems(g, shapes):
        units = sum(len(lane_pieces(shape[-2:])) for shape in shapes)
        slots = units * sum(sizes(g).values())
        dma = pltpu.SemaphoreType.DMA
        return [dma((slots,)), dma((slots,)), dma((units,))]

    def source(self, unit):
        index, cols = self.units[unit]
        return self.ins[index].at[(*([slice(None)] * (len(self.ins[index].shape) - 1)), cols)]

    def view(self, unit, done):
        index, cols = self.units[unit]
        spot = tuple(slice(None) if axis in done else self.at[axis] for axis in self.dims)
        return self.outs[index].at[(*spot, slice(None), cols)]

    def own(self, unit):
        return pltpu.make_async_copy(
            self.source(unit), self.view(unit, self.done), self.local_sem.at[unit]
        )

    def levels(self, unit):
        return self.plan(unit)

    def moves(self, unit, level):
        g = self.g
        axes = self.levels(unit)
        view = self.view(unit, (*self.done, *axes[:level]))
        src = self.source(unit) if level == 0 else view
        size = sizes(g)
        base = unit * sum(size.values())
        for axis in AXES[: AXES.index(axes[level])]:
            base += size[axis]
        return [
            remote(src, view, self.sends.at[base + k], self.recvs.at[base + k], peer)
            for k, (_, peer) in enumerate(along(g, self.at, axes[level]))
        ]

    def start(self, unit, level):
        if level == 0:
            self.own(unit).start()
        else:
            if level == 1:
                self.own(unit).wait()
            for copy in self.moves(unit, level - 1):
                copy.wait_recv()
        for copy in self.moves(unit, level):
            copy.start()

    def finish(self):
        count = len(self.units)
        for unit in range(count):
            for copy in self.moves(unit, len(self.levels(unit)) - 1):
                copy.wait_recv()
        for unit in range(count):
            for level in range(len(self.levels(unit))):
                for copy in self.moves(unit, level):
                    copy.wait_send()


class Swap:
    def __init__(self, g, src, dst, sends, recvs, pieces=1):
        b, s = lax.axis_index("batch"), lax.axis_index("seq")
        self.native = b % 2 == s // g.half
        self.peer = swap_partner(g)
        self.ends = (src, dst, sends, recvs)
        self.pieces = pieces

    @staticmethod
    def sems(pieces=1):
        return [pltpu.SemaphoreType.DMA((pieces,)), pltpu.SemaphoreType.DMA((pieces,))]

    def piece(self, k):
        src, dst, sends, recvs = self.ends
        size = src.shape[0] // self.pieces
        rows = pl.ds(pl.multiple_of(k * size, size), size)
        return src.at[rows], dst.at[rows], sends.at[k], recvs.at[k]

    def start(self, k=0):
        src, dst, send, recv = self.piece(k)

        @pl.when(self.native)
        def _():
            pltpu.make_async_copy(src, dst, recv).start()

        @pl.when(jnp.logical_not(self.native))
        def _():
            remote(src, dst, send, recv, self.peer).start()

    def wait(self):
        for k in range(self.pieces):
            self.wait_piece(k)

    def wait_piece(self, k):
        src, dst, send, recv = self.piece(k)

        @pl.when(self.native)
        def _():
            pltpu.make_async_copy(src, dst, recv).wait()

        @pl.when(jnp.logical_not(self.native))
        def _():
            remote(src, dst, send, recv, self.peer).wait()


def swap_partner(g):
    b, s = lax.axis_index("batch"), lax.axis_index("seq")
    return (b // 2 * 2 + 1 - b % 2, (s + g.half) % g.seq)


PART = ("h", "l", "x")
PIECES, WINDOW = 16, 2


MASK_AT = 4


def masks_in_order(heads, table_ref, block, size, out_ref):
    tok = table_ref.shape[1]
    start = block * size
    rows = lax.broadcasted_iota(jnp.int32, (size, tok), 0) + start
    lanes = lax.broadcasted_iota(jnp.int32, (size, PAIR), 1)
    mask = table_ref[heads : heads + 1, :] > 0
    made = jnp.zeros((size, PAIR), F32)
    for head in range(heads):
        places = jnp.where(mask, table_ref[head : head + 1, :], -1)
        found = jnp.sum(jnp.where(rows == places, 1.0, 0.0), axis=1, keepdims=True)
        made = jnp.where(lanes == head, found, made)
    out_ref[start : start + size, :] = made.astype(BF16)


def open_kernel(g, n, m, *refs):
    ins, refs = refs[: n + m], refs[n + m :]
    swap_in, refs = refs[:2], refs[2:]
    outs, refs = refs[: n + m], refs[n + m :]
    swap_out, mask_ref, sems = refs[:2], refs[2], refs[3:]
    greet(line_peers(g) + [swap_partner(g)])
    whole = Gather(
        g,
        ins[:n],
        outs[:n],
        AXES,
        (),
        lambda unit: ("h", "l", "x", "y", "c"),
        *sems[:3],
    )
    part = Gather(g, ins[n:], outs[n:], PART, (), lambda unit: PART, *sems[3:6])
    tokens = Swap(g, swap_in[0], swap_out[0], *sems[6:8], PIECES)
    table = Swap(g, swap_in[1], swap_out[1], *sems[8:10])
    plans = [(whole, unit) for unit in range(len(whole.units))]
    plans += [(part, unit) for unit in range(len(part.units))]
    table.start()
    tok, width = swap_in[0].shape
    heads, blocks = width * 2 // PAIR, 8
    for t in range(len(plans) + 4 * WINDOW):
        for level in range(5):
            k = t - level * WINDOW
            if 0 <= k < len(plans):
                plan, unit = plans[k]
                if level < len(plan.levels(unit)):
                    plan.start(unit, level)
        if t < PIECES:
            tokens.start(t)
        if t == MASK_AT:
            table.wait()
        if 0 <= t - MASK_AT < blocks:
            masks_in_order(heads, swap_out[1], t - MASK_AT, tok // blocks, mask_ref)
    whole.finish()
    part.finish()
    tokens.wait()


def open_call(g, whole, part, swapped):
    any_space = pl.BlockSpec(memory_space=pl.ANY)
    shape = jax.ShapeDtypeStruct
    size = sizes(g)
    n, m = len(whole), len(part)
    outs = [
        *(shape((*(size[axis] for axis in AXES), *item.shape), item.dtype) for item in whole),
        *(shape((*(size[axis] for axis in PART), *item.shape), item.dtype) for item in part),
        *(shape(item.shape, item.dtype) for item in swapped),
    ]
    vmem = pl.BlockSpec(memory_space=pltpu.VMEM)
    made = pl.pallas_call(
        functools.partial(open_kernel, g, n, m),
        out_shape=[*outs, shape((swapped[0].shape[0], PAIR), BF16)],
        in_specs=[any_space] * len(outs),
        out_specs=[any_space] * (len(outs) - 1) + [vmem] * 2,
        scratch_shapes=[
            *Gather.sems(g, [item.shape for item in whole]),
            *Gather.sems(g, [item.shape for item in part]),
            *Swap.sems(PIECES),
            *Swap.sems(),
        ],
        compiler_params=pltpu.CompilerParams(
            collective_id=0, has_side_effects=True, vmem_limit_bytes=VMEM_LIMIT
        ),
        name="open",
    )(*whole, *part, *swapped)
    return made[:n], made[n : n + m], made[n + m :]


class Scatter:
    def __init__(self, g, ins, bufs, plans, sends, recvs):
        self.g, self.ins, self.bufs, self.plans = g, ins, bufs, plans
        self.sends, self.recvs = sends, recvs
        self.at = coords(g)
        self.units = [
            (index, pl.ds(start, size))
            for index, item in enumerate(ins)
            for start, size in lane_pieces(item.shape[-2:])
        ]

    @staticmethod
    def scratch(g, shapes, plans):
        size = sizes(g)
        made = []
        for shape, plan in zip(shapes, plans):
            left = list(AXES)
            for axis in plan:
                left.remove(axis)
                lead = (size[axis] - 1, *(size[other] for other in left))
                made.append(pltpu.VMEM((*lead, *shape[-2:]), BF16))
        units = sum(len(lane_pieces(shape[-2:])) for shape in shapes)
        slots = units * sum(size.values())
        return [*made, pltpu.SemaphoreType.DMA((slots,)), pltpu.SemaphoreType.DMA((slots,))]

    def held(self, index, level):
        return self.bufs[index * len(AXES) + level]

    def store(self, index, level):
        if level == 0:
            return self.ins[index], AXES
        left = tuple(axis for axis in AXES if axis not in self.plans[index][:level])
        return self.held(index, level - 1).at[0], left

    def moves(self, unit, level):
        g = self.g
        index, cols = self.units[unit]
        axis = self.plans[index][level]
        src, left = self.store(index, level)
        held = self.held(index, level)
        size = sizes(g)
        base = unit * sum(size.values())
        for other in AXES[: AXES.index(axis)]:
            base += size[other]
        a = slice(None)
        rest = (a,) * len(left)
        made = []
        for k, (place, peer) in enumerate(along(g, self.at, axis)):
            spot = tuple(place if other == axis else a for other in left)
            made.append(
                remote(
                    src.at[(*spot, a, cols)],
                    held.at[(k, *rest, cols)],
                    self.sends.at[base + k],
                    self.recvs.at[base + k],
                    peer,
                )
            )
        return made

    def add(self, unit, level, out=None):
        g = self.g
        index, cols = self.units[unit]
        axis = self.plans[index][level]
        src, left = self.store(index, level)
        held = self.held(index, level)
        size = sizes(g)
        rest = [other for other in left if other != axis]
        loop = [other for other in rest if other in ("h", "l")]
        count = 1
        for other in loop:
            count *= size[other]
        static = [other for other in rest if other not in loop]
        a = slice(None)

        def some(step, carry):
            spots = [{}]
            for other in static:
                spots = [{**spot, other: k} for spot in spots for k in range(size[other])]
            for spot in spots:
                if len(loop) == 2:
                    spot = {**spot, "h": step // size["l"], "l": step % size["l"]}
                elif loop:
                    spot = {**spot, loop[0]: step}
                where = tuple(spot[other] for other in rest)
                mine = tuple(self.at[axis] if other == axis else spot[other] for other in left)
                total = src[(*mine, a, cols)].astype(F32)
                for k in range(size[axis] - 1):
                    total += held[(k, *where, a, cols)].astype(F32)
                if out is None:
                    held[(0, *where, a, cols)] = total.astype(BF16)
                else:
                    out[(*where, a, cols)] = total.astype(out.dtype)
            return carry

        lax.fori_loop(0, count, some, 0)

    def step(self, unit, level, out=None):
        if level:
            for copy in self.moves(unit, level - 1):
                copy.wait_recv()
            last = level == len(AXES)
            self.add(unit, level - 1, out[self.units[unit][0]] if last else None)
        if level < len(AXES):
            for copy in self.moves(unit, level):
                copy.start()

    def sent(self):
        for unit in range(len(self.units)):
            for level in range(len(AXES)):
                for copy in self.moves(unit, level):
                    copy.wait_send()


class Total:
    def __init__(self, g, held, bufs, sends, recvs):
        self.g, self.held, self.bufs = g, held, bufs
        self.sends, self.recvs = sends, recvs
        self.at = coords(g)

    @staticmethod
    def scratch(g, shape):
        slots = sum(sizes(g).values())
        return [
            *(pltpu.VMEM((sizes(g)[axis], *shape), F32) for axis in AXES),
            pltpu.SemaphoreType.DMA((slots,)),
            pltpu.SemaphoreType.DMA((slots,)),
        ]

    def moves(self, level):
        g = self.g
        axis = AXES[level]
        view = self.bufs[level].at[self.at[axis]]
        base = sum(sizes(g)[other] for other in AXES[:level])
        return [
            remote(view, view, self.sends.at[base + k], self.recvs.at[base + k], peer)
            for k, (_, peer) in enumerate(along(g, self.at, axis))
        ]

    def start(self, level, value):
        self.bufs[level][self.at[AXES[level]]] = value
        for copy in self.moves(level):
            copy.start()

    def take(self, level):
        for copy in self.moves(level):
            copy.wait_recv()
        buf = self.bufs[level]
        total = buf[0]
        for k in range(1, buf.shape[0]):
            total = total + buf[k]
        return total

    def sent(self):
        for level in range(len(AXES)):
            for copy in self.moves(level):
                copy.wait_send()


def dot(left, right):
    return lax.dot_general(left, right, (((1,), (0,)), ((), ())), preferred_element_type=F32)


def dot_nt(left, right):
    return lax.dot_general(left, right, (((1,), (1,)), ((), ())), preferred_element_type=F32)


def dot_tn(left, right):
    return lax.dot_general(left, right, (((0,), (0,)), ((), ())), preferred_element_type=F32)


def head_lanes(shape):
    return lax.broadcasted_iota(jnp.int32, shape, 1) < PAIR // 2


def split_pair(value, axis=0):
    low = head_lanes(value.shape)
    zero = jnp.zeros_like(value)
    return jnp.concatenate(
        [jnp.where(low, value, zero), jnp.where(low, zero, value)], axis=axis
    )


def swap_halves(value):
    return pltpu.roll(value.astype(F32), PAIR // 2, 1).astype(value.dtype)


def pack(q, k, v):
    low = head_lanes(q.shape)
    k = swap_halves(k)
    return jnp.where(low, q, k), jnp.where(low, v, q), jnp.where(low, k, v)


def unpack(first, second, third):
    low = head_lanes(first.shape)
    return (
        jnp.where(low, first, second),
        swap_halves(jnp.where(low, third, first)),
        jnp.where(low, second, third),
    )


def place_rows(places_ref, head, start, size):
    tok = places_ref.shape[1]
    rows = lax.broadcasted_iota(jnp.int32, (size, tok), 0) + start
    return (rows == places_ref[pl.ds(head, 1), :]).astype(F32).astype(BF16)


def token_rows(cols_ref, head, start, size):
    tok, width = cols_ref.shape
    lanes = lax.broadcasted_iota(jnp.int32, (size, tok), 1)
    heads = lax.broadcasted_iota(jnp.int32, (size, width), 1)
    table = cols_ref[pl.ds(start, size), :].astype(F32)
    place = jnp.sum(jnp.where(heads == head, table, 0.0), axis=1, keepdims=True)
    return (lanes == place.astype(jnp.int32)).astype(F32).astype(BF16)


def move_rows(pick, value_ref):
    one = dot(pick(0), value_ref[:, : 2 * PAIR])
    two = dot(pick(1), value_ref[:, PAIR:])
    low = head_lanes((one.shape[0], PAIR))
    return one[:, :PAIR], jnp.where(low, one[:, PAIR:], two[:, :PAIR]), two[:, PAIR:]


def move_pair(pick, value):
    one, two = dot(pick(0), value), dot(pick(1), value)
    return jnp.where(head_lanes(one.shape), one, two)


def gather_rows(block_ref, lead, start, size, lanes):
    part = block_ref[(*lead, slice(None), pl.ds(start, size), lanes)]
    if size % 16:
        part = part.astype(F32)
    return part.reshape(part.shape[0] * size, part.shape[2]).astype(block_ref.dtype)


def spread_rows(value, sources, kind):
    size = value.shape[0] // sources
    if size % 16:
        return value.astype(F32).reshape(sources, size, value.shape[1]).astype(kind)
    return value.astype(kind).reshape(sources, size, value.shape[1])


ROWS = 512


def pair_weights(pair, w_refs, out_ref):
    head = pl.ds(pl.multiple_of(pair * PAIR, PAIR), PAIR)
    for part, value in enumerate(pack(*(w_ref[:, head] for w_ref in w_refs))):
        out_ref[:, part * PAIR : (part + 1) * PAIR] = value


def project_pair(pair, x_ref, w_refs, bias_ref, places_ref, flat, rhs, out_ref):
    tok = x_ref.shape[0]
    head = pl.ds(pl.multiple_of(pair * PAIR, PAIR), PAIR)
    pair_weights(pair, w_refs, flat)
    bias = jnp.concatenate(
        pack(*(jnp.broadcast_to(bias_ref[i : i + 1, head], (8, PAIR)) for i in range(3))), axis=1
    )[0:1]

    def project(step, carry):
        rows = pl.ds(step * ROWS, ROWS)
        rhs[rows, :] = (dot(x_ref[rows, :], flat[...]) + bias).astype(BF16)
        return carry

    lax.fori_loop(0, tok // ROWS, project, 0)

    def permute(step, carry):
        start = step * ROWS
        made = move_rows(lambda i: place_rows(places_ref, 2 * pair + i, start, ROWS), rhs)
        for part, value in enumerate(made):
            out_ref[pair, pl.ds(start, ROWS), part * PAIR : (part + 1) * PAIR] = value.astype(BF16)
        return carry

    lax.fori_loop(0, tok // ROWS, permute, 0)


def attend_pair(pair, scale, qkv_ref, out_ref, entropy_ref):
    _, sources, per_owner, _ = qkv_ref.shape
    size = CLUSTER // sources
    clusters = per_owner // size
    lanes = lax.broadcasted_iota(jnp.int32, (CLUSTER, PAIR), 1)
    for cluster in range(clusters):
        q, k, v = unpack(
            *(
                gather_rows(qkv_ref, (pair,), cluster * size, size, slice(i * PAIR, (i + 1) * PAIR))
                for i in range(3)
            )
        )
        scores = cluster_scores(split_pair(q), k, scale)
        top = jnp.max(scores, axis=1, keepdims=True)
        weights = jnp.exp(scores - top)
        totals = jnp.sum(weights, axis=1, keepdims=True)
        probs = weights / totals
        entropy = top + jnp.log(totals) - jnp.sum(probs * scores, axis=1, keepdims=True)
        low = probs.astype(BF16)
        mixed = dot(
            jnp.concatenate([low[:CLUSTER], low[CLUSTER:]], axis=1), split_pair(v)
        )
        out_ref[pair, :, cluster * size : (cluster + 1) * size, :] = spread_rows(
            mixed, sources, BF16
        )
        entropy_ref[cluster] = jnp.where(
            lanes == 2 * pair,
            entropy[:CLUSTER],
            jnp.where(lanes == 2 * pair + 1, entropy[CLUSTER:], entropy_ref[cluster]),
        )


class Exchange:
    def __init__(self, g, kind, src, dst, sends, recvs, local_sem):
        self.g, self.kind, self.src, self.dst = g, kind, src, dst
        self.sends, self.recvs, self.local_sem = sends, recvs, local_sem
        b, s = lax.axis_index("batch"), lax.axis_index("seq")
        self.b, self.s = b, s
        self.me = s if kind == "work" else group_place(g)
        self.native = b % 2 == s // g.half

    def target(self, place):
        g, b, s = self.g, self.b, self.s
        if self.kind == "home":
            return (b // 2 * 2 + s // g.half, place)
        if self.kind == "work":
            return (b // 2 * 2 + place // g.half, b % 2 * g.half + place % g.half)
        return group_device(g, place)

    @staticmethod
    def senders(g, kind):
        b, s = lax.axis_index("batch"), lax.axis_index("seq")
        if kind == "home":
            places = [(s + k) % g.seq for k in range(1, g.seq)]
            return [
                (b // 2 * 2 + place // g.half, b % 2 * g.half + place % g.half) for place in places
            ]
        places = [(group_place(g) + k) % g.seq for k in range(1, g.seq)]
        if kind == "work":
            return [(b // 2 * 2 + s // g.half, place) for place in places]
        return [group_device(g, place) for place in places]

    def block(self, pair, peer):
        if len(self.src.shape) == 4:
            return self.src.at[pair, peer]
        per = self.src.shape[1] // self.g.seq
        return self.src.at[pair, pl.ds(pl.multiple_of(peer * per, per), per), :]

    def own(self, pair):
        return pltpu.make_async_copy(
            self.block(pair, self.me), self.dst.at[pair, self.me], self.local_sem.at[pair]
        )

    def crossing(self, pair):
        return remote(
            self.block(pair, self.me),
            self.dst.at[pair, self.me],
            self.sends.at[pair, self.g.seq - 1],
            self.local_sem.at[pair],
            swap_partner(self.g),
        )

    def moves(self, pair):
        g = self.g
        made = []
        for k in range(1, g.seq):
            peer = (self.me + k) % g.seq
            made.append(
                remote(
                    self.block(pair, peer),
                    self.dst.at[pair, self.me],
                    self.sends.at[pair, k - 1],
                    self.recvs.at[pair, k - 1],
                    self.target(peer),
                )
            )
        return made

    def either(self, here, there):
        if self.kind == "group":
            here()
            return
        pl.when(self.native)(here)
        pl.when(jnp.logical_not(self.native))(there)

    def start(self, pair):
        self.either(lambda: self.own(pair).start(), lambda: self.crossing(pair).start())
        for copy in self.moves(pair):
            copy.start()

    def arrive(self, pair):
        self.either(lambda: self.own(pair).wait(), lambda: self.crossing(pair).wait_recv())
        for copy in self.moves(pair):
            copy.wait_recv()

    def sent(self, pair):
        self.either(lambda: None, lambda: self.crossing(pair).wait_send())
        for copy in self.moves(pair):
            copy.wait_send()


def exchange_sems(g, pairs):
    return [
        pltpu.SemaphoreType.DMA((pairs, g.seq)),
        pltpu.SemaphoreType.DMA((pairs, g.seq)),
        pltpu.SemaphoreType.DMA((pairs,)),
    ]


LAG = 2
BACK = 2


def unpermute_pair(pair, cols_ref, ret_ref, out_ref):
    tok = out_ref.shape[0]
    head = pl.ds(pl.multiple_of(pair * PAIR, PAIR), PAIR)

    def pick(step, carry):
        start = step * ROWS
        value = ret_ref[pair].reshape(tok, PAIR)
        out_ref[pl.ds(start, ROWS), head] = move_pair(
            lambda i: token_rows(cols_ref, 2 * pair + i, start, ROWS), value
        ).astype(BF16)
        return carry

    lax.fori_loop(0, tok // ROWS, pick, 0)


def forward_kernel(
    g,
    scale,
    factor,
    x_ref,
    wq_ref,
    wk_ref,
    wv_ref,
    bias_ref,
    places_ref,
    cols_ref,
    mask_sent,
    *refs,
):
    parts, wholes = refs[:3], refs[3:6]
    qkv_out, attended_ref, stats_ref = refs[6:9]
    flat, rhs, sent, routed, mixed, ret, mask_routed, entropy = refs[9:17]
    sems = refs[17:]
    pairs = sent.shape[0]
    greet(line_peers(g, ("y", "c")) + Exchange.senders(g, "group"))
    plan = Gather(g, parts, wholes, AXES, PART, lambda unit: ("y", "c"), *sems[:3])
    there = Exchange(g, "group", sent, routed, *sems[3:6])
    back = Exchange(g, "group", mixed, ret, *sems[6:9])
    masks = Exchange(g, "group", mask_sent, mask_routed, *sems[9:12])
    save_sem = sems[12]
    units = len(plan.units)

    def keep(pair):
        return pltpu.make_async_copy(routed.at[pair], qkv_out.at[pair], save_sem.at[pair])

    masks.start(0)
    entropy[...] = jnp.zeros_like(entropy)
    steps = pairs + LAG + BACK

    def step(t, carry):
        @pl.when(t < pairs)
        def _():
            project_pair(
                t,
                x_ref,
                (wq_ref, wk_ref, wv_ref),
                bias_ref,
                places_ref,
                flat,
                rhs,
                sent,
            )
            there.start(t)

        for when in range(steps):
            todo = [
                (unit, level)
                for level in (1, 0)
                for unit in range(units)
                if min(unit + level * WINDOW, steps - 1) == when
            ]
            if todo:

                @pl.when(t == when)
                def _(todo=todo):
                    for unit, level in todo:
                        plan.start(unit, level)

        @pl.when((t >= LAG) & (t < pairs + LAG))
        def _():
            pair = t - LAG
            there.arrive(pair)
            keep(pair).start()
            attend_pair(pair, scale, routed, mixed, entropy)
            back.start(pair)

        @pl.when(t >= LAG + BACK)
        def _():
            pair = t - LAG - BACK
            back.arrive(pair)
            unpermute_pair(pair, cols_ref, ret, attended_ref)

        return carry

    lax.fori_loop(0, steps, step, 0)

    masks.arrive(0)
    sources, per_owner = mask_routed.shape[1:3]
    size = CLUSTER // sources
    blocks = per_owner // size
    spot = lax.broadcasted_iota(jnp.int32, stats_ref.shape, 1) - group_place(g) * blocks
    row = lax.broadcasted_iota(jnp.int32, stats_ref.shape, 0)
    stats = jnp.zeros(stats_ref.shape, F32)
    for cluster in range(blocks):
        mask = gather_rows(mask_routed, (0,), cluster * size, size, slice(None)).astype(F32)
        entropy_sum = jnp.sum(entropy[cluster] * mask) * factor
        count = jnp.sum(mask) * factor
        stats += jnp.where(
            spot == cluster, jnp.where(row == 0, entropy_sum, jnp.where(row == 1, count, 0.0)), 0.0
        )
    stats_ref[...] = stats
    plan.finish()

    def close(pair, carry):
        keep(pair).wait()
        there.sent(pair)
        back.sent(pair)
        return carry

    lax.fori_loop(0, pairs, close, 0)
    masks.sent(0)


def forward(g, scale, factor, x, wq, wk, wv, bias, places, cols, mask, parts):
    tok, width = x.shape
    pairs = width // PAIR
    per_owner = tok // g.seq
    clusters = tok // CLUSTER
    shape = jax.ShapeDtypeStruct
    any_space, vmem = pl.BlockSpec(memory_space=pl.ANY), pl.BlockSpec(memory_space=pltpu.VMEM)
    lead = tuple(sizes(g)[axis] for axis in AXES)
    made = pl.pallas_call(
        functools.partial(forward_kernel, g, scale, factor),
        out_shape=[
            *(shape((*lead, *item.shape[-2:]), BF16) for item in parts),
            shape((pairs, g.seq, per_owner, 3 * PAIR), BF16),
            shape((tok, width), BF16),
            shape((8, PAIR), F32),
        ],
        in_specs=[vmem] * 7 + [any_space] * 4,
        out_specs=[any_space] * 4 + [vmem, vmem],
        scratch_shapes=[
            pltpu.VMEM((width, 3 * PAIR), BF16),
            pltpu.VMEM((tok, 3 * PAIR), BF16),
            pltpu.VMEM((pairs, tok, 3 * PAIR), BF16),
            pltpu.VMEM((pairs, g.seq, per_owner, 3 * PAIR), BF16),
            pltpu.VMEM((pairs, g.seq, per_owner, PAIR), BF16),
            pltpu.VMEM((pairs, g.seq, per_owner, PAIR), BF16),
            pltpu.VMEM((1, g.seq, per_owner, PAIR), BF16),
            pltpu.VMEM((clusters, CLUSTER, PAIR), F32),
            *Gather.sems(g, [item.shape for item in parts]),
            *exchange_sems(g, pairs),
            *exchange_sems(g, pairs),
            *exchange_sems(g, 1),
            pltpu.SemaphoreType.DMA((pairs,)),
        ],
        compiler_params=pltpu.CompilerParams(
            collective_id=2, has_side_effects=True, vmem_limit_bytes=VMEM_LIMIT
        ),
        name="forward",
    )(x, wq, wk, wv, bias, places, cols, mask, *parts)
    return made[:3], made[3:]


def cluster_scores(q, k, scale):
    return dot_nt(q, k) * scale


def attend_back_pair(slot, pair, scale, qkv_ref, grad_ref, out_ref):
    _, sources, per_owner, _ = qkv_ref.shape
    size = CLUSTER // sources
    clusters = per_owner // size
    for cluster in range(clusters):
        q, k, v = unpack(
            *(
                gather_rows(qkv_ref, (slot,), cluster * size, size, slice(i * PAIR, (i + 1) * PAIR))
                for i in range(3)
            )
        )
        grad = gather_rows(grad_ref, (slot,), cluster * size, size, slice(None))
        q2, g2 = split_pair(q), split_pair(grad)
        scores = cluster_scores(q2, k, scale)
        top = jnp.max(scores, axis=1, keepdims=True)
        weights = jnp.exp(scores - top)
        probs = weights / jnp.sum(weights, axis=1, keepdims=True)
        low = probs.astype(BF16)
        d_value = dot_tn(low, g2)
        d_prob = dot_nt(g2, v)
        inner = jnp.sum(probs * d_prob, axis=1, keepdims=True)
        d_score = (probs * (d_prob - inner)).astype(BF16)
        d_query = (
            dot(jnp.concatenate([d_score[:CLUSTER], d_score[CLUSTER:]], axis=1), split_pair(k))
            * scale
        )
        d_key = dot_tn(d_score, q2) * scale
        for i, value in enumerate(pack(d_query, d_key, d_value)):
            out_ref[
                pair, :, cluster * size : (cluster + 1) * size, i * PAIR : (i + 1) * PAIR
            ] = spread_rows(value, sources, BF16)


INV_SQRT2 = 0.7071067811865476
INV_SQRT_2PI = 0.3989422804014327


def norm_parts(value):
    centred = value - jnp.mean(value, axis=1, keepdims=True)
    rate = lax.rsqrt(jnp.mean(centred * centred, axis=1, keepdims=True) + EPSILON)
    return centred * rate, rate


def norm_back(grad, gain, normed, rate):
    inner = grad * gain
    return rate * (
        inner
        - jnp.mean(inner, axis=1, keepdims=True)
        - normed * jnp.mean(inner * normed, axis=1, keepdims=True)
    )


TILE = 512
COLS = 512
PART_ROWS = 256


def column_sum(value):
    return jnp.sum(value, axis=0, keepdims=True)


def middle_forward(x_ref, attended, w_refs, vec_ref, up_bias_ref, out_ref, kept):
    wo_ref, up_ref, down_ref = w_refs
    hidden_all, act_all, dup_all, n1_all, n2_all, r1_all, r2_all = kept
    tok, width = x_ref.shape
    wide = up_ref.shape[1]
    bo, g1, s1, bd, g2, s2 = (vec_ref[i : i + 1, :] for i in range(6))

    def tile(step, carry):
        rows = pl.ds(step * TILE, TILE)
        branch = dot(attended[rows, :], wo_ref[...]) + bo
        n1, r1 = norm_parts(x_ref[rows, :].astype(F32) + branch)
        n1_all[rows, :] = n1
        r1_all[rows, :] = r1
        hidden = (n1 * g1 + s1).astype(BF16)
        hidden_all[rows, :] = hidden
        ffn = hidden.astype(F32) + bd
        for col in range(0, wide, COLS):
            to = slice(col, col + COLS)
            pre = dot(hidden, up_ref[:, to]) + up_bias_ref[0:1, to]
            cdf = 0.5 * (1.0 + lax.erf(pre * INV_SQRT2))
            act = (pre * cdf).astype(BF16)
            dup_all[rows, to] = (cdf + pre * (jnp.exp(-0.5 * pre * pre) * INV_SQRT_2PI)).astype(BF16)
            act_all[rows, to] = act
            ffn += dot(act, down_ref[to, :])
        n2, r2 = norm_parts(ffn)
        n2_all[rows, :] = n2
        r2_all[rows, :] = r2
        out_ref[rows, :] = (n2 * g2 + s2).astype(BF16)
        return carry

    lax.fori_loop(0, tok // TILE, tile, 0)


def middle_backward(grad_ref, cols_ref, heads, w_refs, vec_ref, kept, made):
    wo_ref, up_ref, down_ref = w_refs
    hidden_all, act_all, dup_all, n1_all, n2_all, r1_all, r2_all = kept
    dffn_all, dmid_ref, datt_all, gvec_ref, g_upb_ref = made
    tok, width = dmid_ref.shape
    wide = up_ref.shape[1]
    gvec_ref[...] = jnp.zeros_like(gvec_ref)
    g_upb_ref[...] = jnp.zeros_like(g_upb_ref)
    g1, g2 = vec_ref[1:2, :], vec_ref[4:5, :]

    def tile(step, carry):
        rows = pl.ds(step * TILE, TILE)
        mask = cols_ref[rows, heads : heads + 1].astype(F32)
        gout = grad_ref[rows, :].astype(F32) * mask
        n2 = n2_all[rows, :]
        gvec_ref[4:5, :] += column_sum(gout * n2)
        gvec_ref[5:6, :] += column_sum(gout)
        d_pre = norm_back(gout, g2, n2, r2_all[rows, :])
        d_ffn = d_pre.astype(BF16)
        dffn_all[rows, :] = d_ffn
        gvec_ref[3:4, :] += column_sum(d_ffn.astype(F32))
        d_hidden = d_pre
        for col in range(0, wide, COLS):
            to = slice(col, col + COLS)
            d_up = (dot_nt(d_ffn, down_ref[to, :]) * dup_all[rows, to].astype(F32)).astype(BF16)
            dup_all[rows, to] = d_up
            g_upb_ref[0:1, to] += column_sum(d_up.astype(F32))
            d_hidden += dot_nt(d_up, up_ref[:, to])
        n1 = n1_all[rows, :]
        gvec_ref[1:2, :] += column_sum(d_hidden * n1)
        gvec_ref[2:3, :] += column_sum(d_hidden)
        d_mid = norm_back(d_hidden, g1, n1, r1_all[rows, :])
        d_branch = d_mid.astype(BF16)
        dmid_ref[rows, :] = d_branch
        gvec_ref[0:1, :] += column_sum(d_branch.astype(F32))
        datt_all[rows, :] = dot_nt(d_branch, wo_ref[...]).astype(BF16)
        return carry

    lax.fori_loop(0, tok // TILE, tile, 0)


def permute_pair(pair, places_ref, datt_all, out_ref):
    tok = datt_all.shape[0]
    to = slice(pair * PAIR, (pair + 1) * PAIR)

    def permute(step, carry):
        start = step * ROWS
        out_ref[pair, pl.ds(start, ROWS), :] = move_pair(
            lambda i: place_rows(places_ref, 2 * pair + i, start, ROWS), datt_all[:, to]
        ).astype(BF16)
        return carry

    lax.fori_loop(0, tok // ROWS, permute, 0)


def middle_weights(attended, dmid_ref, kept, dffn_all, grads):
    hidden_all, act_all, dup_all = kept[:3]
    g_out_ref, g_up_ref, g_down_ref = grads
    wide, width = act_all.shape[1], hidden_all.shape[1]

    def weights(step, carry):
        to = pl.ds(pl.multiple_of(step * PART_ROWS, PART_ROWS), PART_ROWS)
        g_down_ref[to, :] = dot_tn(act_all[:, to], dffn_all[...]).astype(BF16)
        g_up_ref[:, to] = dot_tn(hidden_all[...], dup_all[:, to]).astype(BF16)
        return carry

    lax.fori_loop(0, wide // PART_ROWS, weights, 0)

    def out_weights(step, carry):
        to = pl.ds(pl.multiple_of(step * PART_ROWS, PART_ROWS), PART_ROWS)
        g_out_ref[:, to] = dot_tn(attended[...], dmid_ref[:, to]).astype(BF16)
        return carry

    lax.fori_loop(0, width // PART_ROWS, out_weights, 0)


def middle_kernel(
    g,
    x_ref,
    attended,
    places_ref,
    cols_ref,
    wo_ref,
    up_ref,
    down_ref,
    vec_ref,
    up_bias_ref,
    grad_ref,
    out_ref,
    dmid_ref,
    datt_ref,
    g_out_ref,
    g_up_ref,
    g_down_ref,
    gvec_ref,
    g_upb_ref,
    *refs,
):
    kept, sems = refs[:7], refs[12:]
    dffn_all, datt_all, work_out, work_grad, datt_sent = refs[7:12]
    pairs = datt_sent.shape[0]
    greet(Exchange.senders(g, "group") + [swap_partner(g)])
    there = Exchange(g, "group", datt_sent, datt_ref, *sems[:3])
    w_refs = (wo_ref, up_ref, down_ref)
    swap = Swap(g, grad_ref, work_grad, *sems[5:7])
    swap_out = Swap(g, work_out, out_ref, *sems[3:5])
    swap.start()
    middle_forward(x_ref, attended, w_refs, vec_ref, up_bias_ref, work_out, kept)
    swap.wait()
    swap_out.start()
    made = (dffn_all, dmid_ref, datt_all, gvec_ref, g_upb_ref)
    middle_backward(work_grad, cols_ref, 2 * pairs, w_refs, vec_ref, kept, made)
    for pair in range(pairs):
        permute_pair(pair, places_ref, datt_all, datt_sent)
        there.start(pair)
    middle_weights(attended, dmid_ref, kept, dffn_all, (g_out_ref, g_up_ref, g_down_ref))
    for pair in range(pairs):
        there.arrive(pair)
        there.sent(pair)
    swap_out.wait()


def middle_scratch(tok, width, wide):
    return [
        pltpu.VMEM((tok, width), BF16),
        pltpu.VMEM((tok, wide), BF16),
        pltpu.VMEM((tok, wide), BF16),
        pltpu.VMEM((tok, width), F32),
        pltpu.VMEM((tok, width), F32),
        pltpu.VMEM((tok, 1), F32),
        pltpu.VMEM((tok, 1), F32),
        pltpu.VMEM((tok, width), BF16),
        pltpu.VMEM((tok, width), BF16),
        pltpu.VMEM((tok, width), BF16),
        pltpu.VMEM((tok, width), BF16),
        pltpu.VMEM((width // PAIR, tok, PAIR), BF16),
    ]


def middle(g, *args):
    x, up = args[0], args[5]
    tok, width = x.shape
    wide = up.shape[1]
    pairs = width // PAIR
    shape = jax.ShapeDtypeStruct
    any_space, vmem = pl.BlockSpec(memory_space=pl.ANY), pl.BlockSpec(memory_space=pltpu.VMEM)
    return pl.pallas_call(
        functools.partial(middle_kernel, g),
        out_shape=[
            shape((tok, width), BF16),
            shape((tok, width), BF16),
            shape((pairs, g.seq, tok // g.seq, PAIR), BF16),
            shape((width, width), BF16),
            shape((width, wide), BF16),
            shape((wide, width), BF16),
            shape((8, width), F32),
            shape((8, wide), F32),
        ],
        in_specs=[vmem] * (len(args) - 1) + [any_space],
        out_specs=[any_space, vmem, any_space] + [vmem] * 5,
        scratch_shapes=[
            *middle_scratch(tok, width, wide),
            *exchange_sems(g, pairs),
            *Swap.sems(),
            *Swap.sems(),
        ],
        compiler_params=pltpu.CompilerParams(
            collective_id=3, has_side_effects=True, vmem_limit_bytes=VMEM_LIMIT
        ),
        name="middle",
    )(*args)


Y_FIRST = ("c", "y", "x", "l", "h")
TURNS = [("c", "l", "x", "y", "h"), ("c", "x", "l", "y", "h"), ("c", "y", "l", "x", "h"), Y_FIRST]


def step_of(unit, level):
    return unit // 2 + level - (level == 1)


def backward_kernel(
    g,
    scale,
    n,
    x_ref,
    wq_ref,
    wk_ref,
    wv_ref,
    dmid_ref,
    cols_ref,
    *refs,
):
    terms, refs = refs[:n], refs[n:]
    qkv_ref, grad_ref, gtok_ref, gq_ref, gk_ref, gv_ref, gvec_ref = refs[:7]
    sums, refs = refs[7 : 7 + n], refs[7 + n :]
    qkv_slots, grad_slots, sent, home, rhs, local, flat, total = refs[:8]
    bufs, refs = refs[8 : 8 + 5 * n], refs[8 + 5 * n :]
    rs_send, rs_recv, ex_send, ex_recv, ex_local, load_sem = refs
    pairs = sent.shape[0]
    tok, width = x_ref.shape
    greet(line_peers(g) + Exchange.senders(g, "group"))
    plan = Scatter(g, terms, bufs, [Y_FIRST] * n, rs_send, rs_recv)
    there = Exchange(g, "group", sent, home, ex_send, ex_recv, ex_local)
    units = len(plan.units)

    def loads(pair):
        slot = pair % 2
        return (
            pltpu.make_async_copy(qkv_ref.at[pair], qkv_slots.at[slot], load_sem.at[0, slot]),
            pltpu.make_async_copy(grad_ref.at[pair], grad_slots.at[slot], load_sem.at[1, slot]),
        )

    for copy in loads(0):
        copy.start()
    gvec_ref[...] = jnp.zeros_like(gvec_ref)
    total[...] = dmid_ref[...].astype(F32)
    for unit in range(units):
        plan.step(unit, 0)

    def step(t, carry):
        @pl.when(t < pairs)
        def _():
            for copy in loads(t):
                copy.wait()

            @pl.when(t + 1 < pairs)
            def _():
                for copy in loads(t + 1):
                    copy.start()

            attend_back_pair(t % 2, t, scale, qkv_slots, grad_slots, sent)
            there.start(t)

        for when in range(pairs + LAG):
            todo = [
                (unit, level)
                for level in range(1, 6)
                for unit in range(units)
                if step_of(unit, level) == when
            ]
            if todo:

                @pl.when(t == when)
                def _(todo=todo):
                    for unit, level in todo:
                        plan.step(unit, level, sums)

        @pl.when(t >= LAG)
        def _():
            pair = t - LAG
            head = pl.ds(pl.multiple_of(pair * PAIR, PAIR), PAIR)
            there.arrive(pair)
            pair_weights(pair, (wq_ref, wk_ref, wv_ref), flat)

            def gather_home(owner, carry):
                per = tok // g.seq
                rhs[pl.ds(pl.multiple_of(owner * per, per), per), :] = home[pair, owner]
                return carry

            lax.fori_loop(0, g.seq, gather_home, 0)

            def unpermute(k, carry):
                start = k * ROWS
                rows = pl.ds(start, ROWS)
                made = move_rows(lambda i: token_rows(cols_ref, 2 * pair + i, start, ROWS), rhs)
                sums = [column_sum(value) for value in made]
                low = head_lanes(sums[0].shape)
                gvec_ref[0:1, head] += jnp.where(low, sums[0], sums[1])
                gvec_ref[2:3, head] += jnp.where(low, sums[1], sums[2])
                for part, value in enumerate(made):
                    local[rows, part * PAIR : (part + 1) * PAIR] = value.astype(BF16)
                total[rows, :] += dot_nt(local[rows, :], flat[...])
                return carry

            lax.fori_loop(0, tok // ROWS, unpermute, 0)

            def weights(k, carry):
                rows = pl.ds(pl.multiple_of(k * PART_ROWS, PART_ROWS), PART_ROWS)
                value = dot_tn(x_ref[:, rows], local[...])
                made = unpack(*(value[:, i * PAIR : (i + 1) * PAIR] for i in range(3)))
                for part, g_ref in enumerate((gq_ref, gk_ref, gv_ref)):
                    g_ref[rows, head] = made[part].astype(BF16)
                return carry

            lax.fori_loop(0, width // PART_ROWS, weights, 0)

        return carry

    lax.fori_loop(0, pairs + LAG, step, 0)
    gtok_ref[...] = total[...].astype(BF16)
    for when in range(pairs + LAG, step_of(units - 1, 5) + 1):
        for level in range(1, 6):
            for unit in range(units):
                if step_of(unit, level) == when:
                    plan.step(unit, level, sums)
    plan.sent()

    def close(pair, carry):
        there.sent(pair)
        return carry

    lax.fori_loop(0, pairs, close, 0)


def backward(g, scale, x, wq, wk, wv, d_mid, cols, terms, qkv, grad):
    tok, width = x.shape
    pairs = width // PAIR
    n = len(terms)
    shape = jax.ShapeDtypeStruct
    any_space, vmem = pl.BlockSpec(memory_space=pl.ANY), pl.BlockSpec(memory_space=pltpu.VMEM)
    dma = pltpu.SemaphoreType.DMA
    made = pl.pallas_call(
        functools.partial(backward_kernel, g, scale, n),
        out_shape=[
            shape((tok, width), BF16),
            *([shape((width, width), BF16)] * 3),
            shape((8, width), F32),
            *(shape(item.shape[-2:], F32) for item in terms),
        ],
        in_specs=[vmem] * (6 + n) + [any_space] * 2,
        out_specs=[vmem] * (5 + n),
        scratch_shapes=[
            pltpu.VMEM((2, *qkv.shape[1:]), BF16),
            pltpu.VMEM((2, *grad.shape[1:]), BF16),
            pltpu.VMEM(qkv.shape, BF16),
            pltpu.VMEM(qkv.shape, BF16),
            pltpu.VMEM((tok, 3 * PAIR), BF16),
            pltpu.VMEM((tok, 3 * PAIR), BF16),
            pltpu.VMEM((width, 3 * PAIR), BF16),
            pltpu.VMEM((tok, width), F32),
            *Scatter.scratch(g, [item.shape for item in terms], [Y_FIRST] * n),
            *exchange_sems(g, pairs),
            dma((2, 2)),
        ],
        compiler_params=pltpu.CompilerParams(
            collective_id=5, has_side_effects=True, vmem_limit_bytes=VMEM_LIMIT
        ),
        name="backward",
    )(x, wq, wk, wv, d_mid, cols, *terms, qkv, grad)
    return made[0], made[1:4], made[4], made[5 : 5 + n]


def close_kernel(g, n, small_ref, *refs):
    terms, gtok_ref, refs = refs[:n], refs[n], refs[n + 1 :]
    small_out, sums, gtok_home, refs = refs[0], refs[1 : 1 + n], refs[1 + n], refs[2 + n :]
    bufs, refs = refs[: 5 * n], refs[5 * n :]
    rs_send, rs_recv, small_bufs, refs = refs[0], refs[1], refs[2:7], refs[7:]
    small_send, small_recv, swap_send, swap_recv = refs
    greet(line_peers(g) + [swap_partner(g)])
    plan = Scatter(g, terms, bufs, TURNS, rs_send, rs_recv)
    swap = Swap(g, gtok_ref, gtok_home, swap_send, swap_recv)
    small = Total(g, small_ref, small_bufs, small_send, small_recv)
    units = len(plan.units)
    for unit in range(units):
        plan.step(unit, 0)
    small.start(0, small_ref[...])
    swap.start()
    for level in range(1, 6):
        for unit in range(units):
            plan.step(unit, level, sums)
        value = small.take(level - 1)
        if level < len(AXES):
            small.start(level, value)
        else:
            small_out[...] = value
    swap.wait()
    plan.sent()
    small.sent()


def close_call(g, small, terms, gtok):
    n = len(terms)
    shape = jax.ShapeDtypeStruct
    any_space, vmem = pl.BlockSpec(memory_space=pl.ANY), pl.BlockSpec(memory_space=pltpu.VMEM)
    made = pl.pallas_call(
        functools.partial(close_kernel, g, n),
        out_shape=[
            shape(small.shape, F32),
            *(shape(item.shape[-2:], F32) for item in terms),
            shape(gtok.shape, BF16),
        ],
        in_specs=[vmem] * (1 + n) + [any_space],
        out_specs=[vmem] * (1 + n) + [any_space],
        scratch_shapes=[
            *Scatter.scratch(g, [item.shape for item in terms], TURNS),
            *Total.scratch(g, small.shape),
            *Swap.sems(),
        ],
        compiler_params=pltpu.CompilerParams(
            collective_id=6, has_side_effects=True, vmem_limit_bytes=VMEM_LIMIT
        ),
        name="close",
    )(small, *terms, gtok)
    return made[0], made[1:-1], made[-1]


def body(
    g,
    tokens,
    cluster_slot,
    loss_mask,
    out_grad,
    query_weight,
    key_weight,
    value_weight,
    output_weight,
    query_bias,
    value_bias,
    output_bias,
    first_gain,
    first_shift,
    up_weight,
    up_bias,
    down_weight,
    down_bias,
    second_gain,
    second_shift,
):
    tok, width = tokens.shape[1:]
    heads = cluster_slot.shape[1]
    pairs = heads // 2
    wide = up_weight.shape[1]
    per_owner = tok // g.seq
    scale = (width // heads) ** -0.5

    slots = cluster_slot[0]
    places = slots // tok * per_owner + slots % tok // g.seq
    table = jnp.concatenate(
        [places, loss_mask, jnp.zeros((16 - heads - 1, tok), jnp.int32)], axis=0
    )
    vectors = (
        query_bias,
        value_bias,
        output_bias,
        first_gain,
        first_shift,
        down_bias,
        second_gain,
        second_shift,
    )
    count = query_bias.shape[0]
    lines = (*vectors, up_bias)
    line = lax.broadcasted_iota(jnp.int32, (16, PAIR), 0)
    packed = jnp.zeros((16, PAIR), BF16)
    for index, value in enumerate(lines):
        packed = jnp.where(line == index, jnp.pad(value, (0, PAIR - value.shape[0]))[None], packed)
    gathered, partial, (work_x, work_table, work_mask) = open_call(
        g,
        [packed, query_weight, key_weight, value_weight],
        [output_weight, up_weight, down_weight],
        [tokens[0], table],
    )
    work_cols = work_table.T

    def whole(item):
        return item.reshape(g.n * item.shape[-2], item.shape[-1])

    wq, wk, wv = (whole(item) for item in gathered[1:])
    flat = gathered[0].reshape(g.n, 16, PAIR).astype(F32)
    rows = flat[:, :8, :count].transpose(1, 0, 2).reshape(8, width)
    up_row = flat[:, 8, : up_bias.shape[0]].reshape(1, wide)
    qkv_bias = jnp.stack([rows[0], jnp.zeros((width,), F32), rows[1]])

    spread, (qkv, attended, stats) = forward(
        g,
        scale,
        1.0 / (heads * CLUSTER * g.batch),
        work_x,
        wq,
        wk,
        wv,
        qkv_bias,
        work_table,
        work_cols,
        work_mask.reshape(1, tok, PAIR),
        partial,
    )
    wo, up, down = (whole(item) for item in spread)

    out, d_mid, routed, g_out, g_up, g_down, g_rows, g_upb = middle(
        g, work_x, attended, work_table, work_cols, wo, up, down, rows[2:], up_row, out_grad[0]
    )

    def parts(item):
        rows, cols = item.shape[0] // g.n, item.shape[1]
        if rows % 8:
            rows, cols = rows * cols // PAIR, PAIR
        return item.reshape(*(sizes(g)[axis] for axis in AXES), rows, cols)

    grad_tokens, g_attn, g_bias, s_ffn = backward(
        g,
        scale,
        work_x,
        wq,
        wk,
        wv,
        d_mid,
        work_cols,
        [parts(g_up), parts(g_out)],
        qkv,
        routed,
    )
    lines = wide // width
    small = jnp.concatenate(
        [
            g_bias[0:1],
            g_bias[2:3],
            g_rows[:6],
            g_upb[0].reshape(lines, width),
            jnp.pad(stats[:2], ((0, 0), (0, width - stats.shape[1]))),
            jnp.zeros((6 - lines, width), F32),
        ],
        axis=0,
    )
    small, s_attn, grad_tokens = close_call(
        g, small, [parts(item) for item in (*g_attn, g_down)], grad_tokens
    )

    b, s = lax.axis_index("batch"), lax.axis_index("seq")
    here = b * g.seq + s
    mine = lax.dynamic_slice(small, (0, here * count), (8, count))
    wide_count = wide // g.n
    gu = lax.dynamic_slice(small[8 : 8 + lines].reshape(wide), (here * wide_count,), (wide_count,))
    blocks = tok // CLUSTER
    cluster_stats = lax.dynamic_slice(small, (8 + lines, s * blocks), (2, blocks))
    s_up, s_out, s_query, s_key, s_value, s_down = (
        item.reshape(local.shape)
        for item, local in zip(
            (*s_ffn, *s_attn),
            (up_weight, output_weight, query_weight, key_weight, value_weight, down_weight),
        )
    )
    gq, gv, go, gg1, gs1, gd, gg2, gs2 = (mine[i] for i in range(8))
    return (
        out[None],
        grad_tokens[None],
        s_query,
        s_key,
        s_value,
        s_out,
        gq,
        gv,
        go,
        gg1,
        gs1,
        s_up,
        gu,
        s_down,
        gd,
        gg2,
        gs2,
        cluster_stats,
    )


def solution(mesh):
    g = Grid(mesh)
    tokens, rows, flat = P("batch", "seq", None), P(("batch", "seq"), None), P(("batch", "seq"))
    return jax.shard_map(
        functools.partial(body, g),
        mesh=mesh,
        in_specs=(
            tokens,
            P("batch", None, "seq"),
            P("batch", "seq"),
            tokens,
            *([rows] * 4),
            *([flat] * 5),
            rows,
            flat,
            rows,
            *([flat] * 3),
        ),
        out_specs=(
            tokens,
            tokens,
            *([rows] * 4),
            *([flat] * 5),
            rows,
            flat,
            rows,
            *([flat] * 3),
            P(None, "seq"),
        ),
        check_vma=False,
    )
```

time: 479 us -> 461 us (0.962); the launches traced: 478 us -> 455 us
  Pallas kernels: 448 us -> 424 us
    pallas_call x1, Pallas kernels: 126 us -> 95.2 us  [forward(): pl.pallas_call(functools.partial(forward_kernel, g, scale, factor), out_s...]
    pallas_call x1, Pallas kernels: 60.9 us -> 71.8 us  [open_call(): pl.pallas_call(functools.partial(open_kernel, g, n, m), out_shape=[*outs,...]
    pallas_call x1, Pallas kernels: 55.1 us -> 63.5 us  [close_call(): pl.pallas_call(functools.partial(close_kernel, g, n), out_shape=[shape(sm...]
    pallas_call x1, Pallas kernels: 120 us -> 114 us  [backward(): pl.pallas_call(functools.partial(backward_kernel, g, scale, n), out_shape...]
    concatenate x1 -> x0, local copies, waits for them, and re-layouts: 6.1 us -> none  [body(): packed = jnp.concatenate([*vectors, up_bias])]
    pad x0 -> x9, local copies, waits for them, and re-layouts: none -> 5.94 us  [body(): jnp.pad(value, (0, PAIR - value.shape[0]))[None]]
    pallas_call x1, Pallas kernels: 85.6 us -> 80.1 us  [middle(): pl.pallas_call(functools.partial(middle_kernel, g), out_shape=[shape((tok...]
where the time goes in v4:
time: 461 us; the launch traced here: 455 us
  Pallas kernels  424 us (92%)
  local copies, waits for them, and re-layouts  24.3 us (5%)
    pallas_call x1, Pallas kernels, backward(): pl.pallas_call(functools.partial(backward_kernel, g, scale, n), out_shape...  114 us
    pallas_call x1, Pallas kernels, forward(): pl.pallas_call(functools.partial(forward_kernel, g, scale, factor), out_s...  95.2 us
    pallas_call x1, Pallas kernels, middle(): pl.pallas_call(functools.partial(middle_kernel, g), out_shape=[shape((tok...  80.1 us
    pallas_call x1, Pallas kernels, open_call(): pl.pallas_call(functools.partial(open_kernel, g, n, m), out_shape=[*outs,...  71.8 us
    pallas_call x1, Pallas kernels, close_call(): pl.pallas_call(functools.partial(close_kernel, g, n), out_shape=[shape(sm...  63.5 us

profile of v4, /device:TPU:0, one launch (start us, length us, event | category | flops | bytes accessed | tf_op | source)
XLA Modules:
  0.0 454.5 jit_solution(3283222733097510126)
XLA Ops:
  0.7 0.7 pad.33
  1.4 0.7 pad.34
  2.0 0.7 pad.35
  2.7 0.7 pad.36
  3.4 0.7 pad.37
  4.0 0.7 pad.38
  4.7 0.7 pad.39
  5.3 0.7 pad.40
  6.0 0.7 pad.41
  6.7 0.7 select_select_fusion.refs_0_
  7.3 0.9 fusion.1
  8.3 0.1 pad.48.clone
  8.3 1.4 add_add_fusion.refs_8_
  9.7 71.8 %open.1 = (bf16[2,2,2,2,2,16,128]{6,5,4,3,2,1,0:T(8,128)(2,1)}, bf16[2,2,2,2,2,24,768]{6,5,4,3,2,1,0:T(8,128)(2,1)}, bf16[2,2,2,2,2,24,768]{6,5,4,3,2,1,0:T(8,12...) custom-call(bf16[16,128]{1,0:T(8,128)(2,1)} %select_select_fusion.re, ...), custom_call_target="tpu_custom_call" | custom-call | tf_op jit(solution)/shard_map/open/pallas_call | solution.py:287
  81.6 0.9 bitcast_convert_fusion
  82.6 0.1 slice.68
  82.7 0.1 slice.70
  82.7 0.1 pad.44.clone
  82.8 0.7 pad_maximum_fusion.bias_ref
  83.5 1.8 copy.41
  85.3 95.2 %forward.1 = (bf16[2,2,2,2,2,24,768]{6,5,4,3,2,1,0:T(8,128)(2,1)}, bf16[2,2,2,2,2,24,3072]{6,5,4,3,2,1,0:T(8,128)(2,1)}, bf16[2,2,2,2,2,96,768]{6,5,4,3,2,1,0:T(...) custom-call(bf16[1024,768]{1,0:T(8,128)(2,1)} %get-tuple-element.55.x_ref, ...), custom_call_target="tpu_custom_call" | custom-call | tf_op jit(solution)/shard_map/forward/pallas_call | solution.py:847
  180.6 0.7 slice.72.vec_ref
  181.3 0.7 reshape_squeeze.6.up_bias_ref
  182.0 80.1 %middle.1 = (bf16[1024,768]{1,0:T(8,128)(2,1)}, bf16[1024,768]{1,0:T(8,128)(2,1)}, bf16[6,8,128,128]{3,2,1,0:T(8,128)(2,1)}, bf16[768,768]{1,0:T(8,128)(2,1)}, b...) custom-call(bf16[1024,768]{1,0:T(8,128)(2,1)} %get-tuple-element.55.x_ref, ...), custom_call_target="tpu_custom_call" | custom-call | tf_op jit(solution)/shard_map/middle/pallas_call | solution.py:1124
  262.2 0.0 copy-start.8
  262.2 113.6 %backward.1 = (bf16[1024,768]{1,0:T(8,128)(2,1)}, bf16[768,768]{1,0:T(8,128)(2,1)}, bf16[768,768]{1,0:T(8,128)(2,1)}, bf16[768,768]{1,0:T(8,128)(2,1)}, f32[8,76...) custom-call(bf16[1024,768]{1,0:T(8,128)(2,1)} %get-tuple-element.55.x_ref, bf16[768,768]{1,0:T(8,128)(2,1)} %bitcast.65, ...), custom_call_target="tpu_custom_call" | custom-call | tf_op jit(solution)/shard_map/backward/pallas_call | solution.py:1290
  375.7 0.8 fusion.8
  376.6 0.9 slice_reduce_fusion
  377.5 0.7 slice.78
  378.2 0.0 copy-done.8
  378.2 1.3 concatenate.7.small_ref
  379.5 0.0 copy-start
  379.5 63.5 %close.1 = (f32[16,768]{1,0:T(8,128)}, f32[24,768]{1,0:T(8,128)}, f32[24,768]{1,0:T(8,128)}, f32[24,768]{1,0:T(8,128)}, f32[96,768]{1,0:T(8,128)}, /*index=5*/bf16[1024,768]{1,0:T(8,128)(2,1)}) custom-call(f32[16,768]{1,0:T(8,128)} %concatenate.7.small_ref, bf16[2,2,2,2,2,24,768]{6,5,4,3,2,1,0:T(8,128)(2,1)} %bitcast.78, ...), custom_call_target="tpu_custom_call" | custom-call | tf_op jit(solution)/shard_map/close/pallas_call | solution.py:1353
  443.0 0.7 slice.84
  443.8 0.6 dynamic_slice.10
  444.4 0.8 constant_dynamic-slice_fusion.1
  445.1 0.5 slice_bitcast_fusion
  445.7 1.3 constant_dynamic-slice_fusion
  447.0 0.0 copy-done
  447.0 0.0 copy-start.1
  447.0 1.1 copy.71
  448.1 0.8 copy-done.1
  449.0 0.0 copy-start.7
  449.0 0.0 copy-start.6
  449.0 0.0 copy-start.5
  449.0 0.0 copy-start.4
  449.0 0.0 copy-start.2
  449.0 0.0 copy-start.3
  449.0 1.1 copy.72
  450.1 0.0 copy-done.7
  450.1 0.6 copy.73
  450.8 0.0 copy-done.6
  450.8 0.6 copy.74
  451.4 0.0 copy-done.5
  451.4 0.6 copy.75
  452.0 0.0 copy-done.4
  452.0 0.6 copy.76
  452.7 0.0 copy-done.2
  452.7 0.7 copy.77
  453.4 0.0 copy-done.3
  453.4 0.7 copy.78
  (15 shorter events, 0.1 us)
Async XLA Ops:
  262.2 116.0 %copy-start.8 = (f32[8,768]{1,0:T(8,128)S(1)}, f32[8,768]{1,0:T(8,128)}, u32[]{:S(2)}) copy-start(f32[8,768]{1,0:T(8,128)} %get-tuple-element.76) | copy-start | bytes 73732
  379.5 67.5 %copy-start = (bf16[1024,768]{1,0:T(8,128)(2,1)S(1)}, bf16[1024,768]{1,0:T(8,128)(2,1)}, u32[]{:S(2)}) copy-start(bf16[1024,768]{1,0:T(8,128)(2,1)} %get-tuple-element.69) | copy-start | bytes 4718596
  447.0 2.0 copy-start.1
  449.0 1.2 copy-start.7
  449.0 1.8 copy-start.6
  449.0 2.4 copy-start.5
  449.0 3.1 copy-start.4
  449.0 3.7 copy-start.2
  449.0 4.4 copy-start.3

commit v5 on v4

--- a/solution.py
+++ b/solution.py
@@ -287,8 +287,8 @@
     made = pl.pallas_call(
         functools.partial(open_kernel, g, n, m),
         out_shape=[*outs, shape((swapped[0].shape[0], PAIR), BF16)],
-        in_specs=[any_space] * len(outs),
-        out_specs=[any_space] * (len(outs) - 1) + [vmem] * 2,
+        in_specs=[vmem] * (n + m) + [any_space, vmem],
+        out_specs=[any_space] * (n + m) + [vmem] * 3,
         scratch_shapes=[
             *Gather.sems(g, [item.shape for item in whole]),
             *Gather.sems(g, [item.shape for item in part]),
@@ -852,7 +852,7 @@
             shape((tok, width), BF16),
             shape((8, PAIR), F32),
         ],
-        in_specs=[vmem] * 7 + [any_space] * 4,
+        in_specs=[vmem] * 11,
         out_specs=[any_space] * 4 + [vmem, vmem],
         scratch_shapes=[
             pltpu.VMEM((width, 3 * PAIR), BF16),
@@ -1318,20 +1318,61 @@
     return made[0], made[1:4], made[4], made[5 : 5 + n]
 
 
-def close_kernel(g, n, small_ref, *refs):
+def small_lines(bias_ref, rows_ref, up_ref, stats_ref):
+    width = bias_ref.shape[1]
+    lines = up_ref.shape[1] // width
+    stats = jnp.concatenate(
+        [stats_ref[0:2, :], jnp.zeros((2, width - stats_ref.shape[1]), F32)], axis=1
+    )
+    return jnp.concatenate(
+        [
+            bias_ref[0:1, :],
+            bias_ref[2:3, :],
+            rows_ref[0:6, :],
+            *(up_ref[0:1, i * width : (i + 1) * width] for i in range(lines)),
+            stats,
+            jnp.zeros((6 - lines, width), F32),
+        ],
+        axis=0,
+    )
+
+
+def own_lines(g, held, outs):
+    width = held.shape[1]
+    b, s = lax.axis_index("batch"), lax.axis_index("seq")
+    here = b * g.seq + s
+    vectors, (up_out, stats_out) = outs[:8], outs[8:]
+    count, wide = vectors[0].shape[1], up_out.shape[1]
+    lines = wide * g.n // width
+    per_line = width // wide
+    mine = pltpu.roll(held[...], (width - here * count) % width, 1)
+    for i, out in enumerate(vectors):
+        out[...] = mine[i : i + 1, :count]
+    up = pltpu.roll(held[...], (width - here % per_line * wide) % width, 1)
+    total = jnp.zeros((1, wide), F32)
+    for i in range(lines):
+        total += jnp.where(here // per_line == i, up[8 + i : 9 + i, :wide], 0.0)
+    up_out[...] = total
+    blocks = stats_out.shape[1]
+    stats = pltpu.roll(held[...], (width - s * blocks) % width, 1)
+    stats_out[...] = stats[8 + lines : 10 + lines, :blocks]
+
+
+def close_kernel(g, n, bias_ref, rows_ref, up_ref, stats_ref, *refs):
     terms, gtok_ref, refs = refs[:n], refs[n], refs[n + 1 :]
-    small_out, sums, gtok_home, refs = refs[0], refs[1 : 1 + n], refs[1 + n], refs[2 + n :]
+    small_outs, sums, gtok_home, refs = refs[:10], refs[10 : 10 + n], refs[10 + n], refs[11 + n :]
+    held, refs = refs[0], refs[1:]
     bufs, refs = refs[: 5 * n], refs[5 * n :]
     rs_send, rs_recv, small_bufs, refs = refs[0], refs[1], refs[2:7], refs[7:]
     small_send, small_recv, swap_send, swap_recv = refs
     greet(line_peers(g) + [swap_partner(g)])
     plan = Scatter(g, terms, bufs, TURNS, rs_send, rs_recv)
     swap = Swap(g, gtok_ref, gtok_home, swap_send, swap_recv)
-    small = Total(g, small_ref, small_bufs, small_send, small_recv)
+    small = Total(g, held, small_bufs, small_send, small_recv)
     units = len(plan.units)
     for unit in range(units):
         plan.step(unit, 0)
-    small.start(0, small_ref[...])
+    small.start(0, small_lines(bias_ref, rows_ref, up_ref, stats_ref))
     swap.start()
     for level in range(1, 6):
         for unit in range(units):
@@ -1340,36 +1381,63 @@
         if level < len(AXES):
             small.start(level, value)
         else:
-            small_out[...] = value
+            held[...] = value
+            own_lines(g, held, small_outs)
     swap.wait()
     plan.sent()
     small.sent()
 
 
-def close_call(g, small, terms, gtok):
+def close_call(g, small, sizes_out, terms, gtok):
     n = len(terms)
+    lines = (16, small[0].shape[1])
     shape = jax.ShapeDtypeStruct
     any_space, vmem = pl.BlockSpec(memory_space=pl.ANY), pl.BlockSpec(memory_space=pltpu.VMEM)
     made = pl.pallas_call(
         functools.partial(close_kernel, g, n),
         out_shape=[
-            shape(small.shape, F32),
+            *(shape(item, F32) for item in sizes_out),
             *(shape(item.shape[-2:], F32) for item in terms),
             shape(gtok.shape, BF16),
         ],
-        in_specs=[vmem] * (1 + n) + [any_space],
-        out_specs=[vmem] * (1 + n) + [any_space],
+        in_specs=[vmem] * (5 + n),
+        out_specs=[vmem] * (10 + n) + [any_space],
         scratch_shapes=[
+            pltpu.VMEM(lines, F32),
             *Scatter.scratch(g, [item.shape for item in terms], TURNS),
-            *Total.scratch(g, small.shape),
+            *Total.scratch(g, lines),
             *Swap.sems(),
         ],
         compiler_params=pltpu.CompilerParams(
             collective_id=6, has_side_effects=True, vmem_limit_bytes=VMEM_LIMIT
         ),
         name="close",
-    )(small, *terms, gtok)
-    return made[0], made[1:-1], made[-1]
+    )(*small, *terms, gtok)
+    return made[:10], made[10:-1], made[-1]
+
+
+def finish_kernel(n, *refs):
+    ins, outs, sems = refs[:n], refs[n : 2 * n], refs[2 * n]
+    copies = [
+        pltpu.make_async_copy(src, dst, sems.at[k]) for k, (src, dst) in enumerate(zip(ins, outs))
+    ]
+    for copy in copies:
+        copy.start()
+    for copy in copies:
+        copy.wait()
+
+
+def finish(arrays):
+    n = len(arrays)
+    any_space = pl.BlockSpec(memory_space=pl.ANY)
+    return pl.pallas_call(
+        functools.partial(finish_kernel, n),
+        out_shape=[jax.ShapeDtypeStruct(item.shape, item.dtype) for item in arrays],
+        in_specs=[pl.BlockSpec(memory_space=pltpu.VMEM)] * n,
+        out_specs=[any_space] * n,
+        scratch_shapes=[pltpu.SemaphoreType.DMA((n,))],
+        name="finish",
+    )(*arrays)
 
 
 def body(
@@ -1417,11 +1485,9 @@
         second_shift,
     )
     count = query_bias.shape[0]
-    lines = (*vectors, up_bias)
-    line = lax.broadcasted_iota(jnp.int32, (16, PAIR), 0)
-    packed = jnp.zeros((16, PAIR), BF16)
-    for index, value in enumerate(lines):
-        packed = jnp.where(line == index, jnp.pad(value, (0, PAIR - value.shape[0]))[None], packed)
+    packed = jnp.pad(jnp.stack(vectors), ((0, 8), (0, PAIR - count))) + jnp.pad(
+        up_bias[None], ((8, 7), (0, PAIR - up_bias.shape[0]))
+    )
     gathered, partial, (work_x, work_table, work_mask) = open_call(
         g,
         [packed, query_weight, key_weight, value_weight],
@@ -1478,37 +1544,24 @@
         qkv,
         routed,
     )
-    lines = wide // width
-    small = jnp.concatenate(
-        [
-            g_bias[0:1],
-            g_bias[2:3],
-            g_rows[:6],
-            g_upb[0].reshape(lines, width),
-            jnp.pad(stats[:2], ((0, 0), (0, width - stats.shape[1]))),
-            jnp.zeros((6 - lines, width), F32),
-        ],
-        axis=0,
-    )
+    blocks = tok // CLUSTER
     small, s_attn, grad_tokens = close_call(
-        g, small, [parts(item) for item in (*g_attn, g_down)], grad_tokens
-    )
-
-    b, s = lax.axis_index("batch"), lax.axis_index("seq")
-    here = b * g.seq + s
-    mine = lax.dynamic_slice(small, (0, here * count), (8, count))
-    wide_count = wide // g.n
-    gu = lax.dynamic_slice(small[8 : 8 + lines].reshape(wide), (here * wide_count,), (wide_count,))
-    blocks = tok // CLUSTER
-    cluster_stats = lax.dynamic_slice(small, (8 + lines, s * blocks), (2, blocks))
+        g,
+        [g_bias, g_rows, g_upb, stats],
+        [(1, count)] * 8 + [(1, wide // g.n), (2, blocks)],
+        [parts(item) for item in (*g_attn, g_down)],
+        grad_tokens,
+    )
+    made = finish([out, grad_tokens, *small, *s_ffn, *s_attn])
+    out, grad_tokens, small, sums = made[0], made[1], made[2:12], made[12:]
     s_up, s_out, s_query, s_key, s_value, s_down = (
         item.reshape(local.shape)
         for item, local in zip(
-            (*s_ffn, *s_attn),
+            sums,
             (up_weight, output_weight, query_weight, key_weight, value_weight, down_weight),
         )
     )
-    gq, gv, go, gg1, gs1, gd, gg2, gs2 = (mine[i] for i in range(8))
+    gq, gv, go, gg1, gs1, gd, gg2, gs2, gu = (item.reshape(-1) for item in small[:9])
     return (
         out[None],
         grad_tokens[None],
@@ -1527,7 +1580,7 @@
         gd,
         gg2,
         gs2,
-        cluster_stats,
+        small[9],
     )
 
 

time: 461 us -> 431 us (0.935)
  local copies, waits for them, and re-layouts: 24.3 us -> 4.41 us
  Pallas kernels: 424 us -> 414 us
    pallas_call x1, Pallas kernels: 95.2 us -> 84.7 us  [forward(): pl.pallas_call(functools.partial(forward_kernel, g, scale, factor), out_s...]
    unnamed x27 -> x1, local copies, waits for them, and re-layouts: 7.14 us -> 0.03 us
    pad x10 -> x0, local copies, waits for them, and re-layouts: 5.94 us -> none  [the longest x9 5.94 us: body(): jnp.pad(value, (0, PAIR - value.shape[0]))[None]]
    pallas_call x1 -> x2, Pallas kernels: 63.5 us -> 68.7 us  [the longest x1 64.4 us: close_call(): pl.pallas_call(functools.partial(close_kernel, g, n), out_shape=[*(shape(...]
where the time goes in v5:
time: 431 us; the launch traced here: 424 us
  Pallas kernels  414 us (96%)
  other arithmetic  5.14 us (1%)
  local copies, waits for them, and re-layouts  4.41 us (1%)
    pallas_call x1, Pallas kernels, backward(): pl.pallas_call(functools.partial(backward_kernel, g, scale, n), out_shape...  112 us
    pallas_call x1, Pallas kernels, forward(): pl.pallas_call(functools.partial(forward_kernel, g, scale, factor), out_s...  84.7 us
    pallas_call x1, Pallas kernels, middle(): pl.pallas_call(functools.partial(middle_kernel, g), out_shape=[shape((tok...  76.2 us
    pallas_call x1, Pallas kernels, open_call(): pl.pallas_call(functools.partial(open_kernel, g, n, m), out_shape=[*outs,...  71.5 us
    pallas_call x1, Pallas kernels, close_call(): pl.pallas_call(functools.partial(close_kernel, g, n), out_shape=[*(shape(...  64.4 us

profile of v5, /device:TPU:0, one launch (start us, length us, event | category | flops | bytes accessed | tf_op | source)
XLA Modules:
  0.0 424.3 jit_solution(2815865766192950917)
XLA Ops:
  0.7 0.1 pad.15.clone
  0.7 0.1 pad.11.clone
  0.8 0.8 stack.38
  1.6 1.3 pad_add_fusion.refs_0_
  2.9 0.9 fusion.1
  3.8 1.4 add_add_fusion.refs_8_
  5.2 71.5 %open.1 = (bf16[2,2,2,2,2,16,128]{6,5,4,3,2,1,0:T(8,128)(2,1)}, bf16[2,2,2,2,2,24,768]{6,5,4,3,2,1,0:T(8,128)(2,1)}, bf16[2,2,2,2,2,24,768]{6,5,4,3,2,1,0:T(8,12...) custom-call(bf16[16,128]{1,0:T(8,128)(2,1)} %pad_add_fusion.refs_0_,, ...), custom_call_target="tpu_custom_call" | custom-call | tf_op jit(solution)/shard_map/open/pallas_call | solution.py:287
  76.7 0.9 bitcast_convert_fusion
  77.7 0.7 reshape_squeeze.3.up_bias_ref
  78.4 0.7 slice.30.vec_ref
  79.1 0.1 slice.26
  79.2 0.1 slice.28
  79.3 0.7 pad_maximum_fusion.bias_ref
  80.0 1.8 copy.41
  81.8 84.7 %forward.1 = (bf16[2,2,2,2,2,24,768]{6,5,4,3,2,1,0:T(8,128)(2,1)}, bf16[2,2,2,2,2,24,3072]{6,5,4,3,2,1,0:T(8,128)(2,1)}, bf16[2,2,2,2,2,96,768]{6,5,4,3,2,1,0:T(...) custom-call(bf16[1024,768]{1,0:T(8,128)(2,1)} %get-tuple-element.82.x_ref, ...), custom_call_target="tpu_custom_call" | custom-call | tf_op jit(solution)/shard_map/forward/pallas_call | solution.py:847
  166.5 76.2 %middle.1 = (bf16[1024,768]{1,0:T(8,128)(2,1)}, bf16[1024,768]{1,0:T(8,128)(2,1)}, bf16[6,8,128,128]{3,2,1,0:T(8,128)(2,1)}, bf16[768,768]{1,0:T(8,128)(2,1)}, b...) custom-call(bf16[1024,768]{1,0:T(8,128)(2,1)} %get-tuple-element.82.x_ref, ...), custom_call_target="tpu_custom_call" | custom-call | tf_op jit(solution)/shard_map/middle/pallas_call | solution.py:1124
  242.6 112.4 %backward.1 = (bf16[1024,768]{1,0:T(8,128)(2,1)}, bf16[768,768]{1,0:T(8,128)(2,1)}, bf16[768,768]{1,0:T(8,128)(2,1)}, bf16[768,768]{1,0:T(8,128)(2,1)}, f32[8,76...) custom-call(bf16[1024,768]{1,0:T(8,128)(2,1)} %get-tuple-element.82.x_ref, bf16[768,768]{1,0:T(8,128)(2,1)} %bitcast.66, ...), custom_call_target="tpu_custom_call" | custom-call | tf_op jit(solution)/shard_map/backward/pallas_call | solution.py:1290
  355.1 64.4 %close.1 = (f32[1,24]{1,0:T(1,128)}, f32[1,24]{1,0:T(1,128)}, f32[1,24]{1,0:T(1,128)}, f32[1,24]{1,0:T(1,128)}, f32[1,24]{1,0:T(1,128)}, /*index=5*/f32[1,24]{1,...) custom-call(f32[8,768]{1,0:T(8,128)} %get-tuple-element.102.bias_ref, ...), custom_call_target="tpu_custom_call" | custom-call | tf_op jit(solution)/shard_map/close/pallas_call | solution.py:1396
  419.5 4.3 %finish.1 = (bf16[1024,768]{1,0:T(8,128)(2,1)}, bf16[1024,768]{1,0:T(8,128)(2,1)}, f32[1,24]{1,0:T(1,128)}, f32[1,24]{1,0:T(1,128)}, f32[1,24]{1,0:T(1,128)}, /*...) custom-call(bf16[1024,768]{1,0:T(8,128)(2,1)} %get-tuple-element.96., ...), custom_call_target="tpu_custom_call" | custom-call | tf_op jit(solution)/shard_map/finish/pallas_call | solution.py:1433
  (6 shorter events, 0.1 us)

commit v6 on v5

--- a/solution.py
+++ b/solution.py
@@ -546,7 +546,7 @@
     return value.astype(kind).reshape(sources, size, value.shape[1])
 
 
-ROWS = 512
+ROWS = 1024
 
 
 def pair_weights(pair, w_refs, out_ref):

time: 431 us -> 428 us (level)
  no operation moved by 1% of the time
where the time goes in v6:
time: 428 us; the launch traced here: 422 us
  Pallas kernels  411 us (96%)
  other arithmetic  5.14 us (1%)
  local copies, waits for them, and re-layouts  4.41 us (1%)
    pallas_call x1, Pallas kernels, backward(): pl.pallas_call(functools.partial(backward_kernel, g, scale, n), out_shape...  111 us
    pallas_call x1, Pallas kernels, forward(): pl.pallas_call(functools.partial(forward_kernel, g, scale, factor), out_s...  84.2 us
    pallas_call x1, Pallas kernels, middle(): pl.pallas_call(functools.partial(middle_kernel, g), out_shape=[shape((tok...  75.2 us
    pallas_call x1, Pallas kernels, open_call(): pl.pallas_call(functools.partial(open_kernel, g, n, m), out_shape=[*outs,...  71.5 us
    pallas_call x1, Pallas kernels, close_call(): pl.pallas_call(functools.partial(close_kernel, g, n), out_shape=[*(shape(...  65.2 us

profile of v6, /device:TPU:0, one launch (start us, length us, event | category | flops | bytes accessed | tf_op | source)
XLA Modules:
  0.0 421.7 jit_solution(9653578620346862016)
XLA Ops:
  0.7 0.1 pad.15.clone
  0.7 0.1 pad.11.clone
  0.8 0.8 stack.38
  1.6 1.3 pad_add_fusion.refs_0_
  2.9 0.9 fusion.1
  3.8 1.4 add_add_fusion.refs_8_
  5.2 71.5 %open.1 = (bf16[2,2,2,2,2,16,128]{6,5,4,3,2,1,0:T(8,128)(2,1)}, bf16[2,2,2,2,2,24,768]{6,5,4,3,2,1,0:T(8,128)(2,1)}, bf16[2,2,2,2,2,24,768]{6,5,4,3,2,1,0:T(8,12...) custom-call(bf16[16,128]{1,0:T(8,128)(2,1)} %pad_add_fusion.refs_0_,, ...), custom_call_target="tpu_custom_call" | custom-call | tf_op jit(solution)/shard_map/open/pallas_call | solution.py:287
  76.7 0.9 bitcast_convert_fusion
  77.7 0.7 reshape_squeeze.3.up_bias_ref
  78.4 0.7 slice.30.vec_ref
  79.1 0.1 slice.26
  79.2 0.1 slice.28
  79.3 0.7 pad_maximum_fusion.bias_ref
  80.0 1.8 copy.41
  81.8 84.2 %forward.1 = (bf16[2,2,2,2,2,24,768]{6,5,4,3,2,1,0:T(8,128)(2,1)}, bf16[2,2,2,2,2,24,3072]{6,5,4,3,2,1,0:T(8,128)(2,1)}, bf16[2,2,2,2,2,96,768]{6,5,4,3,2,1,0:T(...) custom-call(bf16[1024,768]{1,0:T(8,128)(2,1)} %get-tuple-element.82.x_ref, ...), custom_call_target="tpu_custom_call" | custom-call | tf_op jit(solution)/shard_map/forward/pallas_call | solution.py:847
  166.0 75.2 %middle.1 = (bf16[1024,768]{1,0:T(8,128)(2,1)}, bf16[1024,768]{1,0:T(8,128)(2,1)}, bf16[6,8,128,128]{3,2,1,0:T(8,128)(2,1)}, bf16[768,768]{1,0:T(8,128)(2,1)}, b...) custom-call(bf16[1024,768]{1,0:T(8,128)(2,1)} %get-tuple-element.82.x_ref, ...), custom_call_target="tpu_custom_call" | custom-call | tf_op jit(solution)/shard_map/middle/pallas_call | solution.py:1124
  241.2 110.8 %backward.1 = (bf16[1024,768]{1,0:T(8,128)(2,1)}, bf16[768,768]{1,0:T(8,128)(2,1)}, bf16[768,768]{1,0:T(8,128)(2,1)}, bf16[768,768]{1,0:T(8,128)(2,1)}, f32[8,76...) custom-call(bf16[1024,768]{1,0:T(8,128)(2,1)} %get-tuple-element.82.x_ref, bf16[768,768]{1,0:T(8,128)(2,1)} %bitcast.66, ...), custom_call_target="tpu_custom_call" | custom-call | tf_op jit(solution)/shard_map/backward/pallas_call | solution.py:1290
  352.0 65.2 %close.1 = (f32[1,24]{1,0:T(1,128)}, f32[1,24]{1,0:T(1,128)}, f32[1,24]{1,0:T(1,128)}, f32[1,24]{1,0:T(1,128)}, f32[1,24]{1,0:T(1,128)}, /*index=5*/f32[1,24]{1,...) custom-call(f32[8,768]{1,0:T(8,128)} %get-tuple-element.102.bias_ref, ...), custom_call_target="tpu_custom_call" | custom-call | tf_op jit(solution)/shard_map/close/pallas_call | solution.py:1396
  417.2 4.3 %finish.1 = (bf16[1024,768]{1,0:T(8,128)(2,1)}, bf16[1024,768]{1,0:T(8,128)(2,1)}, f32[1,24]{1,0:T(1,128)}, f32[1,24]{1,0:T(1,128)}, f32[1,24]{1,0:T(1,128)}, /*...) custom-call(bf16[1024,768]{1,0:T(8,128)(2,1)} %get-tuple-element.96., ...), custom_call_target="tpu_custom_call" | custom-call | tf_op jit(solution)/shard_map/finish/pallas_call | solution.py:1433
  (6 shorter events, 0.1 us)
